TPU v7x, 512 devices: a whole 4x4x16 slice. The times are simulated.
512 devices in a mesh: gx: 128 (over y_lo, x, z), gy: 4 (over y_hi, core).
Axes of the slice: x: 4, y: 4 (y_hi: 2, y_lo: 2; y = y_hi * 2 + y_lo), z: 16, core: 2. Of those that a mesh axis runs over, the one named last changes fastest.
Arguments:
- features: bfloat16 [262144, 128], P(('gx', 'gy')), may hold values from -6 to 6
- cotangent: bfloat16 [262144, 128], P(('gx', 'gy')), may hold values from -6 to 6
- block_pos: int32 [4096], P(('gx', 'gy')), may hold values from -1 to 11, as said below
- weight_one: bfloat16 [3456, 128], replicated, may hold values from -0.1875 to 0.1875
- weight_two: bfloat16 [3456, 128], replicated, may hold values from -0.1875 to 0.1875
Outputs:
- output: bfloat16 [262144, 128], P(('gx', 'gy'))
- input_grad: float32 [262144, 128], P(('gx', 'gy'))
- grad_one: float32 [3456, 128], replicated
- grad_two: float32 [3456, 128], replicated
Inputs may be any that keep to these rules, and one draw needn't show every extreme that they name: `block_pos`: local position p numbers a device's 2 x 2 x 3 block grid as (bx * 2 + by) * 3 + bz. A device's used slots come first and hold distinct positions, the rest hold -1; every device uses 2 or more slots and some device uses all 8.
All inputs are finite; a program needn't handle non-finite values.
Results may differ from a plain program's by a relative error of at most 0.0043.
Values may be sent and summed in bfloat16 or wider, within the bound.
No kernel may reach another device: no remote copies, remote signals or barrier semaphores. Data moves between devices by JAX's collectives and lax.ppermute only.
A program may use at most 128 MiB of HBM per device.

v0:
```python
import jax
import jax.numpy as jnp
from jax import lax
from jax.sharding import PartitionSpec as P

LBX = 2
LBY = 2
LBZ = 3
POS = 12


def padded_2(block, sides, width):
    for axis, dim in sides:
        count = lax.axis_size(axis)
        forward = [(i, i + 1) for i in range(count - 1)]
        backward = [(target, source) for source, target in forward]
        low = lax.ppermute(
            lax.slice_in_dim(block, block.shape[dim] - width, None, axis=dim), axis, forward
        )
        high = lax.ppermute(lax.slice_in_dim(block, 0, width, axis=dim), axis, backward)
        block = jnp.concatenate([low, block, high], axis=dim)
    return block


def flipped(weight):
    width = weight.shape[1]
    return weight.reshape(27, width, width)[::-1].transpose(0, 2, 1).reshape(27 * width, width)


def with_rim(grid):
    padded = padded_2(grid, (("gx", 0), ("gy", 1)), 1)
    return jnp.pad(padded, ((0, 0), (0, 0), (1, 1), (0, 0)))


def per_device(features, cotangent, block_pos, weight_one, weight_two):
    slot_count = block_pos.shape[0]
    chan_width = features.shape[1]
    active = block_pos >= 0
    row_mask = jnp.repeat(active, 64)[:, None]
    position = jnp.where(active, block_pos, 0)
    select = (
        (position[:, None] == jnp.arange(POS, dtype=jnp.int32)[None, :]) & active[:, None]
    ).astype(jnp.bfloat16)
    corner_x = position // (LBY * LBZ) * 4
    corner_y = position // LBZ % LBY * 4
    corner_z = position % LBZ * 4
    total_rows = slot_count * 64 * lax.axis_size("gx") * lax.axis_size("gy")
    weight_scale = 1.0 / jnp.sqrt(jnp.float32(total_rows))

    def to_grid(values):
        blocks = values.reshape(slot_count, 64 * chan_width)
        placed = jnp.dot(select.T, blocks, preferred_element_type=jnp.float32).astype(jnp.bfloat16)
        placed = placed.reshape(LBX, LBY, LBZ, 4, 4, 4, chan_width).transpose(0, 3, 1, 4, 2, 5, 6)
        return placed.reshape(LBX * 4, LBY * 4, LBZ * 4, chan_width)

    def columns(values):
        padded = with_rim(to_grid(values))

        def window(start_x, start_y, start_z):
            starts = (start_x, start_y, start_z, jnp.zeros((), jnp.int32))
            return lax.dynamic_slice(padded, starts, (6, 6, 6, chan_width))

        windows = jax.vmap(window)(corner_x, corner_y, corner_z)
        pieces = [
            windows[:, off_x : off_x + 4, off_y : off_y + 4, off_z : off_z + 4]
            for off_x in range(3)
            for off_y in range(3)
            for off_z in range(3)
        ]
        stacked = jnp.stack(pieces, axis=4)
        return stacked.reshape(slot_count * 64, 27 * chan_width)

    def gram(cols, grads):
        term = lax.dot_general(
            cols, grads, (((0,), (0,)), ((), ())), preferred_element_type=jnp.float32
        )
        return term * weight_scale

    x_in = jnp.where(row_mask, features, 0)
    cols_x = columns(x_in)
    pre_one = jnp.dot(cols_x, weight_one, preferred_element_type=jnp.float32)
    sigmoid_one = jax.nn.sigmoid(pre_one)
    hidden = jnp.where(row_mask, pre_one * sigmoid_one, 0.0).astype(jnp.bfloat16)
    cols_h = columns(hidden)
    pre_two = jnp.dot(cols_h, weight_two, preferred_element_type=jnp.float32)
    output = jnp.where(row_mask, pre_two + x_in.astype(jnp.float32), 0.0).astype(jnp.bfloat16)
    upstream = jnp.where(row_mask, cotangent, 0)
    term_two = gram(cols_h, upstream)
    back_two = jnp.dot(columns(upstream), flipped(weight_two), preferred_element_type=jnp.float32)
    slope = sigmoid_one * (1.0 + pre_one * (1.0 - sigmoid_one))
    hidden_grad = jnp.where(row_mask, back_two * slope, 0.0).astype(jnp.bfloat16)
    term_one = gram(cols_x, hidden_grad)
    back_one = jnp.dot(
        columns(hidden_grad), flipped(weight_one), preferred_element_type=jnp.float32
    )
    input_grad = jnp.where(row_mask, upstream.astype(jnp.float32) + back_one, 0.0)
    grad_one, grad_two = lax.psum((term_one, term_two), ("gx", "gy"))
    return (output, input_grad, grad_one, grad_two)


def solution(mesh):
    in_specs = (P(("gx", "gy"), None), P(("gx", "gy"), None), P(("gx", "gy")), P(), P())
    out_specs = (P(("gx", "gy"), None), P(("gx", "gy"), None), P(), P())
    return jax.shard_map(
        per_device, mesh=mesh, in_specs=in_specs, out_specs=out_specs, check_vma=False
    )
```

profile of v0, /device:TPU:1, one launch (start us, length us, event | category | flops | bytes accessed | tf_op | source)
XLA Modules:
  0.0 721.8 jit_solution(6517857502068382059)
XLA Ops:
  10.6 4.4 collective-permute-start.8
  17.0 4.2 collective-permute-start
  26.2 6.0 collective-permute-start.10
  34.2 5.1 collective-permute-start.2
  41.7 20.5 %while.6 = (s32[]{:T(128)}, bf16[10,10,14,128]{3,1,2,0:T(8,128)(2,1)S(1)}, s32[8,4]{0,1:T(4,128)S(1)}, bf16[8,6,6,6,128]{4,3,2,1,0:T(8,128)(2,1)S(1)}, s32[]{:T(128)}) while((s32[]{:T(128)}, bf16[10,10,14,128]{3,1,2,0:T(8,128)(2,1)S(1)}, s32[8,4]{0,1:T(4,128)S(1)}, bf16[8,6,6,6,128]{4,3,2,1,0:T(8,128)(2,1)S(1)}, s32[]{:T(128)}) %tuple.96), condition=%wide.while_cond.2, body=%wide.while_body.2.sunk | while | flops 2 | bytes 258185 | solution.py:61
  64.4 6.2 copy.33
  71.0 20.7 %while.4 = (s32[]{:T(128)}, bf16[10,10,14,128]{3,1,2,0:T(8,128)(2,1)S(1)}, s32[8,4]{0,1:T(4,128)S(1)}, bf16[8,6,6,6,128]{4,3,2,1,0:T(8,128)(2,1)S(1)}, s32[]{:T(128)}) while((s32[]{:T(128)}, bf16[10,10,14,128]{3,1,2,0:T(8,128)(2,1)S(1)}, s32[8,4]{0,1:T(4,128)S(1)}, bf16[8,6,6,6,128]{4,3,2,1,0:T(8,128)(2,1)S(1)}, s32[]{:T(128)}) %tuple.106), condition=%wide.while_cond, body=%wide.while_body.sunk | while | flops 2 | bytes 258185 | solution.py:61
  93.9 4.2 copy.27
  101.8 5.1 convolution_multiply_fusion.1
  107.7 4.3 collective-permute-start.4
  113.9 5.2 collective-permute-start.12
  120.5 5.7 collective-permute-start.6
  128.2 5.1 collective-permute-start.14
  135.7 21.4 %while.5 = (s32[]{:T(128)}, bf16[10,10,14,128]{3,1,2,0:T(8,128)(2,1)S(1)}, s32[8,4]{0,1:T(4,128)S(1)}, bf16[8,6,6,6,128]{4,3,2,1,0:T(8,128)(2,1)S(1)}, s32[]{:T(128)}) while((s32[]{:T(128)}, bf16[10,10,14,128]{3,1,2,0:T(8,128)(2,1)S(1)}, s32[8,4]{0,1:T(4,128)S(1)}, bf16[8,6,6,6,128]{4,3,2,1,0:T(8,128)(2,1)S(1)}, s32[]{:T(128)}) %tuple.107), condition=%wide.while_cond.1, body=%wide.while_body.1.sunk | while | flops 2 | bytes 258185 | solution.py:61
  136.4 2.0 constant_dynamic-slice_fusion.19
  139.1 2.0 constant_dynamic-slice_fusion.19
  141.8 2.0 constant_dynamic-slice_fusion.19
  144.5 2.0 constant_dynamic-slice_fusion.19
  147.1 2.0 constant_dynamic-slice_fusion.19
  149.8 2.0 constant_dynamic-slice_fusion.19
  152.5 2.0 constant_dynamic-slice_fusion.19
  155.2 2.0 constant_dynamic-slice_fusion.19
  159.4 4.2 copy.30
  163.6 2.0 copy-done
  165.6 4.9 convolution_multiply_fusion
  170.9 21.6 %while.7 = (s32[]{:T(128)}, bf16[10,10,14,128]{3,1,2,0:T(8,128)(2,1)S(1)}, s32[8,4]{0,1:T(4,128)S(1)}, bf16[8,6,6,6,128]{4,3,2,1,0:T(8,128)(2,1)S(1)}, s32[]{:T(128)}) while((s32[]{:T(128)}, bf16[10,10,14,128]{3,1,2,0:T(8,128)(2,1)S(1)}, s32[8,4]{0,1:T(4,128)S(1)}, bf16[8,6,6,6,128]{4,3,2,1,0:T(8,128)(2,1)S(1)}, s32[]{:T(128)}) %tuple.108), condition=%wide.while_cond.3, body=%wide.while_body.3.sunk | while | flops 2 | bytes 258185 | solution.py:61
  176.9 2.0 constant_dynamic-slice_fusion.23
  179.5 2.0 constant_dynamic-slice_fusion.23
  182.2 2.0 constant_dynamic-slice_fusion.23
  211.9 6.3 copy.37
  222.6 487.9 %all-reduce.7.cloned.1.call-done = (f32[3456,128]{1,0:T(8,128)}, f32[3456,128]{1,0:T(8,128)}) async-done(((f32[3456,128]{1,0:T(8,128)}, f32[3456,128]{1,0:T(8,128)}), (f32[3456,128]{1,0:T(8,128)}, f32[3456,128]{1,0:T(8,128)})) %all-reduce.7.cloned.1.call-update) | async-done | bytes 3538960 | tf_op jit(solution)/shard_map/psum | solution.py:97
  710.4 2.9 copy.244
  (318 shorter events, 119.9 us)
Async XLA Ops:
  7.2 15.4 %copy-start.5 = (bf16[3456,128]{1,0:T(8,128)(2,1)S(1)}, bf16[3456,128]{1,0:T(8,128)(2,1)}, u32[]{:S(2)}) copy-start(bf16[3456,128]{1,0:T(8,128)(2,1)} %param.9) | copy-start | bytes 2654212
  7.2 15.5 %copy-start.4 = (bf16[3456,128]{1,0:T(8,128)(2,1)S(1)}, bf16[3456,128]{1,0:T(8,128)(2,1)}, u32[]{:S(2)}) copy-start(bf16[3456,128]{1,0:T(8,128)(2,1)} %param.8) | copy-start | bytes 2654212
  7.2 703.2 %all-reduce.7.cloned.1.call-start = ((), (), s32[]{:S(2)}) async-start(), calls=%async_computation | async-start | bytes 7077888 | tf_op jit(solution)/shard_map/psum | solution.py:97
  10.6 15.4 %collective-permute-start.8 = (bf16[1,8,12,128]{3,1,2,0:T(8,128)(2,1)S(1)}, bf16[1,8,12,128]{3,1,2,0:T(8,128)(2,1)S(1)}, u32[]{:S(2)}, u32[]{:S(2)}) collective-permute-start(bf16[1,8,12,128]{3,1,2,0:T(8,128)(2,1)S(1)} %get-tuple-element.124), channel_id=1, source_target_pairs={{0,4},{4,8},{8,12},{12,16},{16,20},{20,24},{24,28},{28,32},{32,36}... | collective-permute-start | bytes 73736 | tf_op jit(solution)/shard_map/ppermute | solution.py:17
  15.0 11.1 %collective-permute-start.9 = (bf16[1,8,12,128]{3,1,2,0:T(8,128)(2,1)S(1)}, bf16[1,8,12,128]{3,1,2,0:T(8,128)(2,1)S(1)}, u32[]{:S(2)}, u32[]{:S(2)}) collective-permute-start(bf16[1,8,12,128]{3,1,2,0:T(8,128)(2,1)S(1)} %get-tuple-element.125), channel_id=1, source_target_pairs={{4,0},{8,4},{12,8},{16,12},{20,16},{24,20},{28,24},{32,28},{36,32}... | collective-permute-start | bytes 73736 | tf_op jit(solution)/shard_map/ppermute | solution.py:20
  17.0 17.2 %collective-permute-start = (bf16[1,8,12,128]{3,1,2,0:T(8,128)(2,1)S(1)}, bf16[1,8,12,128]{3,1,2,0:T(8,128)(2,1)S(1)}, u32[]{:S(2)}, u32[]{:S(2)}) collective-permute-start(bf16[1,8,12,128]{3,1,2,0:T(8,128)(2,1)S(1)} %get-tuple-element.128), channel_id=1, source_target_pairs={{0,4},{4,8},{8,12},{12,16},{16,20},{20,24},{24,28},{28,32},{32,36}... | collective-permute-start | bytes 73736 | tf_op jit(solution)/shard_map/ppermute | solution.py:17
  21.1 13.0 %collective-permute-start.1 = (bf16[1,8,12,128]{3,1,2,0:T(8,128)(2,1)S(1)}, bf16[1,8,12,128]{3,1,2,0:T(8,128)(2,1)S(1)}, u32[]{:S(2)}, u32[]{:S(2)}) collective-permute-start(bf16[1,8,12,128]{3,1,2,0:T(8,128)(2,1)S(1)} %get-tuple-element.129), channel_id=1, source_target_pairs={{4,0},{8,4},{12,8},{16,12},{20,16},{24,20},{28,24},{32,28},{36,32}... | collective-permute-start | bytes 73736 | tf_op jit(solution)/shard_map/ppermute | solution.py:20
  26.2 15.2 %collective-permute-start.10 = (bf16[10,1,12,128]{3,1,2,0:T(2,128)(2,1)S(1)}, bf16[10,1,12,128]{3,1,2,0:T(2,128)(2,1)S(1)}, u32[]{:S(2)}, u32[]{:S(2)}) collective-permute-start(bf16[10,1,12,128]{3,1,2,0:T(2,128)(2,1)S(1)} %get-tuple-element.116), channel_id=1, source_target_pairs={{0,1},{1,2},{2,3},{4,5},{5,6},{6,7},{8,9},{9,10},{10,11},{12,13},{... | collective-permute-start | bytes 92168 | tf_op jit(solution)/shard_map/ppermute | solution.py:17
  32.2 9.1 %collective-permute-start.11 = (bf16[10,1,12,128]{3,1,2,0:T(2,128)(2,1)S(1)}, bf16[10,1,12,128]{3,1,2,0:T(2,128)(2,1)S(1)}, u32[]{:S(2)}, u32[]{:S(2)}) collective-permute-start(bf16[10,1,12,128]{3,1,2,0:T(2,128)(2,1)S(1)} %get-tuple-element.117), channel_id=1, source_target_pairs={{1,0},{2,1},{3,2},{5,4},{6,5},{7,6},{9,8},{10,9},{11,10},{13,12},{... | collective-permute-start | bytes 92168 | tf_op jit(solution)/shard_map/ppermute | solution.py:20
  34.2 36.4 %collective-permute-start.2 = (bf16[10,1,12,128]{3,1,2,0:T(2,128)(2,1)S(1)}, bf16[10,1,12,128]{3,1,2,0:T(2,128)(2,1)S(1)}, u32[]{:S(2)}, u32[]{:S(2)}) collective-permute-start(bf16[10,1,12,128]{3,1,2,0:T(2,128)(2,1)S(1)} %get-tuple-element.120), channel_id=1, source_target_pairs={{0,1},{1,2},{2,3},{4,5},{5,6},{6,7},{8,9},{9,10},{10,11},{12,13},{... | collective-permute-start | bytes 92168 | tf_op jit(solution)/shard_map/ppermute | solution.py:17
  39.4 31.2 %collective-permute-start.3 = (bf16[10,1,12,128]{3,1,2,0:T(2,128)(2,1)S(1)}, bf16[10,1,12,128]{3,1,2,0:T(2,128)(2,1)S(1)}, u32[]{:S(2)}, u32[]{:S(2)}) collective-permute-start(bf16[10,1,12,128]{3,1,2,0:T(2,128)(2,1)S(1)} %get-tuple-element.121), channel_id=1, source_target_pairs={{1,0},{2,1},{3,2},{5,4},{6,5},{7,6},{9,8},{10,9},{11,10},{13,12},{... | collective-permute-start | bytes 92168 | tf_op jit(solution)/shard_map/ppermute | solution.py:20
  98.2 2.2 copy-start.2
  98.2 2.4 copy-start.8
  107.7 12.7 %collective-permute-start.4 = (bf16[1,8,12,128]{3,1,2,0:T(8,128)(2,1)S(1)}, bf16[1,8,12,128]{3,1,2,0:T(8,128)(2,1)S(1)}, u32[]{:S(2)}, u32[]{:S(2)}) collective-permute-start(bf16[1,8,12,128]{3,1,2,0:T(8,128)(2,1)S(1)} %get-tuple-element.126), channel_id=1, source_target_pairs={{0,4},{4,8},{8,12},{12,16},{16,20},{20,24},{24,28},{28,32},{32,36}... | collective-permute-start | bytes 73736 | tf_op jit(solution)/shard_map/ppermute | solution.py:17
  112.0 8.4 %collective-permute-start.5 = (bf16[1,8,12,128]{3,1,2,0:T(8,128)(2,1)S(1)}, bf16[1,8,12,128]{3,1,2,0:T(8,128)(2,1)S(1)}, u32[]{:S(2)}, u32[]{:S(2)}) collective-permute-start(bf16[1,8,12,128]{3,1,2,0:T(8,128)(2,1)S(1)} %get-tuple-element.127), channel_id=1, source_target_pairs={{4,0},{8,4},{12,8},{16,12},{20,16},{24,20},{28,24},{32,28},{36,32}... | collective-permute-start | bytes 73736 | tf_op jit(solution)/shard_map/ppermute | solution.py:20
  113.9 14.3 %collective-permute-start.12 = (bf16[1,8,12,128]{3,1,2,0:T(8,128)(2,1)S(1)}, bf16[1,8,12,128]{3,1,2,0:T(8,128)(2,1)S(1)}, u32[]{:S(2)}, u32[]{:S(2)}) collective-permute-start(bf16[1,8,12,128]{3,1,2,0:T(8,128)(2,1)S(1)} %get-tuple-element.122), channel_id=1, source_target_pairs={{0,4},{4,8},{8,12},{12,16},{16,20},{20,24},{24,28},{28,32},{32,36}... | collective-permute-start | bytes 73736 | tf_op jit(solution)/shard_map/ppermute | solution.py:17
  119.1 9.1 %collective-permute-start.13 = (bf16[1,8,12,128]{3,1,2,0:T(8,128)(2,1)S(1)}, bf16[1,8,12,128]{3,1,2,0:T(8,128)(2,1)S(1)}, u32[]{:S(2)}, u32[]{:S(2)}) collective-permute-start(bf16[1,8,12,128]{3,1,2,0:T(8,128)(2,1)S(1)} %get-tuple-element.123), channel_id=1, source_target_pairs={{4,0},{8,4},{12,8},{16,12},{20,16},{24,20},{28,24},{32,28},{36,32}... | collective-permute-start | bytes 73736 | tf_op jit(solution)/shard_map/ppermute | solution.py:20
  120.5 14.8 %collective-permute-start.6 = (bf16[10,1,12,128]{3,1,2,0:T(2,128)(2,1)S(1)}, bf16[10,1,12,128]{3,1,2,0:T(2,128)(2,1)S(1)}, u32[]{:S(2)}, u32[]{:S(2)}) collective-permute-start(bf16[10,1,12,128]{3,1,2,0:T(2,128)(2,1)S(1)} %get-tuple-element.118), channel_id=1, source_target_pairs={{0,1},{1,2},{2,3},{4,5},{5,6},{6,7},{8,9},{9,10},{10,11},{12,13},{... | collective-permute-start | bytes 92168 | tf_op jit(solution)/shard_map/ppermute | solution.py:17
  126.2 9.1 %collective-permute-start.7 = (bf16[10,1,12,128]{3,1,2,0:T(2,128)(2,1)S(1)}, bf16[10,1,12,128]{3,1,2,0:T(2,128)(2,1)S(1)}, u32[]{:S(2)}, u32[]{:S(2)}) collective-permute-start(bf16[10,1,12,128]{3,1,2,0:T(2,128)(2,1)S(1)} %get-tuple-element.119), channel_id=1, source_target_pairs={{1,0},{2,1},{3,2},{5,4},{6,5},{7,6},{9,8},{10,9},{11,10},{13,12},{... | collective-permute-start | bytes 92168 | tf_op jit(solution)/shard_map/ppermute | solution.py:20
  128.2 42.3 %collective-permute-start.14 = (bf16[10,1,12,128]{3,1,2,0:T(2,128)(2,1)S(1)}, bf16[10,1,12,128]{3,1,2,0:T(2,128)(2,1)S(1)}, u32[]{:S(2)}, u32[]{:S(2)}) collective-permute-start(bf16[10,1,12,128]{3,1,2,0:T(2,128)(2,1)S(1)} %get-tuple-element.114), channel_id=1, source_target_pairs={{0,1},{1,2},{2,3},{4,5},{5,6},{6,7},{8,9},{9,10},{10,11},{12,13},{... | collective-permute-start | bytes 92168 | tf_op jit(solution)/shard_map/ppermute | solution.py:17
  133.4 37.1 %collective-permute-start.15 = (bf16[10,1,12,128]{3,1,2,0:T(2,128)(2,1)S(1)}, bf16[10,1,12,128]{3,1,2,0:T(2,128)(2,1)S(1)}, u32[]{:S(2)}, u32[]{:S(2)}) collective-permute-start(bf16[10,1,12,128]{3,1,2,0:T(2,128)(2,1)S(1)} %get-tuple-element.115), channel_id=1, source_target_pairs={{1,0},{2,1},{3,2},{5,4},{6,5},{7,6},{9,8},{10,9},{11,10},{13,12},{... | collective-permute-start | bytes 92168 | tf_op jit(solution)/shard_map/ppermute | solution.py:20
  163.6 2.0 copy-start
  211.8 6.3 copy-start.7
  218.2 2.2 copy-start.1
  218.2 2.5 copy-start.6
  218.2 2.5 copy-start.9
  710.4 2.9 copy-start.3
Sparse Core Ops, SparseCore 0:
  208.4 502.0 all-reduce.6
where the time goes:
time: 731 us; the launch traced here: 722 us
  waiting for transfers between devices  488 us (67%)
  local copies, waits for them, and re-layouts  142 us (19%)
  starting transfers between devices  52.9 us (7%)
  matrix products  17.8 us (2%)
  between operations  15.4 us (2%)
    psum x1, waiting for transfers between devices, per_device(): grad_one, grad_two = lax.psum((term_one, term_two), ('gx', 'gy'))  488 us
    gather x128, local copies, waits for them, and re-layouts  82.9 us
    ppermute x8, starting transfers between devices, padded_2(): lax.ppermute(lax.slice_in_dim(block, block.shape[dim] - width, None, axis...  40 us
    unnamed x130, local copies, waits for them, and re-layouts  32.7 us
    another operation x8, local copies, waits for them, and re-layouts, columns(): stacked = jnp.stack(pieces, axis=4)  21.9 us
  transfers between devices with their start and end apart: 17, of which 1 were waited for; matrix products, arithmetic and copies ran while one was open for 11% of the time, Pallas kernels for 0%

commit v1 on v0

v1 whole, which is shorter than its diff:
```python
import jax
import jax.numpy as jnp
from jax import lax
from jax.experimental import pallas as pl
from jax.experimental.pallas import tpu as pltpu
from jax.sharding import Mesh
from jax.sharding import PartitionSpec as P

LBY, LBZ = 2, 3
SLOTS = 8
C = 128
GX, GY, GZ = 8, 8, 16
PX, PY = GX + 2, GY + 2
ROWS = GX * GY * GZ
PAD_ROWS = PX * PY * GZ
DIMS = (2, 4, 4, 4, 2, 2)
NAMES = ("y_lo", "x", "z_hi", "z_lo", "y_hi", "core")
INTERPRET = False
BF = jnp.bfloat16
F32 = jnp.float32


def grid_row(pos_ref, index):
    slot = index >> 6
    pos = jnp.full(index.shape, -1, jnp.int32)
    for s in range(SLOTS):
        pos = jnp.where(slot == s, pos_ref[s], pos)
    safe = jnp.maximum(pos, 0)
    bx = (safe >= 6).astype(jnp.int32)
    rest = safe - 6 * bx
    by = (rest >= 3).astype(jnp.int32)
    bz = rest - 3 * by
    vx = (index >> 4) & 3
    vy = (index >> 2) & 3
    vz = index & 3
    row = ((bx * 4 + vx) * GY + by * 4 + vy) * GZ + bz * 4 + vz
    return jnp.where(pos >= 0, row, -1)


def dot(a, b, dims=((1,), (0,))):
    return lax.dot_general(a, b, (dims, ((), ())), preferred_element_type=F32)


def place_kernel(pos_ref, feat_ref, cot_ref, grid_ref, lo_ref, hi_ref):
    target = grid_row(pos_ref, lax.broadcasted_iota(jnp.int32, (1, SLOTS * 64), 1))
    rows = lax.broadcasted_iota(jnp.int32, (ROWS, SLOTS * 64), 0)
    perm = (rows == target).astype(F32).astype(BF)
    for field, ref in enumerate((feat_ref, cot_ref)):
        placed = dot(perm, ref[...]).astype(BF)
        grid_ref[field] = placed
        lo_ref[field] = placed[: GY * GZ]
        hi_ref[field] = placed[ROWS - GY * GZ :]
    grid_ref[2] = dot(perm, jnp.ones((SLOTS * 64, C), BF)).astype(BF)


def z_shifts(field):
    rows = field.shape[0]
    wide = field.astype(F32)
    before = pltpu.roll(wide, 1, 0).astype(BF)
    after = pltpu.roll(wide, rows - 1, 0).astype(BF)
    return jnp.concatenate([before, field, after], axis=1)


def fill_pad(pad_ref, grid, x_lo, x_hi, y_lo, y_hi):
    pad_ref[1 : PX - 1, 1 : PY - 1] = grid.reshape(GX, GY, GZ, C)
    pad_ref[0, 1 : PY - 1] = x_lo.reshape(GY, GZ, C)
    pad_ref[PX - 1, 1 : PY - 1] = x_hi.reshape(GY, GZ, C)
    pad_ref[:, 0] = y_lo.reshape(PX, GZ, C)
    pad_ref[:, PY - 1] = y_hi.reshape(PX, GZ, C)


def conv(shift_ref, w_ref):
    acc = None
    for k in range(9):
        dx, dy = divmod(k, 3)
        lhs = shift_ref[dx : dx + GX, dy : dy + GY].reshape(ROWS, 3 * C)
        term = dot(lhs, w_ref[k * 3 * C : (k + 1) * 3 * C, :])
        acc = term if acc is None else acc + term
    return acc


def middle_kernel(
    scale, grid_ref, xlo_ref, xhi_ref, ylo_ref, yhi_ref, w1_ref, w2f_ref,
    fields_ref, lo_ref, hi_ref, term1_ref, term2_ref, padx_ref, padu_ref, shift_ref, pre_ref,
):
    mask = grid_ref[2].astype(F32)
    fill_pad(padx_ref, grid_ref[0], xlo_ref[0], xhi_ref[0], ylo_ref[0], yhi_ref[0])
    fill_pad(padu_ref, grid_ref[1], xlo_ref[1], xhi_ref[1], ylo_ref[1], yhi_ref[1])
    shift_ref[...] = z_shifts(padx_ref[...].reshape(PAD_ROWS, C)).reshape(PX, PY, GZ, 3 * C)
    pre_ref[...] = conv(shift_ref, w1_ref)
    shift_ref[...] = z_shifts(padu_ref[...].reshape(PAD_ROWS, C)).reshape(PX, PY, GZ, 3 * C)
    back = conv(shift_ref, w2f_ref)
    pre = pre_ref[...]
    sig = jax.nn.sigmoid(pre)
    hidden = (pre * sig * mask).astype(BF)
    hgrad = (back * (sig * (1.0 + pre * (1.0 - sig))) * mask).astype(BF)
    fields_ref[0] = hidden
    fields_ref[1] = hgrad
    for field, value in enumerate((hidden, hgrad)):
        lo_ref[field] = value[: GY * GZ]
        hi_ref[field] = value[ROWS - GY * GZ :]
    hz = z_shifts(hidden).T
    for k in range(9):
        dx, dy = divmod(k, 3)
        rhs = padu_ref[2 - dx : 2 - dx + GX, 2 - dy : 2 - dy + GY].reshape(ROWS, C)
        term2_ref[k * 3 * C : (k + 1) * 3 * C, :] = (dot(hz, rhs) * scale).astype(term2_ref.dtype)
    gz = z_shifts(hgrad).T
    for k in range(9):
        dx, dy = divmod(k, 3)
        rhs = padx_ref[dx : dx + GX, dy : dy + GY].reshape(ROWS, C)
        prod = dot(gz, rhs) * scale
        for oz in range(3):
            block = prod[(2 - oz) * C : (3 - oz) * C, :].T
            term1_ref[(3 * k + oz) * C : (3 * k + oz + 1) * C, :] = block.astype(term1_ref.dtype)


def final_kernel(
    pos_ref, grid_ref, fields_ref, xlo_ref, xhi_ref, ylo_ref, yhi_ref, w2_ref, w1f_ref,
    out_ref, grad_ref, pad_ref, shift_ref,
):
    target = grid_row(pos_ref, lax.broadcasted_iota(jnp.int32, (SLOTS * 64, 1), 0))
    rows = lax.broadcasted_iota(jnp.int32, (SLOTS * 64, ROWS), 1)
    perm = (rows == target).astype(F32).astype(BF)
    for field, w_ref in enumerate((w2_ref, w1f_ref)):
        fill_pad(pad_ref, fields_ref[field], xlo_ref[field], xhi_ref[field], ylo_ref[field], yhi_ref[field])
        shift_ref[...] = z_shifts(pad_ref[...].reshape(PAD_ROWS, C)).reshape(PX, PY, GZ, 3 * C)
        value = conv(shift_ref, w_ref) + grid_ref[field].astype(F32)
        high = value.astype(BF)
        if field == 0:
            out_ref[...] = dot(perm, high).astype(BF)
        else:
            low = (value - high.astype(F32)).astype(BF)
            grad_ref[...] = dot(perm, high) + dot(perm, low)


def call(kernel, outs, scratch=(), smem=0, args=()):
    specs = [pl.BlockSpec(memory_space=pltpu.SMEM)] * smem
    specs += [pl.BlockSpec(memory_space=pltpu.VMEM)] * (len(args) - smem)
    return pl.pallas_call(
        kernel,
        out_shape=outs,
        in_specs=specs,
        out_specs=jax.tree.map(lambda _: pl.BlockSpec(memory_space=pltpu.VMEM), outs),
        scratch_shapes=list(scratch),
        compiler_params=pltpu.CompilerParams(vmem_limit_bytes=56 << 20),
        interpret=INTERPRET,
    )(*args)


def flipped(weight):
    return weight.reshape(27, C, C)[::-1].transpose(0, 2, 1).reshape(27 * C, C)


def ring(axes):
    count = lax.axis_size(axes)
    forward = [(i, i + 1) for i in range(count - 1)]
    return forward, [(b, a) for a, b in forward]


GXN = ("y_lo", "x", "z_hi", "z_lo")
GYN = ("y_hi", "core")


def exchange(fields, lo, hi):
    forward, backward = ring(GXN)
    x_lo = lax.ppermute(hi, GXN, forward)
    x_hi = lax.ppermute(lo, GXN, backward)
    grid = fields.reshape(-1, GX, GY, GZ, C)[:2]
    lows = x_lo.reshape(2, 1, GY, GZ, C)
    highs = x_hi.reshape(2, 1, GY, GZ, C)

    def face(y):
        return jnp.concatenate([lows[:, :, y], grid[:, :, y], highs[:, :, y]], axis=1).reshape(2, PX * GZ, C)

    forward, backward = ring(GYN)
    y_lo = lax.ppermute(face(GY - 1), GYN, forward)
    y_hi = lax.ppermute(face(0), GYN, backward)
    return x_lo, x_hi, y_lo, y_hi


def scatter_sum(values, axes):
    count = lax.axis_size(axes)
    pieces = lax.all_to_all(values, axes, 0, 0, tiled=True)
    return pieces.reshape(count, -1, C).astype(F32).sum(axis=0)


def group_sum(values, axis):
    count = lax.axis_size(axis)
    got = [lax.ppermute(values, axis, [(i, i ^ d) for i in range(count)]) for d in range(1, count)]
    if count == 1:
        return values
    if count == 2:
        return values + got[0]
    return (values + got[1]) + (got[0] + got[2])


def reduce_terms(terms):
    share = scatter_sum(terms, "core").astype(BF)
    share = scatter_sum(share, ("y_hi", "y_lo", "x"))
    rows = share.shape[0]
    padded = -(-rows // (8 * lax.axis_size("z_lo"))) * 8 * lax.axis_size("z_lo")
    share = jnp.pad(share, ((0, padded - rows), (0, 0)))
    share = group_sum(scatter_sum(share, "z_lo"), "z_hi").astype(BF)
    share = lax.all_gather(share, "z_lo", tiled=True)[:rows]
    share = lax.all_gather(share, "x", tiled=True)
    share = lax.all_gather(share, ("y_hi", "y_lo"), tiled=True)
    other = lax.ppermute(share, "core", [(0, 1), (1, 0)])
    first = lax.axis_index("core") == 0
    return jnp.where(first, share, other).astype(F32), jnp.where(first, other, share).astype(F32)


def per_device(features, cotangent, block_pos, weight_one, weight_two):
    total_rows = block_pos.shape[0] * 64 * lax.axis_size(NAMES)
    scale = float(total_rows) ** -0.5
    grid_shape = jax.ShapeDtypeStruct((3, ROWS, C), BF)
    face_shape = jax.ShapeDtypeStruct((2, GY * GZ, C), BF)
    fields_shape = jax.ShapeDtypeStruct((2, ROWS, C), BF)
    pad = pltpu.VMEM((PX, PY, GZ, C), BF)
    shifts = pltpu.VMEM((PX, PY, GZ, 3 * C), BF)
    grid, lo, hi = call(
        place_kernel, (grid_shape, face_shape, face_shape), smem=1, args=(block_pos, features, cotangent)
    )
    flip_one, flip_two = flipped(weight_one), flipped(weight_two)
    halo = exchange(grid, lo, hi)
    term = jax.ShapeDtypeStruct((27 * C, C), BF)
    fields, lo, hi, term_one, term_two = call(
        lambda *refs: middle_kernel(scale, *refs),
        (fields_shape, face_shape, face_shape, term, term),
        scratch=(pad, pad, shifts, pltpu.VMEM((ROWS, C), F32)),
        args=(grid, *halo, weight_one, flip_two),
    )
    grad_one, grad_two = reduce_terms(jnp.concatenate([term_one, term_two], axis=0))
    halo = exchange(fields, lo, hi)
    output, input_grad = call(
        final_kernel,
        (jax.ShapeDtypeStruct(features.shape, BF), jax.ShapeDtypeStruct(features.shape, F32)),
        scratch=(pad, shifts),
        smem=1,
        args=(block_pos, grid, fields, *halo, weight_two, flip_one),
    )
    return output, input_grad, grad_one, grad_two


def solution(mesh):
    split = Mesh(mesh.devices.reshape(DIMS), NAMES)
    rows = P(NAMES, None)
    return jax.shard_map(
        per_device,
        mesh=split,
        in_specs=(rows, rows, P(NAMES), P(), P()),
        out_specs=(rows, rows, P(), P()),
        check_vma=False,
    )
```

time: 731 us -> 174 us (0.24); the launches traced: 722 us -> 173 us
  waiting for transfers between devices: 488 us -> 12.9 us
  local copies, waits for them, and re-layouts: 142 us -> 7.25 us
  blocking collectives: 0 us -> 67.1 us
  Pallas kernels: 0 us -> 22.5 us
  matrix products: 17.8 us -> 0 us
  between operations: 15.4 us -> 0.95 us
    psum x1 -> x0, waiting for transfers between devices: 488 us -> none  [per_device(): grad_one, grad_two = lax.psum((term_one, term_two), ('gx', 'gy'))]
    gather x128 -> x0, local copies, waits for them, and re-layouts: 82.9 us -> none
    all_to_all x0 -> x3, blocking collectives: none -> 36.4 us  [scatter_sum(): pieces = lax.all_to_all(values, axes, 0, 0, tiled=True)]
    unnamed x130 -> x16, local copies, waits for them, and re-layouts: 32.7 us -> 0.67 us
    all_gather x0 -> x3, blocking collectives: none -> 30.7 us  [the longest x1 10.9 us: reduce_terms(): share = lax.all_gather(share, ('y_hi', 'y_lo'), tiled=True)]
    pallas_call x0 -> x3, Pallas kernels: none -> 22.5 us  [call(): pl.pallas_call(kernel, out_shape=outs, in_specs=specs, out_specs=jax.tree...]
    another operation x8 -> x0, local copies, waits for them, and re-layouts: 21.9 us -> none  [columns(): stacked = jnp.stack(pieces, axis=4)]
    dot_general x10 -> x0, matrix products: 17.8 us -> none  [the longest x2 10 us: gram(): lax.dot_general(cols, grads, (((0,), (0,)), ((), ())), preferred_element_...]
  transfers between devices with their start and end apart: 17 -> 12, of which waited for: 1 -> 4; matrix products, arithmetic and copies ran while one was open for 11% -> 5% of each run, Pallas kernels for 0% -> 5%
where the time goes in v1:
time: 174 us; the launch traced here: 173 us
  blocking collectives  67.1 us (39%)
  starting transfers between devices  56.4 us (32%)
  Pallas kernels  22.5 us (13%)
  waiting for transfers between devices  12.9 us (7%)
  local copies, waits for them, and re-layouts  7.25 us (4%)
  other arithmetic  5.95 us (3%)
    all_to_all x3, blocking collectives, scatter_sum(): pieces = lax.all_to_all(values, axes, 0, 0, tiled=True)  36.4 us
    pallas_call x3, Pallas kernels, call(): pl.pallas_call(kernel, out_shape=outs, in_specs=specs, out_specs=jax.tree...  22.5 us
    ppermute x3, starting transfers between devices, group_sum(): lax.ppermute(values, axis, [(i, i ^ d) for i in range(count)])  18.3 us
    ppermute x1, starting transfers between devices, reduce_terms(): other = lax.ppermute(share, 'core', [(0, 1), (1, 0)])  14.7 us
    all_gather x1, blocking collectives, reduce_terms(): share = lax.all_gather(share, ('y_hi', 'y_lo'), tiled=True)  10.9 us
    all_gather x1, blocking collectives, reduce_terms(): share = lax.all_gather(share, 'z_lo', tiled=True)[:rows]  10.5 us
    ppermute x2, starting transfers between devices, exchange(): y_lo = lax.ppermute(face(GY - 1), GYN, forward)  9.6 us
    all_gather x1, blocking collectives, reduce_terms(): share = lax.all_gather(share, 'x', tiled=True)  9.3 us
  transfers between devices with their start and end apart: 12, of which 4 were waited for; matrix products, arithmetic and copies ran while one was open for 5% of the time, Pallas kernels for 5%

profile of v1, /device:TPU:1, one launch (start us, length us, event | category | flops | bytes accessed | tf_op | source)
XLA Modules:
  0.0 173.0 jit_solution(12339188291129236788)
XLA Ops:
  0.6 3.0 %shard_map.84 = (bf16[3,1024,128]{2,1,0:T(8,128)(2,1)}, bf16[2,128,128]{2,1,0:T(8,128)(2,1)}, bf16[2,128,128]{2,1,0:T(8,128)(2,1)}) custom-call(s32[8]{0:T(128)} %pos_ref.3, bf16[512,128]{1,0:T(8,128)(2,1)} %feat_ref.1, bf16[512,128]{1,0:T(8,128)(2,1)} %cot_ref.1), custom_call_target="tpu_custom_call" | custom-call | tf_op jit(solution)/shard_map/pallas_call | solution.py:139
  3.6 4.3 %collective-permute-start = (bf16[2,128,128]{2,1,0:T(8,128)(2,1)}, bf16[2,128,128]{2,1,0:T(8,128)(2,1)S(1)}, u32[]{:S(2)}, u32[]{:S(2)}) collective-permute-start(bf16[2,128,128]{2,1,0:T(8,128)(2,1)} %get-tuple-element.15), channel_id=1, source_target_pairs={{0,4},{4,8},{8,12},{12,16},{16,20},{20,24},{24,28},{28,32},{32,36}... | collective-permute-start | bytes 196616 | tf_op jit(solution)/shard_map/ppermute | solution.py:166
  8.0 1.3 collective-permute-start.1
  9.3 1.1 slice.46
  10.4 3.0 %collective-permute-done.1.refs_2_ = bf16[2,128,128]{2,1,0:T(8,128)(2,1)S(1)} collective-permute-done((bf16[2,128,128]{2,1,0:T(8,128)(2,1)}, bf16[2,128,128]{2,1,0:T(8,128)(2,1)S(1)}, u32[]{:S(2)}, u32[]{:S(2)}) %collective-permute-start.1) | collective-permute-done | bytes 65568 | tf_op jit(solution)/shard_map/ppermute | solution.py:167
  13.4 6.6 %collective-permute-start.2 = (bf16[2,160,128]{2,1,0:T(8,128)(2,1)S(1)}, bf16[2,160,128]{2,1,0:T(8,128)(2,1)S(1)}, u32[]{:S(2)}, u32[]{:S(2)}) collective-permute-start(bf16[2,160,128]{2,1,0:T(8,128)(2,1)S(1)} %bitcast.82), channel_id=1, source_target_pairs={{0,1},{1,2},{2,3},{4,5},{5,6},{6,7},{8,9},{9,10},{10,11},{12,13},{... | collective-permute-start | bytes 245768 | tf_op jit(solution)/shard_map/ppermute | solution.py:176
  20.1 1.9 %collective-permute-start.3 = (bf16[2,160,128]{2,1,0:T(8,128)(2,1)S(1)}, bf16[2,160,128]{2,1,0:T(8,128)(2,1)S(1)}, u32[]{:S(2)}, u32[]{:S(2)}) collective-permute-start(bf16[2,160,128]{2,1,0:T(8,128)(2,1)S(1)} %bitcast.83), channel_id=1, source_target_pairs={{1,0},{2,1},{3,2},{5,4},{6,5},{7,6},{9,8},{10,9},{11,10},{13,12},{... | collective-permute-start | bytes 245768 | tf_op jit(solution)/shard_map/ppermute | solution.py:177
  22.0 1.3 copy.29
  23.3 1.0 rev.6
  24.3 3.0 %collective-permute-done.3.refs_4_ = bf16[2,160,128]{2,1,0:T(8,128)(2,1)S(1)} collective-permute-done((bf16[2,160,128]{2,1,0:T(8,128)(2,1)S(1)}, bf16[2,160,128]{2,1,0:T(8,128)(2,1)S(1)}, u32[]{:S(2)}, u32[]{:S(2)}) %collective-permute-start.3) | collective-permute-done | bytes 81952 | tf_op jit(solution)/shard_map/ppermute | solution.py:177
  28.0 10.8 %shard_map.85 = (bf16[2,1024,128]{2,1,0:T(8,128)(2,1)}, bf16[2,128,128]{2,1,0:T(8,128)(2,1)}, bf16[2,128,128]{2,1,0:T(8,128)(2,1)}, bf16[3456,128]{1,0:T(8,128)(2,1)}, bf16[3456,128]{1,0:T(8,128)(2,1)}) custom-call(bf16[3,1024,128]{2,1,0:T(8,128)(2,1)} %get-tuple-element.14.refs_0_.grid_ref, bf16[2,128,128]{2,1,0:T(8,128)(2,1)} %copy-done.4, ...), custom_call_target="tpu_custom_call" | custom-call | tf_op jit(solution)/shard_map/pallas_call | solution.py:139
  38.7 1.5 pad_maximum_fusion
  40.3 4.8 %all_to_all.27 = bf16[2,3456,128]{2,1,0:T(8,128)(2,1)S(1)} all-to-all(bf16[2,3456,128]{2,1,0:T(8,128)(2,1)S(1)} %bitcast.69), channel_id=1, replica_groups=mesh['y_lo'=2,'x'=4,'z_hi'=4,'z_lo'=4,'y_hi'=2,'core'=2] {'core'}, dimensions={0} | all-to-all | bytes 3538944 | tf_op jit(solution)/shard_map/all_to_all | solution.py:183
  46.0 24.3 %all_to_all.28 = bf16[16,216,128]{2,1,0:T(8,128)(2,1)S(1)} all-to-all(bf16[16,216,128]{2,1,0:T(8,128)(2,1)S(1)} %bitcast.74), channel_id=1, replica_groups=mesh['y_lo'=2,'x'=4,'z_hi'=4,'z_lo'=4,'y_hi'=2,'core'=2] {'y_hi','y_lo',..., dimensions={0} | all-to-all | bytes 1769472 | tf_op jit(solution)/shard_map/all_to_all | solution.py:183
  70.4 7.4 %all_to_all.29 = f32[4,56,128]{2,1,0:T(8,128)S(1)} all-to-all(f32[4,56,128]{2,1,0:T(8,128)S(1)} %bitcast.77), channel_id=1, replica_groups=mesh['y_lo'=2,'x'=4,'z_hi'=4,'z_lo'=4,'y_hi'=2,'core'=2] {'z_lo'}, dimensions={0} | all-to-all | bytes 229376 | tf_op jit(solution)/shard_map/all_to_all | solution.py:183
  77.8 9.3 %collective-permute-start.10 = (f32[56,128]{1,0:T(8,128)S(1)}, f32[56,128]{1,0:T(8,128)S(1)}, u32[]{:S(2)}, u32[]{:S(2)}) collective-permute-start(f32[56,128]{1,0:T(8,128)S(1)} %reduce_sum.32), channel_id=1, source_target_pairs={{0,48},{16,32},{32,16},{48,0},{1,49},{17,33},{33,17},{49,1},{2,50}... | collective-permute-start | bytes 86024 | tf_op jit(solution)/shard_map/ppermute | solution.py:189
  87.1 3.5 %collective-permute-start.9 = (f32[56,128]{1,0:T(8,128)S(1)}, f32[56,128]{1,0:T(8,128)S(1)}, u32[]{:S(2)}, u32[]{:S(2)}) collective-permute-start(f32[56,128]{1,0:T(8,128)S(1)} %reduce_sum.32), channel_id=1, source_target_pairs={{0,16},{16,0},{32,48},{48,32},{1,17},{17,1},{33,49},{49,33},{2,18}... | collective-permute-start | bytes 86024 | tf_op jit(solution)/shard_map/ppermute | solution.py:189
  90.6 5.4 %collective-permute-start.8 = (f32[56,128]{1,0:T(8,128)S(1)}, f32[56,128]{1,0:T(8,128)S(1)}, u32[]{:S(2)}, u32[]{:S(2)}) collective-permute-start(f32[56,128]{1,0:T(8,128)S(1)} %reduce_sum.32), channel_id=1, source_target_pairs={{0,32},{16,48},{32,0},{48,16},{1,33},{17,49},{33,1},{49,17},{2,34}... | collective-permute-start | bytes 86024 | tf_op jit(solution)/shard_map/ppermute | solution.py:189
  96.1 2.8 %collective-permute-start.4 = (bf16[2,128,128]{2,1,0:T(8,128)(2,1)}, bf16[2,128,128]{2,1,0:T(8,128)(2,1)S(1)}, u32[]{:S(2)}, u32[]{:S(2)}) collective-permute-start(bf16[2,128,128]{2,1,0:T(8,128)(2,1)} %get-tuple-element.18), channel_id=1, source_target_pairs={{0,4},{4,8},{8,12},{12,16},{16,20},{20,24},{24,28},{28,32},{32,36}... | collective-permute-start | bytes 196616 | tf_op jit(solution)/shard_map/ppermute | solution.py:166
  98.9 1.3 collective-permute-start.5
  100.2 3.8 %collective-permute-done.8 = f32[56,128]{1,0:T(8,128)S(1)} collective-permute-done((f32[56,128]{1,0:T(8,128)S(1)}, f32[56,128]{1,0:T(8,128)S(1)}, u32[]{:S(2)}, u32[]{:S(2)}) %collective-permute-start.8) | collective-permute-done | bytes 28704 | tf_op jit(solution)/shard_map/ppermute | solution.py:189
  104.0 10.5 %all_gather.9 = bf16[224,128]{1,0:T(8,128)(2,1)S(1)} all-gather(bf16[56,128]{1,0:T(8,128)(2,1)S(1)} %add_convert_fusion), channel_id=1, replica_groups=mesh['y_lo'=2,'x'=4,'z_hi'=4,'z_lo'=4,'y_hi'=2,'core'=2] {'z_lo'}, dimensions={0}, use_global_device_ids=true | all-gather | bytes 71680 | tf_op jit(solution)/shard_map/all_gather | solution.py:204
  114.5 9.3 %all_gather.10 = bf16[864,128]{1,0:T(8,128)(2,1)S(1)} all-gather(bf16[216,128]{1,0:T(8,128)(2,1)S(1)} %slice.72), channel_id=1, replica_groups=mesh['y_lo'=2,'x'=4,'z_hi'=4,'z_lo'=4,'y_hi'=2,'core'=2] {'x'}, dimensions={0}, use_global_device_ids=true | all-gather | bytes 276480 | tf_op jit(solution)/shard_map/all_gather | solution.py:205
  123.8 10.9 %all_gather.11 = bf16[3456,128]{1,0:T(8,128)(2,1)S(1)} all-gather(bf16[864,128]{1,0:T(8,128)(2,1)S(1)} %all_gather.10), channel_id=1, replica_groups=mesh['y_lo'=2,'x'=4,'z_hi'=4,'z_lo'=4,'y_hi'=2,'core'=2] {'y_hi','y_lo'}, dimensions={0}, use_global_device_ids=true | all-gather | bytes 1105920 | tf_op jit(solution)/shard_map/all_gather | solution.py:206
  134.7 14.7 %collective-permute-start.11 = (bf16[3456,128]{1,0:T(8,128)(2,1)S(1)}, bf16[3456,128]{1,0:T(8,128)(2,1)S(1)}, u32[]{:S(2)}, u32[]{:S(2)}) collective-permute-start(bf16[3456,128]{1,0:T(8,128)(2,1)S(1)} %all_gather.11), channel_id=1, source_target_pairs={{0,1},{1,0},{2,3},{3,2},{4,5},{5,4},{6,7},{7,6},{8,9},{9,8},{10,11... | collective-permute-start | bytes 2654216 | tf_op jit(solution)/shard_map/ppermute | solution.py:207
  151.0 3.0 %collective-permute-start.6 = (bf16[2,160,128]{2,1,0:T(8,128)(2,1)}, bf16[2,160,128]{2,1,0:T(8,128)(2,1)}, u32[]{:S(2)}, u32[]{:S(2)}) collective-permute-start(bf16[2,160,128]{2,1,0:T(8,128)(2,1)} %bitcast.20), channel_id=1, source_target_pairs={{0,1},{1,2},{2,3},{4,5},{5,6},{6,7},{8,9},{9,10},{10,11},{12,13},{... | collective-permute-start | bytes 245768 | tf_op jit(solution)/shard_map/ppermute | solution.py:176
  154.7 2.1 %collective-permute-start.7 = (bf16[2,160,128]{2,1,0:T(8,128)(2,1)}, bf16[2,160,128]{2,1,0:T(8,128)(2,1)}, u32[]{:S(2)}, u32[]{:S(2)}) collective-permute-start(bf16[2,160,128]{2,1,0:T(8,128)(2,1)} %bitcast.24), channel_id=1, source_target_pairs={{1,0},{2,1},{3,2},{5,4},{6,5},{7,6},{9,8},{10,9},{11,10},{13,12},{... | collective-permute-start | bytes 245768 | tf_op jit(solution)/shard_map/ppermute | solution.py:177
  156.8 1.3 copy.36
  158.2 1.0 rev.7
  159.1 3.1 %collective-permute-done.7.yhi_ref = bf16[2,160,128]{2,1,0:T(8,128)(2,1)} collective-permute-done((bf16[2,160,128]{2,1,0:T(8,128)(2,1)}, bf16[2,160,128]{2,1,0:T(8,128)(2,1)}, u32[]{:S(2)}, u32[]{:S(2)}) %collective-permute-start.7) | collective-permute-done | bytes 81952 | tf_op jit(solution)/shard_map/ppermute | solution.py:177
  162.2 8.7 %shard_map.86 = (bf16[512,128]{1,0:T(8,128)(2,1)}, f32[512,128]{1,0:T(8,128)}) custom-call(s32[8]{0:T(128)} %pos_ref.3, bf16[3,1024,128]{2,1,0:T(8,128)(2,1)} %get-tuple-element.14.refs_0_.grid_ref, bf16[2,1024,128]{2,1,0:T(8,128)(2,1)} %get-tuple-element.17.fields_ref, bf16[2,128,128]{2,1,0:T(8,128)(2,1)} %copy-done.2, bf16[2,128,128]{2,1,0:T(8,128)(2,1)} %copy-done.3, ...), custom_call_target="tpu_custom_call" | custom-call | tf_op jit(solution)/shard_map/pallas_call | solution.py:139
  171.0 2.0 %select_convert_fusion = (f32[3456,128]{1,0:T(8,128)}, f32[3456,128]{1,0:T(8,128)}) fusion(bf16[3456,128]{1,0:T(8,128)(2,1)S(1)} %collective-permute-done.11, bf16[3456,128]{1,0:T(8,128)(2,1)S(1)} %all_gather.11, pred[]{:T(512)S(6)} %eq.3), kind=kLoop, calls=%fused_computation.2 | loop fusion | flops 1769472 | bytes 5308417 | tf_op jit(solution)/shard_map/convert_element_type | solution.py:209
  (40 shorter events, 4.0 us)
Async XLA Ops:
  0.6 21.4 %copy-start.1 = (bf16[3456,128]{1,0:T(8,128)(2,1)S(1)}, bf16[3456,128]{1,0:T(8,128)(2,1)}, u32[]{:S(2)}) copy-start(bf16[3456,128]{1,0:T(8,128)(2,1)} %w2_ref.1) | copy-start | bytes 2654212
  3.6 6.8 %collective-permute-start = (bf16[2,128,128]{2,1,0:T(8,128)(2,1)}, bf16[2,128,128]{2,1,0:T(8,128)(2,1)S(1)}, u32[]{:S(2)}, u32[]{:S(2)}) collective-permute-start(bf16[2,128,128]{2,1,0:T(8,128)(2,1)} %get-tuple-element.15), channel_id=1, source_target_pairs={{0,4},{4,8},{8,12},{12,16},{16,20},{20,24},{24,28},{28,32},{32,36}... | collective-permute-start | bytes 196616 | tf_op jit(solution)/shard_map/ppermute | solution.py:166
  8.0 5.4 %collective-permute-start.1 = (bf16[2,128,128]{2,1,0:T(8,128)(2,1)}, bf16[2,128,128]{2,1,0:T(8,128)(2,1)S(1)}, u32[]{:S(2)}, u32[]{:S(2)}) collective-permute-start(bf16[2,128,128]{2,1,0:T(8,128)(2,1)} %get-tuple-element.16), channel_id=1, source_target_pairs={{4,0},{8,4},{12,8},{16,12},{20,16},{24,20},{28,24},{32,28},{36,32}... | collective-permute-start | bytes 196616 | tf_op jit(solution)/shard_map/ppermute | solution.py:167
  10.4 13.9 %copy-start.4 = (bf16[2,128,128]{2,1,0:T(8,128)(2,1)}, bf16[2,128,128]{2,1,0:T(8,128)(2,1)S(1)}, u32[]{:S(2)}) copy-start(bf16[2,128,128]{2,1,0:T(8,128)(2,1)S(1)} %collective-permute-done.refs_1_) | copy-start | bytes 196612
  13.4 10.9 %copy-start.5 = (bf16[2,128,128]{2,1,0:T(8,128)(2,1)}, bf16[2,128,128]{2,1,0:T(8,128)(2,1)S(1)}, u32[]{:S(2)}) copy-start(bf16[2,128,128]{2,1,0:T(8,128)(2,1)S(1)} %collective-permute-done.1.refs_2_) | copy-start | bytes 196612
  13.4 10.9 %collective-permute-start.2 = (bf16[2,160,128]{2,1,0:T(8,128)(2,1)S(1)}, bf16[2,160,128]{2,1,0:T(8,128)(2,1)S(1)}, u32[]{:S(2)}, u32[]{:S(2)}) collective-permute-start(bf16[2,160,128]{2,1,0:T(8,128)(2,1)S(1)} %bitcast.82), channel_id=1, source_target_pairs={{0,1},{1,2},{2,3},{4,5},{5,6},{6,7},{8,9},{9,10},{10,11},{12,13},{... | collective-permute-start | bytes 245768 | tf_op jit(solution)/shard_map/ppermute | solution.py:176
  20.1 7.3 %collective-permute-start.3 = (bf16[2,160,128]{2,1,0:T(8,128)(2,1)S(1)}, bf16[2,160,128]{2,1,0:T(8,128)(2,1)S(1)}, u32[]{:S(2)}, u32[]{:S(2)}) collective-permute-start(bf16[2,160,128]{2,1,0:T(8,128)(2,1)S(1)} %bitcast.83), channel_id=1, source_target_pairs={{1,0},{2,1},{3,2},{5,4},{6,5},{7,6},{9,8},{10,9},{11,10},{13,12},{... | collective-permute-start | bytes 245768 | tf_op jit(solution)/shard_map/ppermute | solution.py:177
  24.3 3.0 %copy-start.6 = (bf16[2,160,128]{2,1,0:T(8,128)(2,1)}, bf16[2,160,128]{2,1,0:T(8,128)(2,1)S(1)}, u32[]{:S(2)}) copy-start(bf16[2,160,128]{2,1,0:T(8,128)(2,1)S(1)} %collective-permute-done.2.refs_3_) | copy-start | bytes 245764
  27.3 0.6 copy-start.7
  70.3 86.6 %copy-start = (bf16[3456,128]{1,0:T(8,128)(2,1)S(1)}, bf16[3456,128]{1,0:T(8,128)(2,1)}, u32[]{:S(2)}) copy-start(bf16[3456,128]{1,0:T(8,128)(2,1)} %refs_5_.1) | copy-start | bytes 2654212
  77.8 22.4 %collective-permute-start.10 = (f32[56,128]{1,0:T(8,128)S(1)}, f32[56,128]{1,0:T(8,128)S(1)}, u32[]{:S(2)}, u32[]{:S(2)}) collective-permute-start(f32[56,128]{1,0:T(8,128)S(1)} %reduce_sum.32), channel_id=1, source_target_pairs={{0,48},{16,32},{32,16},{48,0},{1,49},{17,33},{33,17},{49,1},{2,50}... | collective-permute-start | bytes 86024 | tf_op jit(solution)/shard_map/ppermute | solution.py:189
  87.1 13.1 %collective-permute-start.9 = (f32[56,128]{1,0:T(8,128)S(1)}, f32[56,128]{1,0:T(8,128)S(1)}, u32[]{:S(2)}, u32[]{:S(2)}) collective-permute-start(f32[56,128]{1,0:T(8,128)S(1)} %reduce_sum.32), channel_id=1, source_target_pairs={{0,16},{16,0},{32,48},{48,32},{1,17},{17,1},{33,49},{49,33},{2,18}... | collective-permute-start | bytes 86024 | tf_op jit(solution)/shard_map/ppermute | solution.py:189
  90.6 13.3 %collective-permute-start.8 = (f32[56,128]{1,0:T(8,128)S(1)}, f32[56,128]{1,0:T(8,128)S(1)}, u32[]{:S(2)}, u32[]{:S(2)}) collective-permute-start(f32[56,128]{1,0:T(8,128)S(1)} %reduce_sum.32), channel_id=1, source_target_pairs={{0,32},{16,48},{32,0},{48,16},{1,33},{17,49},{33,1},{49,17},{2,34}... | collective-permute-start | bytes 86024 | tf_op jit(solution)/shard_map/ppermute | solution.py:189
  96.1 54.2 %collective-permute-start.4 = (bf16[2,128,128]{2,1,0:T(8,128)(2,1)}, bf16[2,128,128]{2,1,0:T(8,128)(2,1)S(1)}, u32[]{:S(2)}, u32[]{:S(2)}) collective-permute-start(bf16[2,128,128]{2,1,0:T(8,128)(2,1)} %get-tuple-element.18), channel_id=1, source_target_pairs={{0,4},{4,8},{8,12},{12,16},{16,20},{20,24},{24,28},{28,32},{32,36}... | collective-permute-start | bytes 196616 | tf_op jit(solution)/shard_map/ppermute | solution.py:166
  98.9 51.5 %collective-permute-start.5 = (bf16[2,128,128]{2,1,0:T(8,128)(2,1)}, bf16[2,128,128]{2,1,0:T(8,128)(2,1)S(1)}, u32[]{:S(2)}, u32[]{:S(2)}) collective-permute-start(bf16[2,128,128]{2,1,0:T(8,128)(2,1)} %get-tuple-element.19), channel_id=1, source_target_pairs={{4,0},{8,4},{12,8},{16,12},{20,16},{24,20},{28,24},{32,28},{36,32}... | collective-permute-start | bytes 196616 | tf_op jit(solution)/shard_map/ppermute | solution.py:167
  134.7 36.3 %collective-permute-start.11 = (bf16[3456,128]{1,0:T(8,128)(2,1)S(1)}, bf16[3456,128]{1,0:T(8,128)(2,1)S(1)}, u32[]{:S(2)}, u32[]{:S(2)}) collective-permute-start(bf16[3456,128]{1,0:T(8,128)(2,1)S(1)} %all_gather.11), channel_id=1, source_target_pairs={{0,1},{1,0},{2,3},{3,2},{4,5},{5,4},{6,7},{7,6},{8,9},{9,8},{10,11... | collective-permute-start | bytes 2654216 | tf_op jit(solution)/shard_map/ppermute | solution.py:207
  150.3 6.5 %copy-start.2 = (bf16[2,128,128]{2,1,0:T(8,128)(2,1)}, bf16[2,128,128]{2,1,0:T(8,128)(2,1)S(1)}, u32[]{:S(2)}) copy-start(bf16[2,128,128]{2,1,0:T(8,128)(2,1)S(1)} %collective-permute-done.4.xlo_ref) | copy-start | bytes 196612
  150.4 6.5 %copy-start.3 = (bf16[2,128,128]{2,1,0:T(8,128)(2,1)}, bf16[2,128,128]{2,1,0:T(8,128)(2,1)S(1)}, u32[]{:S(2)}) copy-start(bf16[2,128,128]{2,1,0:T(8,128)(2,1)S(1)} %collective-permute-done.5.xhi_ref) | copy-start | bytes 196612
  151.0 8.1 %collective-permute-start.6 = (bf16[2,160,128]{2,1,0:T(8,128)(2,1)}, bf16[2,160,128]{2,1,0:T(8,128)(2,1)}, u32[]{:S(2)}, u32[]{:S(2)}) collective-permute-start(bf16[2,160,128]{2,1,0:T(8,128)(2,1)} %bitcast.20), channel_id=1, source_target_pairs={{0,1},{1,2},{2,3},{4,5},{5,6},{6,7},{8,9},{9,10},{10,11},{12,13},{... | collective-permute-start | bytes 245768 | tf_op jit(solution)/shard_map/ppermute | solution.py:176
  154.7 7.6 %collective-permute-start.7 = (bf16[2,160,128]{2,1,0:T(8,128)(2,1)}, bf16[2,160,128]{2,1,0:T(8,128)(2,1)}, u32[]{:S(2)}, u32[]{:S(2)}) collective-permute-start(bf16[2,160,128]{2,1,0:T(8,128)(2,1)} %bitcast.24), channel_id=1, source_target_pairs={{1,0},{2,1},{3,2},{5,4},{6,5},{7,6},{9,8},{10,9},{11,10},{13,12},{... | collective-permute-start | bytes 245768 | tf_op jit(solution)/shard_map/ppermute | solution.py:177

commit v2 on v1

--- a/solution.py
+++ b/solution.py
@@ -53,12 +53,12 @@
     grid_ref[2] = dot(perm, jnp.ones((SLOTS * 64, C), BF)).astype(BF)
 
 
-def z_shifts(field):
+def z_shifts(field, flip=False):
     rows = field.shape[0]
     wide = field.astype(F32)
     before = pltpu.roll(wide, 1, 0).astype(BF)
     after = pltpu.roll(wide, rows - 1, 0).astype(BF)
-    return jnp.concatenate([before, field, after], axis=1)
+    return jnp.concatenate([after, field, before] if flip else [before, field, after], axis=1)
 
 
 def fill_pad(pad_ref, grid, x_lo, x_hi, y_lo, y_hi):
@@ -69,27 +69,28 @@
     pad_ref[:, PY - 1] = y_hi.reshape(PX, GZ, C)
 
 
-def conv(shift_ref, w_ref):
+def conv(shift_ref, w_ref, flip):
     acc = None
     for k in range(9):
         dx, dy = divmod(k, 3)
         lhs = shift_ref[dx : dx + GX, dy : dy + GY].reshape(ROWS, 3 * C)
-        term = dot(lhs, w_ref[k * 3 * C : (k + 1) * 3 * C, :])
+        at = 8 - k if flip else k
+        term = dot(lhs, w_ref[at * 3 * C : (at + 1) * 3 * C, :])
         acc = term if acc is None else acc + term
     return acc
 
 
 def middle_kernel(
     scale, grid_ref, xlo_ref, xhi_ref, ylo_ref, yhi_ref, w1_ref, w2f_ref,
-    fields_ref, lo_ref, hi_ref, term1_ref, term2_ref, padx_ref, padu_ref, shift_ref, pre_ref,
+    fields_ref, lo_ref, hi_ref, terms_ref, padx_ref, padu_ref, shift_ref, pre_ref,
 ):
     mask = grid_ref[2].astype(F32)
     fill_pad(padx_ref, grid_ref[0], xlo_ref[0], xhi_ref[0], ylo_ref[0], yhi_ref[0])
     fill_pad(padu_ref, grid_ref[1], xlo_ref[1], xhi_ref[1], ylo_ref[1], yhi_ref[1])
     shift_ref[...] = z_shifts(padx_ref[...].reshape(PAD_ROWS, C)).reshape(PX, PY, GZ, 3 * C)
-    pre_ref[...] = conv(shift_ref, w1_ref)
-    shift_ref[...] = z_shifts(padu_ref[...].reshape(PAD_ROWS, C)).reshape(PX, PY, GZ, 3 * C)
-    back = conv(shift_ref, w2f_ref)
+    pre_ref[...] = conv(shift_ref, w1_ref, False)
+    shift_ref[...] = z_shifts(padu_ref[...].reshape(PAD_ROWS, C), True).reshape(PX, PY, GZ, 3 * C)
+    back = conv(shift_ref, w2f_ref, True)
     pre = pre_ref[...]
     sig = jax.nn.sigmoid(pre)
     hidden = (pre * sig * mask).astype(BF)
@@ -103,7 +104,7 @@
     for k in range(9):
         dx, dy = divmod(k, 3)
         rhs = padu_ref[2 - dx : 2 - dx + GX, 2 - dy : 2 - dy + GY].reshape(ROWS, C)
-        term2_ref[k * 3 * C : (k + 1) * 3 * C, :] = (dot(hz, rhs) * scale).astype(term2_ref.dtype)
+        terms_ref[(27 + 3 * k) * C : (30 + 3 * k) * C, :] = (dot(hz, rhs) * scale).astype(BF)
     gz = z_shifts(hgrad).T
     for k in range(9):
         dx, dy = divmod(k, 3)
@@ -111,7 +112,7 @@
         prod = dot(gz, rhs) * scale
         for oz in range(3):
             block = prod[(2 - oz) * C : (3 - oz) * C, :].T
-            term1_ref[(3 * k + oz) * C : (3 * k + oz + 1) * C, :] = block.astype(term1_ref.dtype)
+            terms_ref[(3 * k + oz) * C : (3 * k + oz + 1) * C, :] = block.astype(BF)
 
 
 def final_kernel(
@@ -123,8 +124,8 @@
     perm = (rows == target).astype(F32).astype(BF)
     for field, w_ref in enumerate((w2_ref, w1f_ref)):
         fill_pad(pad_ref, fields_ref[field], xlo_ref[field], xhi_ref[field], ylo_ref[field], yhi_ref[field])
-        shift_ref[...] = z_shifts(pad_ref[...].reshape(PAD_ROWS, C)).reshape(PX, PY, GZ, 3 * C)
-        value = conv(shift_ref, w_ref) + grid_ref[field].astype(F32)
+        shift_ref[...] = z_shifts(pad_ref[...].reshape(PAD_ROWS, C), field == 1).reshape(PX, PY, GZ, 3 * C)
+        value = conv(shift_ref, w_ref, field == 1) + grid_ref[field].astype(F32)
         high = value.astype(BF)
         if field == 0:
             out_ref[...] = dot(perm, high).astype(BF)
@@ -147,8 +148,8 @@
     )(*args)
 
 
-def flipped(weight):
-    return weight.reshape(27, C, C)[::-1].transpose(0, 2, 1).reshape(27 * C, C)
+def transposed(weight):
+    return weight.reshape(27, C, C).transpose(0, 2, 1).reshape(27 * C, C)
 
 
 def ring(axes):
@@ -159,6 +160,7 @@
 
 GXN = ("y_lo", "x", "z_hi", "z_lo")
 GYN = ("y_hi", "core")
+YX = ("y_hi", "y_lo", "x")
 
 
 def exchange(fields, lo, hi):
@@ -178,32 +180,29 @@
     return x_lo, x_hi, y_lo, y_hi
 
 
+def swap(values, axes):
+    return lax.all_to_all(values, axes, 0, 0, tiled=True)
+
+
 def scatter_sum(values, axes):
     count = lax.axis_size(axes)
-    pieces = lax.all_to_all(values, axes, 0, 0, tiled=True)
-    return pieces.reshape(count, -1, C).astype(F32).sum(axis=0)
-
-
-def group_sum(values, axis):
-    count = lax.axis_size(axis)
-    got = [lax.ppermute(values, axis, [(i, i ^ d) for i in range(count)]) for d in range(1, count)]
-    if count == 1:
-        return values
-    if count == 2:
-        return values + got[0]
-    return (values + got[1]) + (got[0] + got[2])
+    return swap(values.reshape(count, -1, C), axes).astype(F32).sum(axis=0)
+
+
+def gather(values, axes):
+    return swap(jnp.broadcast_to(values, (lax.axis_size(axes), *values.shape)), axes)
 
 
 def reduce_terms(terms):
     share = scatter_sum(terms, "core").astype(BF)
-    share = scatter_sum(share, ("y_hi", "y_lo", "x"))
+    share = scatter_sum(share, YX)
     rows = share.shape[0]
     padded = -(-rows // (8 * lax.axis_size("z_lo"))) * 8 * lax.axis_size("z_lo")
     share = jnp.pad(share, ((0, padded - rows), (0, 0)))
-    share = group_sum(scatter_sum(share, "z_lo"), "z_hi").astype(BF)
-    share = lax.all_gather(share, "z_lo", tiled=True)[:rows]
-    share = lax.all_gather(share, "x", tiled=True)
-    share = lax.all_gather(share, ("y_hi", "y_lo"), tiled=True)
+    share = scatter_sum(share, "z_lo")
+    share = gather(share, "z_hi").sum(axis=0).astype(BF)
+    share = gather(share, "z_lo").reshape(padded, C)[:rows]
+    share = gather(share, YX).reshape(-1, C)
     other = lax.ppermute(share, "core", [(0, 1), (1, 0)])
     first = lax.axis_index("core") == 0
     return jnp.where(first, share, other).astype(F32), jnp.where(first, other, share).astype(F32)
@@ -220,16 +219,16 @@
     grid, lo, hi = call(
         place_kernel, (grid_shape, face_shape, face_shape), smem=1, args=(block_pos, features, cotangent)
     )
-    flip_one, flip_two = flipped(weight_one), flipped(weight_two)
+    flip_one, flip_two = transposed(weight_one), transposed(weight_two)
     halo = exchange(grid, lo, hi)
-    term = jax.ShapeDtypeStruct((27 * C, C), BF)
-    fields, lo, hi, term_one, term_two = call(
+    terms_shape = jax.ShapeDtypeStruct((54 * C, C), BF)
+    fields, lo, hi, terms = call(
         lambda *refs: middle_kernel(scale, *refs),
-        (fields_shape, face_shape, face_shape, term, term),
+        (fields_shape, face_shape, face_shape, terms_shape),
         scratch=(pad, pad, shifts, pltpu.VMEM((ROWS, C), F32)),
         args=(grid, *halo, weight_one, flip_two),
     )
-    grad_one, grad_two = reduce_terms(jnp.concatenate([term_one, term_two], axis=0))
+    grad_one, grad_two = reduce_terms(terms)
     halo = exchange(fields, lo, hi)
     output, input_grad = call(
         final_kernel,

time: 174 us -> 159 us (0.914)
  starting transfers between devices: 56.4 us -> 37.6 us
  waiting for transfers between devices: 12.9 us -> 16.4 us
  other arithmetic: 5.95 us -> 3.19 us
  blocking collectives: 67.1 us -> 69.8 us
    all_to_all x3 -> x5, blocking collectives: 36.4 us -> 69.8 us  [swap(): return lax.all_to_all(values, axes, 0, 0, tiled=True)]
    all_gather x3 -> x0, blocking collectives: 30.7 us -> none  [the longest x1 10.9 us: reduce_terms(): share = lax.all_gather(share, ('y_hi', 'y_lo'), tiled=True)]
    ppermute x3 -> x0, starting transfers between devices: 18.3 us -> none  [group_sum(): lax.ppermute(values, axis, [(i, i ^ d) for i in range(count)])]
    all_to_all x0 -> x1, waiting for transfers between devices: none -> 9.24 us  [swap(): return lax.all_to_all(values, axes, 0, 0, tiled=True)]
    ppermute x2, waiting for transfers between devices: 6.09 us -> 0.01 us  [exchange(): y_hi = lax.ppermute(face(0), GYN, backward)]
    ppermute x1, starting transfers between devices: 14.7 us -> 8.77 us  [reduce_terms(): other = lax.ppermute(share, 'core', [(0, 1), (1, 0)])]
    ppermute x2, starting transfers between devices: 4.06 us -> 9.42 us  [exchange(): y_hi = lax.ppermute(face(0), GYN, backward)]
    ppermute x2, waiting for transfers between devices: 2.98 us -> 7.17 us  [exchange(): x_hi = lax.ppermute(lo, GXN, backward)]
  transfers between devices with their start and end apart: 12 -> 10, of which waited for: 4 -> 3; matrix products, arithmetic and copies ran while one was open for 5% -> 3% of each run, Pallas kernels for 5% -> 6%
where the time goes in v2:
time: 159 us; the launch traced here: 158 us
  blocking collectives  69.8 us (44%)
  starting transfers between devices  37.6 us (24%)
  Pallas kernels  22.5 us (14%)
  waiting for transfers between devices  16.4 us (10%)
  local copies, waits for them, and re-layouts  7.62 us (5%)
  other arithmetic  3.19 us (2%)
    all_to_all x5, blocking collectives, swap(): return lax.all_to_all(values, axes, 0, 0, tiled=True)  69.8 us
    pallas_call x3, Pallas kernels, call(): pl.pallas_call(kernel, out_shape=outs, in_specs=specs, out_specs=jax.tree...  22.5 us
    ppermute x2, starting transfers between devices, exchange(): y_hi = lax.ppermute(face(0), GYN, backward)  9.42 us
    all_to_all x1, waiting for transfers between devices, swap(): return lax.all_to_all(values, axes, 0, 0, tiled=True)  9.24 us
    ppermute x1, starting transfers between devices, reduce_terms(): other = lax.ppermute(share, 'core', [(0, 1), (1, 0)])  8.77 us
    ppermute x2, waiting for transfers between devices, exchange(): x_hi = lax.ppermute(lo, GXN, backward)  7.17 us
    ppermute x2, starting transfers between devices, exchange(): x_lo = lax.ppermute(hi, GXN, forward)  6.85 us
    ppermute x2, starting transfers between devices, exchange(): y_lo = lax.ppermute(face(GY - 1), GYN, forward)  6.39 us
  transfers between devices with their start and end apart: 10, of which 3 were waited for; matrix products, arithmetic and copies ran while one was open for 3% of the time, Pallas kernels for 6%

profile of v2, /device:TPU:1, one launch (start us, length us, event | category | flops | bytes accessed | tf_op | source)
XLA Modules:
  0.0 158.2 jit_solution(6601844431965752353)
XLA Ops:
  0.6 2.9 %shard_map.84 = (bf16[3,1024,128]{2,1,0:T(8,128)(2,1)}, bf16[2,128,128]{2,1,0:T(8,128)(2,1)}, bf16[2,128,128]{2,1,0:T(8,128)(2,1)}) custom-call(s32[8]{0:T(128)} %pos_ref.3, bf16[512,128]{1,0:T(8,128)(2,1)} %feat_ref.1, bf16[512,128]{1,0:T(8,128)(2,1)} %cot_ref.1), custom_call_target="tpu_custom_call" | custom-call | tf_op jit(solution)/shard_map/pallas_call | solution.py:140
  3.6 4.3 %collective-permute-start = (bf16[2,128,128]{2,1,0:T(8,128)(2,1)}, bf16[2,128,128]{2,1,0:T(8,128)(2,1)S(1)}, u32[]{:S(2)}, u32[]{:S(2)}) collective-permute-start(bf16[2,128,128]{2,1,0:T(8,128)(2,1)} %get-tuple-element.14), channel_id=1, source_target_pairs={{0,4},{4,8},{8,12},{12,16},{16,20},{20,24},{24,28},{28,32},{32,36}... | collective-permute-start | bytes 196616 | tf_op jit(solution)/shard_map/ppermute | solution.py:168
  7.9 1.3 collective-permute-start.1
  9.2 1.1 slice.46
  10.4 3.0 %collective-permute-done.1.refs_2_ = bf16[2,128,128]{2,1,0:T(8,128)(2,1)S(1)} collective-permute-done((bf16[2,128,128]{2,1,0:T(8,128)(2,1)}, bf16[2,128,128]{2,1,0:T(8,128)(2,1)S(1)}, u32[]{:S(2)}, u32[]{:S(2)}) %collective-permute-start.1) | collective-permute-done | bytes 65568 | tf_op jit(solution)/shard_map/ppermute | solution.py:169
  13.4 6.6 %collective-permute-start.3 = (bf16[2,160,128]{2,1,0:T(8,128)(2,1)S(1)}, bf16[2,160,128]{2,1,0:T(8,128)(2,1)S(1)}, u32[]{:S(2)}, u32[]{:S(2)}) collective-permute-start(bf16[2,160,128]{2,1,0:T(8,128)(2,1)S(1)} %bitcast.90), channel_id=1, source_target_pairs={{1,0},{2,1},{3,2},{5,4},{6,5},{7,6},{9,8},{10,9},{11,10},{13,12},{... | collective-permute-start | bytes 245768 | tf_op jit(solution)/shard_map/ppermute | solution.py:179
  20.0 1.9 %collective-permute-start.2 = (bf16[2,160,128]{2,1,0:T(8,128)(2,1)S(1)}, bf16[2,160,128]{2,1,0:T(8,128)(2,1)S(1)}, u32[]{:S(2)}, u32[]{:S(2)}) collective-permute-start(bf16[2,160,128]{2,1,0:T(8,128)(2,1)S(1)} %bitcast.91), channel_id=1, source_target_pairs={{0,1},{1,2},{2,3},{4,5},{5,6},{6,7},{8,9},{9,10},{10,11},{12,13},{... | collective-permute-start | bytes 245768 | tf_op jit(solution)/shard_map/ppermute | solution.py:178
  22.0 1.6 %copy.29 = bf16[27,128,128]{1,2,0:T(8,128)(2,1)} copy(bf16[27,128,128]{2,1,0:T(8,128)(2,1)S(1)} %bitcast.74) | data formatting | bytes 1769472 | tf_op jit(solution)/shard_map/reshape | solution.py:152
  23.7 0.6 copy-done.7
  24.3 10.8 %shard_map.85 = (bf16[2,1024,128]{2,1,0:T(8,128)(2,1)}, bf16[2,128,128]{2,1,0:T(8,128)(2,1)}, bf16[2,128,128]{2,1,0:T(8,128)(2,1)}, bf16[6912,128]{1,0:T(8,128)(2,1)}) custom-call(bf16[3,1024,128]{2,1,0:T(8,128)(2,1)} %get-tuple-element.13.refs_0_.grid_ref, bf16[2,128,128]{2,1,0:T(8,128)(2,1)} %copy-done.3, bf16[2,128,128]{2,1,0:T(8,128)(2,1)} %copy-done.5, ...), custom_call_target="tpu_custom_call" | custom-call | tf_op jit(solution)/shard_map/pallas_call | solution.py:140
  35.1 6.4 %all_to_all.30 = bf16[2,3456,128]{2,1,0:T(8,128)(2,1)S(1)} all-to-all(bf16[2,3456,128]{2,1,0:T(8,128)(2,1)} %bitcast.79), channel_id=1, replica_groups=mesh['y_lo'=2,'x'=4,'z_hi'=4,'z_lo'=4,'y_hi'=2,'core'=2] {'core'}, dimensions={0} | all-to-all | bytes 3538944 | tf_op jit(solution)/shard_map/all_to_all | solution.py:184
  41.5 0.9 reduce_sum.39
  42.4 27.1 %all_to_all.31 = bf16[16,216,128]{2,1,0:T(8,128)(2,1)S(1)} all-to-all(bf16[16,216,128]{2,1,0:T(8,128)(2,1)S(1)} %bitcast.77), channel_id=1, replica_groups=mesh['y_lo'=2,'x'=4,'z_hi'=4,'z_lo'=4,'y_hi'=2,'core'=2] {'y_hi','y_lo',..., dimensions={0} | all-to-all | bytes 1769472 | tf_op jit(solution)/shard_map/all_to_all | solution.py:184
  69.6 0.1 convert_reduce_fusion
  69.7 7.2 %all_to_all.32 = f32[4,56,128]{2,1,0:T(8,128)S(1)} all-to-all(f32[4,56,128]{2,1,0:T(8,128)S(1)} %bitcast.82), channel_id=1, replica_groups=mesh['y_lo'=2,'x'=4,'z_hi'=4,'z_lo'=4,'y_hi'=2,'core'=2] {'z_lo'}, dimensions={0} | all-to-all | bytes 229376 | tf_op jit(solution)/shard_map/all_to_all | solution.py:184
  77.0 21.9 %all_to_all.33 = f32[4,56,128]{2,1,0:T(8,128)S(1)} all-to-all(f32[4,56,128]{2,1,0:T(8,128)S(1)} %broadcast_in_dim.9), channel_id=1, replica_groups=mesh['y_lo'=2,'x'=4,'z_hi'=4,'z_lo'=4,'y_hi'=2,'core'=2] {'z_hi'}, dimensions={0} | all-to-all | bytes 229376 | tf_op jit(solution)/shard_map/all_to_all | solution.py:184
  98.9 7.1 %all_to_all.34 = bf16[4,56,128]{2,1,0:T(8,128)(2,1)S(1)} all-to-all(bf16[4,56,128]{2,1,0:T(8,128)(2,1)S(1)} %broadcast_in_dim.10), channel_id=1, replica_groups=mesh['y_lo'=2,'x'=4,'z_hi'=4,'z_lo'=4,'y_hi'=2,'core'=2] {'z_lo'}, dimensions={0} | all-to-all | bytes 114688 | tf_op jit(solution)/shard_map/all_to_all | solution.py:184
  106.1 1.0 broadcast_in_dim.11
  107.1 3.6 %all-to-all-start.5 = ((bf16[16,216,128]{2,1,0:T(8,128)(2,1)}), bf16[16,216,128]{2,1,0:T(8,128)(2,1)S(1)}, u32[]{:S(2)}, u32[]{:S(2)}) async-start(bf16[16,216,128]{2,1,0:T(8,128)(2,1)} %broadcast_in_dim.11), calls=%async_computation.5 | async-start | bytes 1769472 | tf_op jit(solution)/shard_map/all_to_all | solution.py:184
  110.7 2.5 %collective-permute-start.4 = (bf16[2,128,128]{2,1,0:T(8,128)(2,1)S(1)}, bf16[2,128,128]{2,1,0:T(8,128)(2,1)S(1)}, u32[]{:S(2)}, u32[]{:S(2)}) collective-permute-start(bf16[2,128,128]{2,1,0:T(8,128)(2,1)S(1)} %copy-done.11), channel_id=1, source_target_pairs={{0,4},{4,8},{8,12},{12,16},{16,20},{20,24},{24,28},{28,32},{32,36}... | collective-permute-start | bytes 196616 | tf_op jit(solution)/shard_map/ppermute | solution.py:168
  113.2 9.2 %all-to-all-done.5 = bf16[16,216,128]{2,1,0:T(8,128)(2,1)S(1)} async-done(((bf16[16,216,128]{2,1,0:T(8,128)(2,1)}), bf16[16,216,128]{2,1,0:T(8,128)(2,1)S(1)}, u32[]{:S(2)}, u32[]{:S(2)}) %all-to-all-start.5) | async-done | bytes 884768 | tf_op jit(solution)/shard_map/all_to_all | solution.py:184
  122.5 8.8 %collective-permute-start.8 = (bf16[3456,128]{1,0:T(8,128)(2,1)S(1)}, bf16[3456,128]{1,0:T(8,128)(2,1)S(1)}, u32[]{:S(2)}, u32[]{:S(2)}) collective-permute-start(bf16[3456,128]{1,0:T(8,128)(2,1)S(1)} %bitcast.78), channel_id=1, source_target_pairs={{0,1},{1,0},{2,3},{3,2},{4,5},{5,4},{6,7},{7,6},{8,9},{9,8},{10,11... | collective-permute-start | bytes 2654216 | tf_op jit(solution)/shard_map/ppermute | solution.py:206
  131.3 0.9 slice_bitcast_fusion
  132.2 1.3 collective-permute-start.5
  133.5 4.2 %collective-permute-done.5.xhi_ref = bf16[2,128,128]{2,1,0:T(8,128)(2,1)S(1)} collective-permute-done((bf16[2,128,128]{2,1,0:T(8,128)(2,1)S(1)}, bf16[2,128,128]{2,1,0:T(8,128)(2,1)S(1)}, u32[]{:S(2)}, u32[]{:S(2)}) %collective-permute-start.5) | collective-permute-done | bytes 65568 | tf_op jit(solution)/shard_map/ppermute | solution.py:169
  137.7 2.8 %collective-permute-start.7 = (bf16[2,160,128]{2,1,0:T(8,128)(2,1)S(1)}, bf16[2,160,128]{2,1,0:T(8,128)(2,1)S(1)}, u32[]{:S(2)}, u32[]{:S(2)}) collective-permute-start(bf16[2,160,128]{2,1,0:T(8,128)(2,1)S(1)} %bitcast.88), channel_id=1, source_target_pairs={{1,0},{2,1},{3,2},{5,4},{6,5},{7,6},{9,8},{10,9},{11,10},{13,12},{... | collective-permute-start | bytes 245768 | tf_op jit(solution)/shard_map/ppermute | solution.py:179
  140.5 4.5 %collective-permute-start.6 = (bf16[2,160,128]{2,1,0:T(8,128)(2,1)S(1)}, bf16[2,160,128]{2,1,0:T(8,128)(2,1)S(1)}, u32[]{:S(2)}, u32[]{:S(2)}) collective-permute-start(bf16[2,160,128]{2,1,0:T(8,128)(2,1)S(1)} %bitcast.89), channel_id=1, source_target_pairs={{0,1},{1,2},{2,3},{4,5},{5,6},{6,7},{8,9},{9,10},{10,11},{12,13},{... | collective-permute-start | bytes 245768 | tf_op jit(solution)/shard_map/ppermute | solution.py:178
  145.0 1.6 %copy.36 = bf16[27,128,128]{1,2,0:T(8,128)(2,1)} copy(bf16[27,128,128]{2,1,0:T(8,128)(2,1)S(1)} %bitcast.73) | data formatting | bytes 1769472 | tf_op jit(solution)/shard_map/reshape | solution.py:152
  146.7 0.6 copy-done.6
  147.3 0.0 copy-done.8
  147.3 8.8 %shard_map.86 = (bf16[512,128]{1,0:T(8,128)(2,1)}, f32[512,128]{1,0:T(8,128)}) custom-call(s32[8]{0:T(128)} %pos_ref.3, bf16[3,1024,128]{2,1,0:T(8,128)(2,1)} %get-tuple-element.13.refs_0_.grid_ref, bf16[2,1024,128]{2,1,0:T(8,128)(2,1)} %get-tuple-element.16.fields_ref, bf16[2,128,128]{2,1,0:T(8,128)(2,1)} %copy-done.2, bf16[2,128,128]{2,1,0:T(8,128)(2,1)} %copy-done.4, ...), custom_call_target="tpu_custom_call" | custom-call | tf_op jit(solution)/shard_map/pallas_call | solution.py:140
  156.1 2.1 %select_convert_fusion = (f32[3456,128]{1,0:T(8,128)}, f32[3456,128]{1,0:T(8,128)}) fusion(bf16[3456,128]{1,0:T(8,128)(2,1)S(1)} %collective-permute-done.8, pred[]{:T(512)S(6)} %eq.3, bf16[16,216,128]{2,1,0:T(8,128)(2,1)S(1)} %all-to-all-done.5), kind=kLoop, calls=%fused_computation.1 | loop fusion | flops 1769472 | bytes 5308417 | tf_op jit(solution)/shard_map/convert_element_type | solution.py:208
  (43 shorter events, 0.2 us)
Async XLA Ops:
  0.6 21.3 %copy-start.1 = (bf16[3456,128]{1,0:T(8,128)(2,1)S(1)}, bf16[3456,128]{1,0:T(8,128)(2,1)}, u32[]{:S(2)}) copy-start(bf16[3456,128]{1,0:T(8,128)(2,1)} %w2_ref.1) | copy-start | bytes 2654212
  3.6 6.8 %collective-permute-start = (bf16[2,128,128]{2,1,0:T(8,128)(2,1)}, bf16[2,128,128]{2,1,0:T(8,128)(2,1)S(1)}, u32[]{:S(2)}, u32[]{:S(2)}) collective-permute-start(bf16[2,128,128]{2,1,0:T(8,128)(2,1)} %get-tuple-element.14), channel_id=1, source_target_pairs={{0,4},{4,8},{8,12},{12,16},{16,20},{20,24},{24,28},{28,32},{32,36}... | collective-permute-start | bytes 196616 | tf_op jit(solution)/shard_map/ppermute | solution.py:168
  7.9 5.4 %collective-permute-start.1 = (bf16[2,128,128]{2,1,0:T(8,128)(2,1)}, bf16[2,128,128]{2,1,0:T(8,128)(2,1)S(1)}, u32[]{:S(2)}, u32[]{:S(2)}) collective-permute-start(bf16[2,128,128]{2,1,0:T(8,128)(2,1)} %get-tuple-element.15), channel_id=1, source_target_pairs={{4,0},{8,4},{12,8},{16,12},{20,16},{24,20},{28,24},{32,28},{36,32}... | collective-permute-start | bytes 196616 | tf_op jit(solution)/shard_map/ppermute | solution.py:169
  10.3 13.3 %copy-start.3 = (bf16[2,128,128]{2,1,0:T(8,128)(2,1)}, bf16[2,128,128]{2,1,0:T(8,128)(2,1)S(1)}, u32[]{:S(2)}) copy-start(bf16[2,128,128]{2,1,0:T(8,128)(2,1)S(1)} %collective-permute-done.refs_1_) | copy-start | bytes 196612
  13.3 10.3 %copy-start.5 = (bf16[2,128,128]{2,1,0:T(8,128)(2,1)}, bf16[2,128,128]{2,1,0:T(8,128)(2,1)S(1)}, u32[]{:S(2)}) copy-start(bf16[2,128,128]{2,1,0:T(8,128)(2,1)S(1)} %collective-permute-done.1.refs_2_) | copy-start | bytes 196612
  13.4 10.3 %collective-permute-start.3 = (bf16[2,160,128]{2,1,0:T(8,128)(2,1)S(1)}, bf16[2,160,128]{2,1,0:T(8,128)(2,1)S(1)}, u32[]{:S(2)}, u32[]{:S(2)}) collective-permute-start(bf16[2,160,128]{2,1,0:T(8,128)(2,1)S(1)} %bitcast.90), channel_id=1, source_target_pairs={{1,0},{2,1},{3,2},{5,4},{6,5},{7,6},{9,8},{10,9},{11,10},{13,12},{... | collective-permute-start | bytes 245768 | tf_op jit(solution)/shard_map/ppermute | solution.py:179
  20.0 3.6 %collective-permute-start.2 = (bf16[2,160,128]{2,1,0:T(8,128)(2,1)S(1)}, bf16[2,160,128]{2,1,0:T(8,128)(2,1)S(1)}, u32[]{:S(2)}, u32[]{:S(2)}) collective-permute-start(bf16[2,160,128]{2,1,0:T(8,128)(2,1)S(1)} %bitcast.91), channel_id=1, source_target_pairs={{0,1},{1,2},{2,3},{4,5},{5,6},{6,7},{8,9},{9,10},{10,11},{12,13},{... | collective-permute-start | bytes 245768 | tf_op jit(solution)/shard_map/ppermute | solution.py:178
  23.6 0.6 copy-start.7
  23.6 0.7 copy-start.9
  77.0 33.8 %copy-start.11 = (bf16[2,128,128]{2,1,0:T(8,128)(2,1)S(1)}, bf16[2,128,128]{2,1,0:T(8,128)(2,1)}, u32[]{:S(2)}) copy-start(bf16[2,128,128]{2,1,0:T(8,128)(2,1)} %get-tuple-element.17) | copy-start | bytes 196612
  77.0 55.2 %copy-start.10 = (bf16[2,128,128]{2,1,0:T(8,128)(2,1)S(1)}, bf16[2,128,128]{2,1,0:T(8,128)(2,1)}, u32[]{:S(2)}) copy-start(bf16[2,128,128]{2,1,0:T(8,128)(2,1)} %get-tuple-element.18) | copy-start | bytes 196612
  106.1 39.0 %copy-start = (bf16[3456,128]{1,0:T(8,128)(2,1)S(1)}, bf16[3456,128]{1,0:T(8,128)(2,1)}, u32[]{:S(2)}) copy-start(bf16[3456,128]{1,0:T(8,128)(2,1)} %refs_5_.1) | copy-start | bytes 2654212
  107.1 15.4 %all-to-all-start.5 = ((bf16[16,216,128]{2,1,0:T(8,128)(2,1)}), bf16[16,216,128]{2,1,0:T(8,128)(2,1)S(1)}, u32[]{:S(2)}, u32[]{:S(2)}) async-start(bf16[16,216,128]{2,1,0:T(8,128)(2,1)} %broadcast_in_dim.11), calls=%async_computation.5 | async-start | bytes 1769472 | tf_op jit(solution)/shard_map/all_to_all | solution.py:184
  110.7 22.7 %collective-permute-start.4 = (bf16[2,128,128]{2,1,0:T(8,128)(2,1)S(1)}, bf16[2,128,128]{2,1,0:T(8,128)(2,1)S(1)}, u32[]{:S(2)}, u32[]{:S(2)}) collective-permute-start(bf16[2,128,128]{2,1,0:T(8,128)(2,1)S(1)} %copy-done.11), channel_id=1, source_target_pairs={{0,4},{4,8},{8,12},{12,16},{16,20},{20,24},{24,28},{28,32},{32,36}... | collective-permute-start | bytes 196616 | tf_op jit(solution)/shard_map/ppermute | solution.py:168
  122.5 33.6 %collective-permute-start.8 = (bf16[3456,128]{1,0:T(8,128)(2,1)S(1)}, bf16[3456,128]{1,0:T(8,128)(2,1)S(1)}, u32[]{:S(2)}, u32[]{:S(2)}) collective-permute-start(bf16[3456,128]{1,0:T(8,128)(2,1)S(1)} %bitcast.78), channel_id=1, source_target_pairs={{0,1},{1,0},{2,3},{3,2},{4,5},{5,4},{6,7},{7,6},{8,9},{9,8},{10,11... | collective-permute-start | bytes 2654216 | tf_op jit(solution)/shard_map/ppermute | solution.py:206
  132.2 5.5 %collective-permute-start.5 = (bf16[2,128,128]{2,1,0:T(8,128)(2,1)S(1)}, bf16[2,128,128]{2,1,0:T(8,128)(2,1)S(1)}, u32[]{:S(2)}, u32[]{:S(2)}) collective-permute-start(bf16[2,128,128]{2,1,0:T(8,128)(2,1)S(1)} %copy-done.10), channel_id=1, source_target_pairs={{4,0},{8,4},{12,8},{16,12},{20,16},{24,20},{28,24},{32,28},{36,32}... | collective-permute-start | bytes 196616 | tf_op jit(solution)/shard_map/ppermute | solution.py:169
  133.5 13.2 %copy-start.2 = (bf16[2,128,128]{2,1,0:T(8,128)(2,1)}, bf16[2,128,128]{2,1,0:T(8,128)(2,1)S(1)}, u32[]{:S(2)}) copy-start(bf16[2,128,128]{2,1,0:T(8,128)(2,1)S(1)} %collective-permute-done.4.xlo_ref) | copy-start | bytes 196612
  137.7 9.0 %copy-start.4 = (bf16[2,128,128]{2,1,0:T(8,128)(2,1)}, bf16[2,128,128]{2,1,0:T(8,128)(2,1)S(1)}, u32[]{:S(2)}) copy-start(bf16[2,128,128]{2,1,0:T(8,128)(2,1)S(1)} %collective-permute-done.5.xhi_ref) | copy-start | bytes 196612
  137.7 8.9 %collective-permute-start.7 = (bf16[2,160,128]{2,1,0:T(8,128)(2,1)S(1)}, bf16[2,160,128]{2,1,0:T(8,128)(2,1)S(1)}, u32[]{:S(2)}, u32[]{:S(2)}) collective-permute-start(bf16[2,160,128]{2,1,0:T(8,128)(2,1)S(1)} %bitcast.88), channel_id=1, source_target_pairs={{1,0},{2,1},{3,2},{5,4},{6,5},{7,6},{9,8},{10,9},{11,10},{13,12},{... | collective-permute-start | bytes 245768 | tf_op jit(solution)/shard_map/ppermute | solution.py:179
  140.5 6.1 %collective-permute-start.6 = (bf16[2,160,128]{2,1,0:T(8,128)(2,1)S(1)}, bf16[2,160,128]{2,1,0:T(8,128)(2,1)S(1)}, u32[]{:S(2)}, u32[]{:S(2)}) collective-permute-start(bf16[2,160,128]{2,1,0:T(8,128)(2,1)S(1)} %bitcast.89), channel_id=1, source_target_pairs={{0,1},{1,2},{2,3},{4,5},{5,6},{6,7},{8,9},{9,10},{10,11},{12,13},{... | collective-permute-start | bytes 245768 | tf_op jit(solution)/shard_map/ppermute | solution.py:178
  146.7 0.6 copy-start.6
  146.7 0.7 copy-start.8

commit v3 on v2

v3 whole, which is shorter than its diff:
```python
import jax
import jax.numpy as jnp
from jax import lax
from jax.experimental import pallas as pl
from jax.experimental.pallas import tpu as pltpu
from jax.sharding import Mesh
from jax.sharding import PartitionSpec as P

LBY, LBZ = 2, 3
SLOTS = 8
C = 128
GX, GY, GZ = 8, 8, 16
EX, EY = GX + 2, GY + 2
PX, PY = GX + 4, GY + 4
ROWS = GX * GY * GZ
EXT_ROWS = EX * EY * GZ
PAD_ROWS = PX * PY * GZ
FACE = 2 * GY * GZ
DIMS = (2, 4, 4, 4, 2, 2)
NAMES = ("y_lo", "x", "z_hi", "z_lo", "y_hi", "core")
INTERPRET = False
BF = jnp.bfloat16
F32 = jnp.float32


def grid_row(pos_ref, index):
    slot = index >> 6
    pos = jnp.full(index.shape, -1, jnp.int32)
    for s in range(SLOTS):
        pos = jnp.where(slot == s, pos_ref[s], pos)
    safe = jnp.maximum(pos, 0)
    bx = (safe >= 6).astype(jnp.int32)
    rest = safe - 6 * bx
    by = (rest >= 3).astype(jnp.int32)
    bz = rest - 3 * by
    vx = (index >> 4) & 3
    vy = (index >> 2) & 3
    vz = index & 3
    row = ((bx * 4 + vx) * GY + by * 4 + vy) * GZ + bz * 4 + vz
    return jnp.where(pos >= 0, row, -1)


def dot(a, b, dims=((1,), (0,))):
    return lax.dot_general(a, b, (dims, ((), ())), preferred_element_type=F32)


def place_kernel(pos_ref, feat_ref, cot_ref, grid_ref, xlo_ref, xhi_ref, ylo_ref, yhi_ref):
    target = grid_row(pos_ref, lax.broadcasted_iota(jnp.int32, (1, SLOTS * 64), 1))
    rows = lax.broadcasted_iota(jnp.int32, (ROWS, SLOTS * 64), 0)
    perm = (rows == target).astype(F32).astype(BF)
    mask = dot(perm, jnp.ones((SLOTS * 64, C), BF))
    z = lax.broadcasted_iota(jnp.int32, (ROWS, C), 0) & (GZ - 1)
    flags = jnp.where(z == 13, pltpu.roll(mask, 13, 0) + 2.0 * pltpu.roll(mask, 5, 0), 0.0)
    flags = jnp.where(z == 14, pltpu.roll(mask, 10, 0), flags)
    for field, ref in enumerate((feat_ref, cot_ref)):
        placed = dot(perm, ref[...])
        placed = (placed + flags if field == 0 else placed).astype(BF)
        grid_ref[field] = placed
        xlo_ref[field] = placed[:FACE]
        xhi_ref[field] = placed[ROWS - FACE :]
        columns = placed.reshape(GX, GY * GZ, C)
        ylo_ref[field] = columns[:, : 2 * GZ]
        yhi_ref[field] = columns[:, (GY - 2) * GZ :]


def z_shifts(field, flip=False):
    rows = field.shape[0]
    wide = field.astype(F32)
    before = pltpu.roll(wide, 1, 0).astype(BF)
    after = pltpu.roll(wide, rows - 1, 0).astype(BF)
    return jnp.concatenate([after, field, before] if flip else [before, field, after], axis=1)


def fill_pad(pad_ref, grid, x_lo, x_hi, y_lo, y_hi):
    pad_ref[2 : PX - 2, 2 : PY - 2] = grid.reshape(GX, GY, GZ, C)
    pad_ref[:2, 2 : PY - 2] = x_lo.reshape(2, GY, GZ, C)
    pad_ref[PX - 2 :, 2 : PY - 2] = x_hi.reshape(2, GY, GZ, C)
    pad_ref[:, :2] = y_lo.reshape(PX, 2, GZ, C)
    pad_ref[:, PY - 2 :] = y_hi.reshape(PX, 2, GZ, C)


def conv(shift_ref, w_ref, flip):
    nx, ny = shift_ref.shape[0] - 2, shift_ref.shape[1] - 2
    acc = None
    for k in range(9):
        dx, dy = divmod(k, 3)
        lhs = shift_ref[dx : dx + nx, dy : dy + ny].reshape(nx * ny * GZ, 3 * C)
        at = 8 - k if flip else k
        term = dot(lhs, w_ref[at * 3 * C : (at + 1) * 3 * C, :])
        acc = term if acc is None else acc + term
    return acc


def active_rows(field):
    both, middle = field[:, :, 13:14], field[:, :, 14:15]
    high = (both > 1.5).astype(F32)
    low = both - 2.0 * high
    z = lax.broadcasted_iota(jnp.int32, field.shape, 2)
    upper = jnp.where(z < 8, jnp.broadcast_to(middle, field.shape), jnp.broadcast_to(high, field.shape))
    mask = jnp.where(z < 4, jnp.broadcast_to(low, field.shape), upper)
    return jnp.where(z < 12, mask, 0.0)


def middle_kernel(
    scale, grid_ref, xlo_ref, xhi_ref, ylo_ref, yhi_ref, w1_ref, w2t_ref,
    fields_ref, terms_ref, padx_ref, padu_ref, shift_ref, pre_ref,
):
    fill_pad(padx_ref, grid_ref[0], xlo_ref[0], xhi_ref[0], ylo_ref[0], yhi_ref[0])
    fill_pad(padu_ref, grid_ref[1], xlo_ref[1], xhi_ref[1], ylo_ref[1], yhi_ref[1])
    shift_ref[...] = z_shifts(padx_ref[...].reshape(PAD_ROWS, C)).reshape(PX, PY, GZ, 3 * C)
    pre_ref[...] = conv(shift_ref, w1_ref, False)
    shift_ref[...] = z_shifts(padu_ref[...].reshape(PAD_ROWS, C), True).reshape(PX, PY, GZ, 3 * C)
    back = conv(shift_ref, w2t_ref, True)
    pre = pre_ref[...]
    mask = active_rows(padx_ref[1 : PX - 1, 1 : PY - 1].astype(F32)).reshape(EXT_ROWS, C)
    sig = jax.nn.sigmoid(pre)
    fields_ref[0] = (pre * sig * mask).astype(BF).reshape(EX, EY, GZ, C)
    fields_ref[1] = (back * (sig * (1.0 + pre * (1.0 - sig))) * mask).astype(BF).reshape(EX, EY, GZ, C)

    def own(field):
        return fields_ref[field, 1 : EX - 1, 1 : EY - 1].reshape(ROWS, C)

    hz = z_shifts(own(0)).T
    for k in range(9):
        dx, dy = divmod(k, 3)
        rhs = padu_ref[3 - dx : 3 - dx + GX, 3 - dy : 3 - dy + GY].reshape(ROWS, C)
        terms_ref[(27 + 3 * k) * C : (30 + 3 * k) * C, :] = (dot(hz, rhs) * scale).astype(BF)
    gz = z_shifts(own(1)).T
    for k in range(9):
        dx, dy = divmod(k, 3)
        rhs = padx_ref[dx + 1 : dx + 1 + GX, dy + 1 : dy + 1 + GY].reshape(ROWS, C)
        prod = dot(gz, rhs) * scale
        for oz in range(3):
            block = prod[(2 - oz) * C : (3 - oz) * C, :].T
            terms_ref[(3 * k + oz) * C : (3 * k + oz + 1) * C, :] = block.astype(BF)


def final_kernel(pos_ref, grid_ref, fields_ref, w2_ref, w1t_ref, out_ref, grad_ref, shift_ref):
    target = grid_row(pos_ref, lax.broadcasted_iota(jnp.int32, (SLOTS * 64, 1), 0))
    rows = lax.broadcasted_iota(jnp.int32, (SLOTS * 64, ROWS), 1)
    perm = (rows == target).astype(F32).astype(BF)
    for field, w_ref in enumerate((w2_ref, w1t_ref)):
        shift_ref[...] = z_shifts(fields_ref[field].reshape(EXT_ROWS, C), field == 1).reshape(EX, EY, GZ, 3 * C)
        value = conv(shift_ref, w_ref, field == 1) + grid_ref[field].astype(F32)
        high = value.astype(BF)
        if field == 0:
            out_ref[...] = dot(perm, high).astype(BF)
        else:
            low = (value - high.astype(F32)).astype(BF)
            grad_ref[...] = dot(perm, high) + dot(perm, low)


def call(kernel, outs, scratch=(), smem=0, args=(), cost=None):
    specs = [pl.BlockSpec(memory_space=pltpu.SMEM)] * smem
    specs += [pl.BlockSpec(memory_space=pltpu.VMEM)] * (len(args) - smem)
    return pl.pallas_call(
        kernel,
        out_shape=outs,
        in_specs=specs,
        out_specs=jax.tree.map(lambda _: pl.BlockSpec(memory_space=pltpu.VMEM), outs),
        scratch_shapes=list(scratch),
        compiler_params=pltpu.CompilerParams(vmem_limit_bytes=56 << 20),
        interpret=INTERPRET,
        cost_estimate=cost,
    )(*args)


def transposed(weight):
    return weight.reshape(27, C, C).transpose(0, 2, 1).reshape(27 * C, C)


def ring(axes):
    count = lax.axis_size(axes)
    forward = [(i, i + 1) for i in range(count - 1)]
    return forward, [(b, a) for a, b in forward]


GXN = ("y_lo", "x", "z_hi", "z_lo")
GYN = ("y_hi", "core")
YX = ("y_hi", "y_lo", "x")


def exchange(x_faces, y_faces):
    forward, backward = ring(GXN)
    x_lo = lax.ppermute(x_faces[1], GXN, forward)
    x_hi = lax.ppermute(x_faces[0], GXN, backward)

    def face(y):
        at = (GY - 2) * GZ if y else 0
        ends = [end.reshape(2, 2, GY * GZ, C)[:, :, at : at + 2 * GZ] for end in (x_lo, x_hi)]
        return jnp.concatenate([ends[0], y_faces[y], ends[1]], axis=1)

    forward, backward = ring(GYN)
    y_lo = lax.ppermute(face(1), GYN, forward)
    y_hi = lax.ppermute(face(0), GYN, backward)
    return x_lo, x_hi, y_lo, y_hi


def swap(values, axes):
    return lax.all_to_all(values, axes, 0, 0, tiled=True)


def scatter_sum(values, axes):
    count = lax.axis_size(axes)
    return swap(values.reshape(count, -1, C), axes).astype(F32).sum(axis=0)


def gather(values, axes):
    return swap(jnp.broadcast_to(values, (lax.axis_size(axes), *values.shape)), axes)


def reduce_terms(terms):
    share = scatter_sum(terms, "core").astype(BF)
    share = scatter_sum(share, YX)
    rows = share.shape[0]
    padded = -(-rows // (8 * lax.axis_size("z_lo"))) * 8 * lax.axis_size("z_lo")
    share = jnp.pad(share, ((0, padded - rows), (0, 0)))
    share = scatter_sum(share, "z_lo")
    share = gather(share, "z_hi").sum(axis=0).astype(BF)
    share = gather(share, "z_lo").reshape(padded, C)[:rows]
    share = gather(share, YX).reshape(-1, C)
    other = lax.ppermute(share, "core", [(0, 1), (1, 0)])
    first = lax.axis_index("core") == 0
    return jnp.where(first, share, other).astype(F32), jnp.where(first, other, share).astype(F32)


def per_device(features, cotangent, block_pos, weight_one, weight_two):
    total_rows = block_pos.shape[0] * 64 * lax.axis_size(NAMES)
    scale = float(total_rows) ** -0.5
    face_x = jax.ShapeDtypeStruct((2, FACE, C), BF)
    face_y = jax.ShapeDtypeStruct((2, GX, 2 * GZ, C), BF)
    grid, *faces = call(
        place_kernel,
        (jax.ShapeDtypeStruct((2, ROWS, C), BF), face_x, face_x, face_y, face_y),
        smem=1,
        args=(block_pos, features, cotangent),
    )
    halo = exchange(faces[:2], faces[2:])
    pad = pltpu.VMEM((PX, PY, GZ, C), BF)
    fields, terms = call(
        lambda *refs: middle_kernel(scale, *refs),
        (jax.ShapeDtypeStruct((2, EX, EY, GZ, C), BF), jax.ShapeDtypeStruct((54 * C, C), BF)),
        scratch=(pad, pad, pltpu.VMEM((PX, PY, GZ, 3 * C), BF), pltpu.VMEM((EXT_ROWS, C), F32)),
        args=(grid, *halo, weight_one, transposed(weight_two)),
    )
    output, input_grad = call(
        final_kernel,
        (jax.ShapeDtypeStruct(features.shape, BF), jax.ShapeDtypeStruct(features.shape, F32)),
        scratch=(pltpu.VMEM((EX, EY, GZ, 3 * C), BF),),
        smem=1,
        args=(block_pos, grid, fields, weight_two, transposed(weight_one)),
        cost=pl.CostEstimate(flops=2 * 2 * 27 * ROWS * C * C, transcendentals=0, bytes_accessed=24 << 20),
    )
    grad_one, grad_two = reduce_terms(terms)
    return output, input_grad, grad_one, grad_two


def solution(mesh):
    split = Mesh(mesh.devices.reshape(DIMS), NAMES)
    rows = P(NAMES, None)
    return jax.shard_map(
        per_device,
        mesh=split,
        in_specs=(rows, rows, P(NAMES), P(), P()),
        out_specs=(rows, rows, P(), P()),
        check_vma=False,
    )
```

time: 159 us -> 149 us (0.937)
  starting transfers between devices: 37.6 us -> 23.5 us
  blocking collectives: 69.8 us -> 80.7 us
  waiting for transfers between devices: 16.4 us -> 9.71 us
  local copies, waits for them, and re-layouts: 7.62 us -> 4.13 us
  Pallas kernels: 22.5 us -> 24.8 us
  other arithmetic: 3.19 us -> 5.05 us
    all_to_all x5 -> x6, blocking collectives: 69.8 us -> 80.7 us  [swap(): return lax.all_to_all(values, axes, 0, 0, tiled=True)]
    all_to_all x1 -> x0, waiting for transfers between devices: 9.24 us -> none  [swap(): return lax.all_to_all(values, axes, 0, 0, tiled=True)]
    ppermute x2 -> x1, starting transfers between devices: 9.42 us -> 1.92 us  [exchange(): y_hi = lax.ppermute(face(0), GYN, backward)]
    ppermute x2 -> x1, waiting for transfers between devices: 0.01 us -> 4.91 us  [exchange(): y_hi = lax.ppermute(face(0), GYN, backward)]
    all_to_all x1 -> x0, starting transfers between devices: 3.63 us -> none  [swap(): return lax.all_to_all(values, axes, 0, 0, tiled=True)]
    ppermute x6 -> x3, starting transfers between devices: 15.8 us -> 12.5 us  [the longest x1 6.81 us: exchange(): y_lo = lax.ppermute(face(1), GYN, forward)]
    ppermute x6 -> x3, waiting for transfers between devices: 7.18 us -> 4.79 us  [the longest x1 3.85 us: exchange(): x_hi = lax.ppermute(x_faces[0], GXN, backward)]
    pallas_call x3, Pallas kernels: 22.5 us -> 24.8 us  [call(): pl.pallas_call(kernel, out_shape=outs, in_specs=specs, out_specs=jax.tree...]
  transfers between devices with their start and end apart: 10 -> 5, of which waited for: 3 -> 3; matrix products, arithmetic and copies ran while one was open for 3% -> 3% of each run, Pallas kernels for 6% -> 6%
where the time goes in v3:
time: 149 us
  blocking collectives  80.7 us (54%)
  Pallas kernels  24.8 us (17%)
  starting transfers between devices  23.5 us (16%)
  waiting for transfers between devices  9.71 us (7%)
  other arithmetic  5.05 us (3%)
  local copies, waits for them, and re-layouts  4.13 us (3%)
    all_to_all x6, blocking collectives, swap(): return lax.all_to_all(values, axes, 0, 0, tiled=True)  80.7 us
    pallas_call x3, Pallas kernels, call(): pl.pallas_call(kernel, out_shape=outs, in_specs=specs, out_specs=jax.tree...  24.8 us
    ppermute x1, starting transfers between devices, reduce_terms(): other = lax.ppermute(share, 'core', [(0, 1), (1, 0)])  9.1 us
    ppermute x1, starting transfers between devices, exchange(): y_lo = lax.ppermute(face(1), GYN, forward)  6.81 us
    ppermute x1, waiting for transfers between devices, exchange(): y_hi = lax.ppermute(face(0), GYN, backward)  4.91 us
    ppermute x1, starting transfers between devices, exchange(): x_lo = lax.ppermute(x_faces[1], GXN, forward)  4.36 us
    ppermute x1, waiting for transfers between devices, exchange(): x_hi = lax.ppermute(x_faces[0], GXN, backward)  3.85 us
    reshape x2, local copies, waits for them, and re-layouts, transposed(): return weight.reshape(27, C, C).transpose(0, 2, 1).reshape(27 * C, C)  3.28 us
  transfers between devices with their start and end apart: 5, of which 3 were waited for; matrix products, arithmetic and copies ran while one was open for 3% of the time, Pallas kernels for 6%

profile of v3, /device:TPU:1, one launch (start us, length us, event | category | flops | bytes accessed | tf_op | source)
XLA Modules:
  0.0 148.6 jit_solution(17350802214684895618)
XLA Ops:
  0.6 0.0 copy-start.1
  0.6 3.0 %shard_map.84 = (bf16[2,1024,128]{2,1,0:T(8,128)(2,1)}, bf16[2,256,128]{2,1,0:T(8,128)(2,1)}, bf16[2,256,128]{2,1,0:T(8,128)(2,1)}, bf16[2,8,32,128]{3,2,1,0:T(8,128)(2,1)}, bf16[2,8,32,128]{3,2,1,0:T(8,128)(2,1)}) custom-call(s32[8]{0:T(128)} %pos_ref.3, bf16[512,128]{1,0:T(8,128)(2,1)} %feat_ref.1, bf16[512,128]{1,0:T(8,128)(2,1)} %cot_ref.1), custom_call_target="tpu_custom_call" | custom-call | tf_op jit(solution)/shard_map/pallas_call | solution.py:156
  3.6 4.4 %collective-permute-start = (bf16[2,256,128]{2,1,0:T(8,128)(2,1)}, bf16[2,256,128]{2,1,0:T(8,128)(2,1)S(1)}, u32[]{:S(2)}, u32[]{:S(2)}) collective-permute-start(bf16[2,256,128]{2,1,0:T(8,128)(2,1)} %get-tuple-element.14), channel_id=1, source_target_pairs={{0,4},{4,8},{8,12},{12,16},{16,20},{20,24},{24,28},{28,32},{32,36}... | collective-permute-start | bytes 393224 | tf_op jit(solution)/shard_map/ppermute | solution.py:185
  8.0 1.3 collective-permute-start.1
  9.3 0.9 collective-permute-done.refs_1_
  10.2 3.9 %collective-permute-done.1.refs_2_ = bf16[2,256,128]{2,1,0:T(8,128)(2,1)S(1)} collective-permute-done((bf16[2,256,128]{2,1,0:T(8,128)(2,1)}, bf16[2,256,128]{2,1,0:T(8,128)(2,1)S(1)}, u32[]{:S(2)}, u32[]{:S(2)}) %collective-permute-start.1) | collective-permute-done | bytes 131104 | tf_op jit(solution)/shard_map/ppermute | solution.py:186
  14.1 1.0 pad_maximum_fusion
  15.1 6.8 %collective-permute-start.2 = (bf16[2,12,32,128]{3,2,1,0:T(8,128)(2,1)S(1)}, bf16[2,12,32,128]{3,2,1,0:T(8,128)(2,1)S(1)}, u32[]{:S(2)}, u32[]{:S(2)}) collective-permute-start(bf16[2,12,32,128]{3,2,1,0:T(8,128)(2,1)S(1)} %pad_maximum_fusion), channel_id=1, source_target_pairs={{0,1},{1,2},{2,3},{4,5},{5,6},{6,7},{8,9},{9,10},{10,11},{12,13},{... | collective-permute-start | bytes 589832 | tf_op jit(solution)/shard_map/ppermute | solution.py:194
  21.9 0.9 pad_maximum_fusion.1
  22.8 1.9 %collective-permute-start.3 = (bf16[2,12,32,128]{3,2,1,0:T(8,128)(2,1)S(1)}, bf16[2,12,32,128]{3,2,1,0:T(8,128)(2,1)S(1)}, u32[]{:S(2)}, u32[]{:S(2)}) collective-permute-start(bf16[2,12,32,128]{3,2,1,0:T(8,128)(2,1)S(1)} %pad_maximum_fusion.1), channel_id=1, source_target_pairs={{1,0},{2,1},{3,2},{5,4},{6,5},{7,6},{9,8},{10,9},{11,10},{13,12},{... | collective-permute-start | bytes 589832 | tf_op jit(solution)/shard_map/ppermute | solution.py:195
  24.8 0.0 copy-done.1
  24.8 1.6 %copy.11 = bf16[27,128,128]{1,2,0:T(8,128)(2,1)} copy(bf16[27,128,128]{2,1,0:T(8,128)(2,1)S(1)} %bitcast.22) | data formatting | bytes 1769472 | tf_op jit(solution)/shard_map/reshape | solution.py:169
  26.4 0.0 collective-permute-done.2.refs_3_
  26.4 4.9 %collective-permute-done.3.refs_4_ = bf16[2,12,32,128]{3,2,1,0:T(8,128)(2,1)S(1)} collective-permute-done((bf16[2,12,32,128]{3,2,1,0:T(8,128)(2,1)S(1)}, bf16[2,12,32,128]{3,2,1,0:T(8,128)(2,1)S(1)}, u32[]{:S(2)}, u32[]{:S(2)}) %collective-permute-start.3) | collective-permute-done | bytes 196640 | tf_op jit(solution)/shard_map/ppermute | solution.py:195
  31.3 0.7 copy-done.5
  32.0 13.2 %shard_map.85 = (bf16[2,10,10,16,128]{4,3,2,1,0:T(8,128)(2,1)}, bf16[6912,128]{1,0:T(8,128)(2,1)}) custom-call(bf16[2,1024,128]{2,1,0:T(8,128)(2,1)} %get-tuple-element.13.refs_0_.grid_ref, bf16[2,256,128]{2,1,0:T(8,128)(2,1)} %copy-done.2, bf16[2,256,128]{2,1,0:T(8,128)(2,1)} %copy-done.3, bf16[2,12,32,128]{3,2,1,0:T(8,128)(2,1)} %copy-done.4, ...), custom_call_target="tpu_custom_call" | custom-call | tf_op jit(solution)/shard_map/pallas_call | solution.py:156
  45.2 6.1 %all_to_all.30 = bf16[2,3456,128]{2,1,0:T(8,128)(2,1)S(1)} all-to-all(bf16[2,3456,128]{2,1,0:T(8,128)(2,1)} %bitcast.21), channel_id=1, replica_groups=mesh['y_lo'=2,'x'=4,'z_hi'=4,'z_lo'=4,'y_hi'=2,'core'=2] {'core'}, dimensions={0} | all-to-all | bytes 3538944 | tf_op jit(solution)/shard_map/all_to_all | solution.py:200
  51.3 0.9 reduce_sum.39
  52.3 24.2 %all_to_all.31 = bf16[16,216,128]{2,1,0:T(8,128)(2,1)S(1)} all-to-all(bf16[16,216,128]{2,1,0:T(8,128)(2,1)S(1)} %bitcast.19), channel_id=1, replica_groups=mesh['y_lo'=2,'x'=4,'z_hi'=4,'z_lo'=4,'y_hi'=2,'core'=2] {'y_hi','y_lo',..., dimensions={0} | all-to-all | bytes 1769472 | tf_op jit(solution)/shard_map/all_to_all | solution.py:200
  76.5 0.1 convert_reduce_fusion
  76.6 7.1 %all_to_all.32 = f32[4,56,128]{2,1,0:T(8,128)S(1)} all-to-all(f32[4,56,128]{2,1,0:T(8,128)S(1)} %bitcast.24), channel_id=1, replica_groups=mesh['y_lo'=2,'x'=4,'z_hi'=4,'z_lo'=4,'y_hi'=2,'core'=2] {'z_lo'}, dimensions={0} | all-to-all | bytes 229376 | tf_op jit(solution)/shard_map/all_to_all | solution.py:200
  83.7 0.0 copy-start
  83.8 21.9 %all_to_all.33 = f32[4,56,128]{2,1,0:T(8,128)S(1)} all-to-all(f32[4,56,128]{2,1,0:T(8,128)S(1)} %broadcast_in_dim.9), channel_id=1, replica_groups=mesh['y_lo'=2,'x'=4,'z_hi'=4,'z_lo'=4,'y_hi'=2,'core'=2] {'z_hi'}, dimensions={0} | all-to-all | bytes 229376 | tf_op jit(solution)/shard_map/all_to_all | solution.py:200
  105.7 7.1 %all_to_all.34 = bf16[4,56,128]{2,1,0:T(8,128)(2,1)S(1)} all-to-all(bf16[4,56,128]{2,1,0:T(8,128)(2,1)S(1)} %broadcast_in_dim.10), channel_id=1, replica_groups=mesh['y_lo'=2,'x'=4,'z_hi'=4,'z_lo'=4,'y_hi'=2,'core'=2] {'z_lo'}, dimensions={0} | all-to-all | bytes 114688 | tf_op jit(solution)/shard_map/all_to_all | solution.py:200
  112.8 0.1 broadcast_in_dim.11
  112.9 14.2 %all_to_all.35 = bf16[16,216,128]{2,1,0:T(8,128)(2,1)S(1)} all-to-all(bf16[16,216,128]{2,1,0:T(8,128)(2,1)S(1)} %broadcast_in_dim.11), channel_id=1, replica_groups=mesh['y_lo'=2,'x'=4,'z_hi'=4,'z_lo'=4,'y_hi'=2,'core'=2] {'y_hi','y_lo',..., dimensions={0} | all-to-all | bytes 1769472 | tf_op jit(solution)/shard_map/all_to_all | solution.py:200
  127.1 9.1 %collective-permute-start.4 = (bf16[3456,128]{1,0:T(8,128)(2,1)S(1)}, bf16[3456,128]{1,0:T(8,128)(2,1)S(1)}, u32[]{:S(2)}, u32[]{:S(2)}) collective-permute-start(bf16[3456,128]{1,0:T(8,128)(2,1)S(1)} %bitcast.20), channel_id=1, source_target_pairs={{0,1},{1,0},{2,3},{3,2},{4,5},{5,4},{6,7},{7,6},{8,9},{9,8},{10,11... | collective-permute-start | bytes 2654216 | tf_op jit(solution)/shard_map/ppermute | solution.py:222
  136.2 0.0 copy-done
  136.2 1.6 %copy.12 = bf16[27,128,128]{1,2,0:T(8,128)(2,1)} copy(bf16[27,128,128]{2,1,0:T(8,128)(2,1)S(1)} %bitcast.17) | data formatting | bytes 1769472 | tf_op jit(solution)/shard_map/reshape | solution.py:169
  137.9 8.6 %shard_map.86 = (bf16[512,128]{1,0:T(8,128)(2,1)}, f32[512,128]{1,0:T(8,128)}) custom-call(s32[8]{0:T(128)} %pos_ref.3, bf16[2,1024,128]{2,1,0:T(8,128)(2,1)} %get-tuple-element.13.refs_0_.grid_ref, bf16[2,10,10,16,128]{4,3,2,1,0:T(8,128)(2,1)} %get-tuple-element.18.fields_ref, bf16[3456,128]{1,0:T(8,128)(2,1)} %w2_ref.1, bf16[3456,128]{1,0:T(8,128)(2,1)} %bitcast.23), custom_call_target="tpu_custom_call" | custom-call | flops 1811939328 | bytes 25165824 | tf_op jit(solution)/shard_map/pallas_call | solution.py:156
  146.5 0.0 collective-permute-done.4
  146.5 2.1 %select_convert_fusion = (f32[3456,128]{1,0:T(8,128)}, f32[3456,128]{1,0:T(8,128)}) fusion(bf16[3456,128]{1,0:T(8,128)(2,1)S(1)} %collective-permute-done.4, pred[]{:T(512)S(6)} %eq.3, bf16[16,216,128]{2,1,0:T(8,128)(2,1)S(1)} %all_to_all.35), kind=kLoop, calls=%fused_computation.1 | loop fusion | flops 1769472 | bytes 5308417 | tf_op jit(solution)/shard_map/convert_element_type | solution.py:224
  (15 shorter events, 0.1 us)
Async XLA Ops:
  0.6 24.1 %copy-start.1 = (bf16[3456,128]{1,0:T(8,128)(2,1)S(1)}, bf16[3456,128]{1,0:T(8,128)(2,1)}, u32[]{:S(2)}) copy-start(bf16[3456,128]{1,0:T(8,128)(2,1)} %w2_ref.1) | copy-start | bytes 2654212
  3.6 6.6 %collective-permute-start = (bf16[2,256,128]{2,1,0:T(8,128)(2,1)}, bf16[2,256,128]{2,1,0:T(8,128)(2,1)S(1)}, u32[]{:S(2)}, u32[]{:S(2)}) collective-permute-start(bf16[2,256,128]{2,1,0:T(8,128)(2,1)} %get-tuple-element.14), channel_id=1, source_target_pairs={{0,4},{4,8},{8,12},{12,16},{16,20},{20,24},{24,28},{28,32},{32,36}... | collective-permute-start | bytes 393224 | tf_op jit(solution)/shard_map/ppermute | solution.py:185
  8.0 6.1 %collective-permute-start.1 = (bf16[2,256,128]{2,1,0:T(8,128)(2,1)}, bf16[2,256,128]{2,1,0:T(8,128)(2,1)S(1)}, u32[]{:S(2)}, u32[]{:S(2)}) collective-permute-start(bf16[2,256,128]{2,1,0:T(8,128)(2,1)} %get-tuple-element.15), channel_id=1, source_target_pairs={{4,0},{8,4},{12,8},{16,12},{20,16},{24,20},{28,24},{32,28},{36,32}... | collective-permute-start | bytes 393224 | tf_op jit(solution)/shard_map/ppermute | solution.py:186
  10.2 21.1 %copy-start.2 = (bf16[2,256,128]{2,1,0:T(8,128)(2,1)}, bf16[2,256,128]{2,1,0:T(8,128)(2,1)S(1)}, u32[]{:S(2)}) copy-start(bf16[2,256,128]{2,1,0:T(8,128)(2,1)S(1)} %collective-permute-done.refs_1_) | copy-start | bytes 393220
  14.1 17.2 %copy-start.3 = (bf16[2,256,128]{2,1,0:T(8,128)(2,1)}, bf16[2,256,128]{2,1,0:T(8,128)(2,1)S(1)}, u32[]{:S(2)}) copy-start(bf16[2,256,128]{2,1,0:T(8,128)(2,1)S(1)} %collective-permute-done.1.refs_2_) | copy-start | bytes 393220
  15.1 11.3 %collective-permute-start.2 = (bf16[2,12,32,128]{3,2,1,0:T(8,128)(2,1)S(1)}, bf16[2,12,32,128]{3,2,1,0:T(8,128)(2,1)S(1)}, u32[]{:S(2)}, u32[]{:S(2)}) collective-permute-start(bf16[2,12,32,128]{3,2,1,0:T(8,128)(2,1)S(1)} %pad_maximum_fusion), channel_id=1, source_target_pairs={{0,1},{1,2},{2,3},{4,5},{5,6},{6,7},{8,9},{9,10},{10,11},{12,13},{... | collective-permute-start | bytes 589832 | tf_op jit(solution)/shard_map/ppermute | solution.py:194
  22.8 8.5 %collective-permute-start.3 = (bf16[2,12,32,128]{3,2,1,0:T(8,128)(2,1)S(1)}, bf16[2,12,32,128]{3,2,1,0:T(8,128)(2,1)S(1)}, u32[]{:S(2)}, u32[]{:S(2)}) collective-permute-start(bf16[2,12,32,128]{3,2,1,0:T(8,128)(2,1)S(1)} %pad_maximum_fusion.1), channel_id=1, source_target_pairs={{1,0},{2,1},{3,2},{5,4},{6,5},{7,6},{9,8},{10,9},{11,10},{13,12},{... | collective-permute-start | bytes 589832 | tf_op jit(solution)/shard_map/ppermute | solution.py:195
  26.4 4.9 %copy-start.4 = (bf16[2,12,32,128]{3,2,1,0:T(8,128)(2,1)}, bf16[2,12,32,128]{3,2,1,0:T(8,128)(2,1)S(1)}, u32[]{:S(2)}) copy-start(bf16[2,12,32,128]{3,2,1,0:T(8,128)(2,1)S(1)} %collective-permute-done.2.refs_3_) | copy-start | bytes 589828
  31.3 0.7 copy-start.5
  83.7 52.5 %copy-start = (bf16[3456,128]{1,0:T(8,128)(2,1)S(1)}, bf16[3456,128]{1,0:T(8,128)(2,1)}, u32[]{:S(2)}) copy-start(bf16[3456,128]{1,0:T(8,128)(2,1)} %refs_5_.1) | copy-start | bytes 2654212
  127.1 19.4 %collective-permute-start.4 = (bf16[3456,128]{1,0:T(8,128)(2,1)S(1)}, bf16[3456,128]{1,0:T(8,128)(2,1)S(1)}, u32[]{:S(2)}, u32[]{:S(2)}) collective-permute-start(bf16[3456,128]{1,0:T(8,128)(2,1)S(1)} %bitcast.20), channel_id=1, source_target_pairs={{0,1},{1,0},{2,3},{3,2},{4,5},{5,4},{6,7},{7,6},{8,9},{9,8},{10,11... | collective-permute-start | bytes 2654216 | tf_op jit(solution)/shard_map/ppermute | solution.py:222

commit v4 on v3

--- a/solution.py
+++ b/solution.py
@@ -6,7 +6,7 @@
 from jax.sharding import Mesh
 from jax.sharding import PartitionSpec as P
 
-LBY, LBZ = 2, 3
+
 SLOTS = 8
 C = 128
 GX, GY, GZ = 8, 8, 16
@@ -81,14 +81,22 @@
 
 def conv(shift_ref, w_ref, flip):
     nx, ny = shift_ref.shape[0] - 2, shift_ref.shape[1] - 2
-    acc = None
-    for k in range(9):
-        dx, dy = divmod(k, 3)
-        lhs = shift_ref[dx : dx + nx, dy : dy + ny].reshape(nx * ny * GZ, 3 * C)
+
+    def weight(dx, dy):
+        k = 3 * dx + dy
         at = 8 - k if flip else k
-        term = dot(lhs, w_ref[at * 3 * C : (at + 1) * 3 * C, :])
-        acc = term if acc is None else acc + term
-    return acc
+        return w_ref[at * 3 * C : (at + 1) * 3 * C, :]
+
+    def product(x, y, mx, my, rhs):
+        lhs = shift_ref[x : x + mx, y : y + my].reshape(mx * my * GZ, 3 * C)
+        return dot(lhs, rhs).reshape(mx, my, GZ, rhs.shape[1])
+
+    acc = product(2, 2, nx, ny, weight(2, 2))
+    for dx in range(3):
+        pair = product(dx, 0, nx, ny + 1, jnp.concatenate([weight(dx, 0), weight(dx, 1)], axis=1))
+        acc = acc + pair[:, :ny, :, :C] + pair[:, 1:, :, C:]
+    pair = product(0, 2, nx + 1, ny, jnp.concatenate([weight(0, 2), weight(1, 2)], axis=1))
+    return acc + pair[:nx, :, :, :C] + pair[1:, :, :, C:]
 
 
 def active_rows(field):
@@ -108,9 +116,9 @@
     fill_pad(padx_ref, grid_ref[0], xlo_ref[0], xhi_ref[0], ylo_ref[0], yhi_ref[0])
     fill_pad(padu_ref, grid_ref[1], xlo_ref[1], xhi_ref[1], ylo_ref[1], yhi_ref[1])
     shift_ref[...] = z_shifts(padx_ref[...].reshape(PAD_ROWS, C)).reshape(PX, PY, GZ, 3 * C)
-    pre_ref[...] = conv(shift_ref, w1_ref, False)
+    pre_ref[...] = conv(shift_ref, w1_ref, False).reshape(EXT_ROWS, C)
     shift_ref[...] = z_shifts(padu_ref[...].reshape(PAD_ROWS, C), True).reshape(PX, PY, GZ, 3 * C)
-    back = conv(shift_ref, w2t_ref, True)
+    back = conv(shift_ref, w2t_ref, True).reshape(EXT_ROWS, C)
     pre = pre_ref[...]
     mask = active_rows(padx_ref[1 : PX - 1, 1 : PY - 1].astype(F32)).reshape(EXT_ROWS, C)
     sig = jax.nn.sigmoid(pre)
@@ -120,16 +128,18 @@
     def own(field):
         return fields_ref[field, 1 : EX - 1, 1 : EY - 1].reshape(ROWS, C)
 
+    def products(lhs, rhs_of):
+        for first in range(0, 9, 2):
+            ks = range(first, min(first + 2, 9))
+            prod = dot(lhs, jnp.concatenate([rhs_of(*divmod(k, 3)).reshape(ROWS, C) for k in ks], axis=1)) * scale
+            for n, k in enumerate(ks):
+                yield k, prod[:, n * C : (n + 1) * C]
+
     hz = z_shifts(own(0)).T
-    for k in range(9):
-        dx, dy = divmod(k, 3)
-        rhs = padu_ref[3 - dx : 3 - dx + GX, 3 - dy : 3 - dy + GY].reshape(ROWS, C)
-        terms_ref[(27 + 3 * k) * C : (30 + 3 * k) * C, :] = (dot(hz, rhs) * scale).astype(BF)
+    for k, prod in products(hz, lambda dx, dy: padu_ref[3 - dx : 3 - dx + GX, 3 - dy : 3 - dy + GY]):
+        terms_ref[(27 + 3 * k) * C : (30 + 3 * k) * C, :] = prod.astype(BF)
     gz = z_shifts(own(1)).T
-    for k in range(9):
-        dx, dy = divmod(k, 3)
-        rhs = padx_ref[dx + 1 : dx + 1 + GX, dy + 1 : dy + 1 + GY].reshape(ROWS, C)
-        prod = dot(gz, rhs) * scale
+    for k, prod in products(gz, lambda dx, dy: padx_ref[dx + 1 : dx + 1 + GX, dy + 1 : dy + 1 + GY]):
         for oz in range(3):
             block = prod[(2 - oz) * C : (3 - oz) * C, :].T
             terms_ref[(3 * k + oz) * C : (3 * k + oz + 1) * C, :] = block.astype(BF)
@@ -141,7 +151,7 @@
     perm = (rows == target).astype(F32).astype(BF)
     for field, w_ref in enumerate((w2_ref, w1t_ref)):
         shift_ref[...] = z_shifts(fields_ref[field].reshape(EXT_ROWS, C), field == 1).reshape(EX, EY, GZ, 3 * C)
-        value = conv(shift_ref, w_ref, field == 1) + grid_ref[field].astype(F32)
+        value = conv(shift_ref, w_ref, field == 1).reshape(ROWS, C) + grid_ref[field].astype(F32)
         high = value.astype(BF)
         if field == 0:
             out_ref[...] = dot(perm, high).astype(BF)
@@ -224,7 +234,7 @@
     return jnp.where(first, share, other).astype(F32), jnp.where(first, other, share).astype(F32)
 
 
-def per_device(features, cotangent, block_pos, weight_one, weight_two):
+def compute(features, cotangent, block_pos, weight_one, weight_two):
     total_rows = block_pos.shape[0] * 64 * lax.axis_size(NAMES)
     scale = float(total_rows) ** -0.5
     face_x = jax.ShapeDtypeStruct((2, FACE, C), BF)
@@ -259,7 +269,7 @@
     split = Mesh(mesh.devices.reshape(DIMS), NAMES)
     rows = P(NAMES, None)
     return jax.shard_map(
-        per_device,
+        compute,
         mesh=split,
         in_specs=(rows, rows, P(NAMES), P(), P()),
         out_specs=(rows, rows, P(), P()),

time: 149 us -> 146 us (0.980)
  Pallas kernels: 24.8 us -> 21.1 us
    pallas_call x3, Pallas kernels: 24.8 us -> 21.1 us  [call(): pl.pallas_call(kernel, out_shape=outs, in_specs=specs, out_specs=jax.tree...]
  transfers between devices with their start and end apart: 5 -> 5, of which waited for: 3 -> 3; matrix products, arithmetic and copies ran while one was open for 3% -> 3% of each run, Pallas kernels for 6% -> 5%
where the time goes in v4:
time: 146 us; the launch traced here: 145 us
  blocking collectives  80.5 us (55%)
  starting transfers between devices  23.7 us (16%)
  Pallas kernels  21.1 us (14%)
  waiting for transfers between devices  9.71 us (7%)
  other arithmetic  5.05 us (3%)
  local copies, waits for them, and re-layouts  4.13 us (3%)
    all_to_all x6, blocking collectives, swap(): return lax.all_to_all(values, axes, 0, 0, tiled=True)  80.5 us
    pallas_call x3, Pallas kernels, call(): pl.pallas_call(kernel, out_shape=outs, in_specs=specs, out_specs=jax.tree...  21.1 us
    ppermute x1, starting transfers between devices, reduce_terms(): other = lax.ppermute(share, 'core', [(0, 1), (1, 0)])  9.29 us
    ppermute x1, starting transfers between devices, exchange(): y_lo = lax.ppermute(face(1), GYN, forward)  6.81 us
    ppermute x1, waiting for transfers between devices, exchange(): y_hi = lax.ppermute(face(0), GYN, backward)  4.91 us
    ppermute x1, starting transfers between devices, exchange(): x_lo = lax.ppermute(x_faces[1], GXN, forward)  4.36 us
    ppermute x1, waiting for transfers between devices, exchange(): x_hi = lax.ppermute(x_faces[0], GXN, backward)  3.85 us
    reshape x2, local copies, waits for them, and re-layouts, transposed(): return weight.reshape(27, C, C).transpose(0, 2, 1).reshape(27 * C, C)  3.28 us
  transfers between devices with their start and end apart: 5, of which 3 were waited for; matrix products, arithmetic and copies ran while one was open for 3% of the time, Pallas kernels for 5%

profile of v4, /device:TPU:1, one launch (start us, length us, event | category | flops | bytes accessed | tf_op | source)
XLA Modules:
  0.0 144.9 jit_solution(3637248352254939237)
XLA Ops:
  0.6 0.0 copy-start.1
  0.6 3.0 %shard_map.84 = (bf16[2,1024,128]{2,1,0:T(8,128)(2,1)}, bf16[2,256,128]{2,1,0:T(8,128)(2,1)}, bf16[2,256,128]{2,1,0:T(8,128)(2,1)}, bf16[2,8,32,128]{3,2,1,0:T(8,128)(2,1)}, bf16[2,8,32,128]{3,2,1,0:T(8,128)(2,1)}) custom-call(s32[8]{0:T(128)} %pos_ref.3, bf16[512,128]{1,0:T(8,128)(2,1)} %feat_ref.1, bf16[512,128]{1,0:T(8,128)(2,1)} %cot_ref.1), custom_call_target="tpu_custom_call" | custom-call | tf_op jit(solution)/shard_map/pallas_call | solution.py:166
  3.6 4.4 %collective-permute-start = (bf16[2,256,128]{2,1,0:T(8,128)(2,1)}, bf16[2,256,128]{2,1,0:T(8,128)(2,1)S(1)}, u32[]{:S(2)}, u32[]{:S(2)}) collective-permute-start(bf16[2,256,128]{2,1,0:T(8,128)(2,1)} %get-tuple-element.14), channel_id=1, source_target_pairs={{0,4},{4,8},{8,12},{12,16},{16,20},{20,24},{24,28},{28,32},{32,36}... | collective-permute-start | bytes 393224 | tf_op jit(solution)/shard_map/ppermute | solution.py:195
  8.0 1.3 collective-permute-start.1
  9.3 0.9 collective-permute-done.refs_1_
  10.2 3.9 %collective-permute-done.1.refs_2_ = bf16[2,256,128]{2,1,0:T(8,128)(2,1)S(1)} collective-permute-done((bf16[2,256,128]{2,1,0:T(8,128)(2,1)}, bf16[2,256,128]{2,1,0:T(8,128)(2,1)S(1)}, u32[]{:S(2)}, u32[]{:S(2)}) %collective-permute-start.1) | collective-permute-done | bytes 131104 | tf_op jit(solution)/shard_map/ppermute | solution.py:196
  14.1 1.0 pad_maximum_fusion
  15.1 6.8 %collective-permute-start.2 = (bf16[2,12,32,128]{3,2,1,0:T(8,128)(2,1)S(1)}, bf16[2,12,32,128]{3,2,1,0:T(8,128)(2,1)S(1)}, u32[]{:S(2)}, u32[]{:S(2)}) collective-permute-start(bf16[2,12,32,128]{3,2,1,0:T(8,128)(2,1)S(1)} %pad_maximum_fusion), channel_id=1, source_target_pairs={{0,1},{1,2},{2,3},{4,5},{5,6},{6,7},{8,9},{9,10},{10,11},{12,13},{... | collective-permute-start | bytes 589832 | tf_op jit(solution)/shard_map/ppermute | solution.py:204
  21.9 0.9 pad_maximum_fusion.1
  22.8 1.9 %collective-permute-start.3 = (bf16[2,12,32,128]{3,2,1,0:T(8,128)(2,1)S(1)}, bf16[2,12,32,128]{3,2,1,0:T(8,128)(2,1)S(1)}, u32[]{:S(2)}, u32[]{:S(2)}) collective-permute-start(bf16[2,12,32,128]{3,2,1,0:T(8,128)(2,1)S(1)} %pad_maximum_fusion.1), channel_id=1, source_target_pairs={{1,0},{2,1},{3,2},{5,4},{6,5},{7,6},{9,8},{10,9},{11,10},{13,12},{... | collective-permute-start | bytes 589832 | tf_op jit(solution)/shard_map/ppermute | solution.py:205
  24.8 1.6 %copy.11 = bf16[27,128,128]{1,2,0:T(8,128)(2,1)} copy(bf16[27,128,128]{2,1,0:T(8,128)(2,1)S(1)} %bitcast.22) | data formatting | bytes 1769472 | tf_op jit(solution)/shard_map/reshape | solution.py:179
  26.4 0.0 collective-permute-done.2.refs_3_
  26.4 4.9 %collective-permute-done.3.refs_4_ = bf16[2,12,32,128]{3,2,1,0:T(8,128)(2,1)S(1)} collective-permute-done((bf16[2,12,32,128]{3,2,1,0:T(8,128)(2,1)S(1)}, bf16[2,12,32,128]{3,2,1,0:T(8,128)(2,1)S(1)}, u32[]{:S(2)}, u32[]{:S(2)}) %collective-permute-start.3) | collective-permute-done | bytes 196640 | tf_op jit(solution)/shard_map/ppermute | solution.py:205
  31.3 0.0 copy-done.2
  31.3 0.7 copy-done.5
  32.0 10.2 %shard_map.85 = (bf16[2,10,10,16,128]{4,3,2,1,0:T(8,128)(2,1)}, bf16[6912,128]{1,0:T(8,128)(2,1)}) custom-call(bf16[2,1024,128]{2,1,0:T(8,128)(2,1)} %get-tuple-element.13.refs_0_.grid_ref, bf16[2,256,128]{2,1,0:T(8,128)(2,1)} %copy-done.2, bf16[2,256,128]{2,1,0:T(8,128)(2,1)} %copy-done.3, bf16[2,12,32,128]{3,2,1,0:T(8,128)(2,1)} %copy-done.4, ...), custom_call_target="tpu_custom_call" | custom-call | tf_op jit(solution)/shard_map/pallas_call | solution.py:166
  42.3 6.0 %all_to_all.30 = bf16[2,3456,128]{2,1,0:T(8,128)(2,1)S(1)} all-to-all(bf16[2,3456,128]{2,1,0:T(8,128)(2,1)} %bitcast.21), channel_id=1, replica_groups=mesh['y_lo'=2,'x'=4,'z_hi'=4,'z_lo'=4,'y_hi'=2,'core'=2] {'core'}, dimensions={0} | all-to-all | bytes 3538944 | tf_op jit(solution)/shard_map/all_to_all | solution.py:210
  48.2 0.9 reduce_sum.39
  49.1 24.2 %all_to_all.31 = bf16[16,216,128]{2,1,0:T(8,128)(2,1)S(1)} all-to-all(bf16[16,216,128]{2,1,0:T(8,128)(2,1)S(1)} %bitcast.19), channel_id=1, replica_groups=mesh['y_lo'=2,'x'=4,'z_hi'=4,'z_lo'=4,'y_hi'=2,'core'=2] {'y_hi','y_lo',..., dimensions={0} | all-to-all | bytes 1769472 | tf_op jit(solution)/shard_map/all_to_all | solution.py:210
  73.4 0.1 convert_reduce_fusion
  73.5 7.1 %all_to_all.32 = f32[4,56,128]{2,1,0:T(8,128)S(1)} all-to-all(f32[4,56,128]{2,1,0:T(8,128)S(1)} %bitcast.24), channel_id=1, replica_groups=mesh['y_lo'=2,'x'=4,'z_hi'=4,'z_lo'=4,'y_hi'=2,'core'=2] {'z_lo'}, dimensions={0} | all-to-all | bytes 229376 | tf_op jit(solution)/shard_map/all_to_all | solution.py:210
  80.6 0.0 copy-start
  80.7 21.9 %all_to_all.33 = f32[4,56,128]{2,1,0:T(8,128)S(1)} all-to-all(f32[4,56,128]{2,1,0:T(8,128)S(1)} %broadcast_in_dim.9), channel_id=1, replica_groups=mesh['y_lo'=2,'x'=4,'z_hi'=4,'z_lo'=4,'y_hi'=2,'core'=2] {'z_hi'}, dimensions={0} | all-to-all | bytes 229376 | tf_op jit(solution)/shard_map/all_to_all | solution.py:210
  102.6 7.1 %all_to_all.34 = bf16[4,56,128]{2,1,0:T(8,128)(2,1)S(1)} all-to-all(bf16[4,56,128]{2,1,0:T(8,128)(2,1)S(1)} %broadcast_in_dim.10), channel_id=1, replica_groups=mesh['y_lo'=2,'x'=4,'z_hi'=4,'z_lo'=4,'y_hi'=2,'core'=2] {'z_lo'}, dimensions={0} | all-to-all | bytes 114688 | tf_op jit(solution)/shard_map/all_to_all | solution.py:210
  109.7 0.1 broadcast_in_dim.11
  109.8 14.2 %all_to_all.35 = bf16[16,216,128]{2,1,0:T(8,128)(2,1)S(1)} all-to-all(bf16[16,216,128]{2,1,0:T(8,128)(2,1)S(1)} %broadcast_in_dim.11), channel_id=1, replica_groups=mesh['y_lo'=2,'x'=4,'z_hi'=4,'z_lo'=4,'y_hi'=2,'core'=2] {'y_hi','y_lo',..., dimensions={0} | all-to-all | bytes 1769472 | tf_op jit(solution)/shard_map/all_to_all | solution.py:210
  124.0 9.3 %collective-permute-start.4 = (bf16[3456,128]{1,0:T(8,128)(2,1)S(1)}, bf16[3456,128]{1,0:T(8,128)(2,1)S(1)}, u32[]{:S(2)}, u32[]{:S(2)}) collective-permute-start(bf16[3456,128]{1,0:T(8,128)(2,1)S(1)} %bitcast.20), channel_id=1, source_target_pairs={{0,1},{1,0},{2,3},{3,2},{4,5},{5,4},{6,7},{7,6},{8,9},{9,8},{10,11... | collective-permute-start | bytes 2654216 | tf_op jit(solution)/shard_map/ppermute | solution.py:232
  133.3 0.0 copy-done
  133.3 1.6 %copy.12 = bf16[27,128,128]{1,2,0:T(8,128)(2,1)} copy(bf16[27,128,128]{2,1,0:T(8,128)(2,1)S(1)} %bitcast.17) | data formatting | bytes 1769472 | tf_op jit(solution)/shard_map/reshape | solution.py:179
  134.9 7.9 %shard_map.86 = (bf16[512,128]{1,0:T(8,128)(2,1)}, f32[512,128]{1,0:T(8,128)}) custom-call(s32[8]{0:T(128)} %pos_ref.3, bf16[2,1024,128]{2,1,0:T(8,128)(2,1)} %get-tuple-element.13.refs_0_.grid_ref, bf16[2,10,10,16,128]{4,3,2,1,0:T(8,128)(2,1)} %get-tuple-element.18.fields_ref, bf16[3456,128]{1,0:T(8,128)(2,1)} %w2_ref.1, bf16[3456,128]{1,0:T(8,128)(2,1)} %bitcast.23), custom_call_target="tpu_custom_call" | custom-call | flops 1811939328 | bytes 25165824 | tf_op jit(solution)/shard_map/pallas_call | solution.py:166
  142.8 0.0 collective-permute-done.4
  142.8 2.1 %select_convert_fusion = (f32[3456,128]{1,0:T(8,128)}, f32[3456,128]{1,0:T(8,128)}) fusion(bf16[3456,128]{1,0:T(8,128)(2,1)S(1)} %collective-permute-done.4, pred[]{:T(512)S(6)} %eq.3, bf16[16,216,128]{2,1,0:T(8,128)(2,1)S(1)} %all_to_all.35), kind=kLoop, calls=%fused_computation.1 | loop fusion | flops 1769472 | bytes 5308417 | tf_op jit(solution)/shard_map/convert_element_type | solution.py:234
  (15 shorter events, 0.1 us)
Async XLA Ops:
  0.6 24.1 %copy-start.1 = (bf16[3456,128]{1,0:T(8,128)(2,1)S(1)}, bf16[3456,128]{1,0:T(8,128)(2,1)}, u32[]{:S(2)}) copy-start(bf16[3456,128]{1,0:T(8,128)(2,1)} %w2_ref.1) | copy-start | bytes 2654212
  3.6 6.6 %collective-permute-start = (bf16[2,256,128]{2,1,0:T(8,128)(2,1)}, bf16[2,256,128]{2,1,0:T(8,128)(2,1)S(1)}, u32[]{:S(2)}, u32[]{:S(2)}) collective-permute-start(bf16[2,256,128]{2,1,0:T(8,128)(2,1)} %get-tuple-element.14), channel_id=1, source_target_pairs={{0,4},{4,8},{8,12},{12,16},{16,20},{20,24},{24,28},{28,32},{32,36}... | collective-permute-start | bytes 393224 | tf_op jit(solution)/shard_map/ppermute | solution.py:195
  8.0 6.1 %collective-permute-start.1 = (bf16[2,256,128]{2,1,0:T(8,128)(2,1)}, bf16[2,256,128]{2,1,0:T(8,128)(2,1)S(1)}, u32[]{:S(2)}, u32[]{:S(2)}) collective-permute-start(bf16[2,256,128]{2,1,0:T(8,128)(2,1)} %get-tuple-element.15), channel_id=1, source_target_pairs={{4,0},{8,4},{12,8},{16,12},{20,16},{24,20},{28,24},{32,28},{36,32}... | collective-permute-start | bytes 393224 | tf_op jit(solution)/shard_map/ppermute | solution.py:196
  10.2 21.1 %copy-start.2 = (bf16[2,256,128]{2,1,0:T(8,128)(2,1)}, bf16[2,256,128]{2,1,0:T(8,128)(2,1)S(1)}, u32[]{:S(2)}) copy-start(bf16[2,256,128]{2,1,0:T(8,128)(2,1)S(1)} %collective-permute-done.refs_1_) | copy-start | bytes 393220
  14.1 17.2 %copy-start.3 = (bf16[2,256,128]{2,1,0:T(8,128)(2,1)}, bf16[2,256,128]{2,1,0:T(8,128)(2,1)S(1)}, u32[]{:S(2)}) copy-start(bf16[2,256,128]{2,1,0:T(8,128)(2,1)S(1)} %collective-permute-done.1.refs_2_) | copy-start | bytes 393220
  15.1 11.3 %collective-permute-start.2 = (bf16[2,12,32,128]{3,2,1,0:T(8,128)(2,1)S(1)}, bf16[2,12,32,128]{3,2,1,0:T(8,128)(2,1)S(1)}, u32[]{:S(2)}, u32[]{:S(2)}) collective-permute-start(bf16[2,12,32,128]{3,2,1,0:T(8,128)(2,1)S(1)} %pad_maximum_fusion), channel_id=1, source_target_pairs={{0,1},{1,2},{2,3},{4,5},{5,6},{6,7},{8,9},{9,10},{10,11},{12,13},{... | collective-permute-start | bytes 589832 | tf_op jit(solution)/shard_map/ppermute | solution.py:204
  22.8 8.5 %collective-permute-start.3 = (bf16[2,12,32,128]{3,2,1,0:T(8,128)(2,1)S(1)}, bf16[2,12,32,128]{3,2,1,0:T(8,128)(2,1)S(1)}, u32[]{:S(2)}, u32[]{:S(2)}) collective-permute-start(bf16[2,12,32,128]{3,2,1,0:T(8,128)(2,1)S(1)} %pad_maximum_fusion.1), channel_id=1, source_target_pairs={{1,0},{2,1},{3,2},{5,4},{6,5},{7,6},{9,8},{10,9},{11,10},{13,12},{... | collective-permute-start | bytes 589832 | tf_op jit(solution)/shard_map/ppermute | solution.py:205
  26.4 4.9 %copy-start.4 = (bf16[2,12,32,128]{3,2,1,0:T(8,128)(2,1)}, bf16[2,12,32,128]{3,2,1,0:T(8,128)(2,1)S(1)}, u32[]{:S(2)}) copy-start(bf16[2,12,32,128]{3,2,1,0:T(8,128)(2,1)S(1)} %collective-permute-done.2.refs_3_) | copy-start | bytes 589828
  31.3 0.7 copy-start.5
  80.6 52.7 %copy-start = (bf16[3456,128]{1,0:T(8,128)(2,1)S(1)}, bf16[3456,128]{1,0:T(8,128)(2,1)}, u32[]{:S(2)}) copy-start(bf16[3456,128]{1,0:T(8,128)(2,1)} %refs_5_.1) | copy-start | bytes 2654212
  124.0 18.8 %collective-permute-start.4 = (bf16[3456,128]{1,0:T(8,128)(2,1)S(1)}, bf16[3456,128]{1,0:T(8,128)(2,1)S(1)}, u32[]{:S(2)}, u32[]{:S(2)}) collective-permute-start(bf16[3456,128]{1,0:T(8,128)(2,1)S(1)} %bitcast.20), channel_id=1, source_target_pairs={{0,1},{1,0},{2,3},{3,2},{4,5},{5,4},{6,7},{7,6},{8,9},{9,8},{10,11... | collective-permute-start | bytes 2654216 | tf_op jit(solution)/shard_map/ppermute | solution.py:232

commit v5 on v4

--- a/solution.py
+++ b/solution.py
@@ -110,11 +110,12 @@
 
 
 def middle_kernel(
-    scale, grid_ref, xlo_ref, xhi_ref, ylo_ref, yhi_ref, w1_ref, w2t_ref,
-    fields_ref, terms_ref, padx_ref, padu_ref, shift_ref, pre_ref,
+    grid_ref, xlo_ref, xhi_ref, ylo_ref, yhi_ref, w1_ref, w2t_ref, pairs_ref, padx_ref, padu_ref, shift_ref, pre_ref,
 ):
     fill_pad(padx_ref, grid_ref[0], xlo_ref[0], xhi_ref[0], ylo_ref[0], yhi_ref[0])
     fill_pad(padu_ref, grid_ref[1], xlo_ref[1], xhi_ref[1], ylo_ref[1], yhi_ref[1])
+    pairs_ref[0, 0] = padx_ref[1 : PX - 1, 1 : PY - 1]
+    pairs_ref[1, 1] = padu_ref[1 : PX - 1, 1 : PY - 1]
     shift_ref[...] = z_shifts(padx_ref[...].reshape(PAD_ROWS, C)).reshape(PX, PY, GZ, 3 * C)
     pre_ref[...] = conv(shift_ref, w1_ref, False).reshape(EXT_ROWS, C)
     shift_ref[...] = z_shifts(padu_ref[...].reshape(PAD_ROWS, C), True).reshape(PX, PY, GZ, 3 * C)
@@ -122,36 +123,49 @@
     pre = pre_ref[...]
     mask = active_rows(padx_ref[1 : PX - 1, 1 : PY - 1].astype(F32)).reshape(EXT_ROWS, C)
     sig = jax.nn.sigmoid(pre)
-    fields_ref[0] = (pre * sig * mask).astype(BF).reshape(EX, EY, GZ, C)
-    fields_ref[1] = (back * (sig * (1.0 + pre * (1.0 - sig))) * mask).astype(BF).reshape(EX, EY, GZ, C)
-
-    def own(field):
-        return fields_ref[field, 1 : EX - 1, 1 : EY - 1].reshape(ROWS, C)
-
-    def products(lhs, rhs_of):
-        for first in range(0, 9, 2):
-            ks = range(first, min(first + 2, 9))
-            prod = dot(lhs, jnp.concatenate([rhs_of(*divmod(k, 3)).reshape(ROWS, C) for k in ks], axis=1)) * scale
-            for n, k in enumerate(ks):
-                yield k, prod[:, n * C : (n + 1) * C]
-
-    hz = z_shifts(own(0)).T
-    for k, prod in products(hz, lambda dx, dy: padu_ref[3 - dx : 3 - dx + GX, 3 - dy : 3 - dy + GY]):
-        terms_ref[(27 + 3 * k) * C : (30 + 3 * k) * C, :] = prod.astype(BF)
-    gz = z_shifts(own(1)).T
-    for k, prod in products(gz, lambda dx, dy: padx_ref[dx + 1 : dx + 1 + GX, dy + 1 : dy + 1 + GY]):
-        for oz in range(3):
-            block = prod[(2 - oz) * C : (3 - oz) * C, :].T
-            terms_ref[(3 * k + oz) * C : (3 * k + oz + 1) * C, :] = block.astype(BF)
-
-
-def final_kernel(pos_ref, grid_ref, fields_ref, w2_ref, w1t_ref, out_ref, grad_ref, shift_ref):
+    pairs_ref[1, 0] = (pre * sig * mask).astype(BF).reshape(EX, EY, GZ, C)
+    pairs_ref[0, 1] = (back * (sig * (1.0 + pre * (1.0 - sig))) * mask).astype(BF).reshape(EX, EY, GZ, C)
+
+
+def gram_kernel(scale, which_ref, pair_ref, term_ref):
+    del which_ref
+    left = pair_ref[0, 0, 1 : EX - 1, 1 : EY - 1].reshape(ROWS, C)
+    lhs = z_shifts(left).T
+    for first in range(0, 9, 2):
+        ks = range(first, min(first + 2, 9))
+        starts = [(2 - k // 3, 2 - k % 3) for k in ks]
+        rhs = [pair_ref[0, 1, x : x + GX, y : y + GY].reshape(ROWS, C) for x, y in starts]
+        prod = dot(lhs, jnp.concatenate(rhs, axis=1)) * scale
+        for n, k in enumerate(ks):
+            term_ref[3 * k * C : 3 * (k + 1) * C, :] = prod[:, n * C : (n + 1) * C].astype(term_ref.dtype)
+
+
+def gram(scale, which, pairs, dtype):
+    spec = pltpu.PrefetchScalarGridSpec(
+        num_scalar_prefetch=1,
+        grid=(1,),
+        in_specs=[pl.BlockSpec((1, 2, EX, EY, GZ, C), lambda i, which_ref: (which_ref[0], 0, 0, 0, 0, 0))],
+        out_specs=pl.BlockSpec((27 * C, C), lambda i, which_ref: (0, 0)),
+    )
+    return pl.pallas_call(
+        lambda *refs: gram_kernel(scale, *refs),
+        grid_spec=spec,
+        out_shape=jax.ShapeDtypeStruct((27 * C, C), dtype),
+        compiler_params=pltpu.CompilerParams(vmem_limit_bytes=56 << 20),
+        interpret=INTERPRET,
+        cost_estimate=pl.CostEstimate(flops=2 * 27 * ROWS * C * C, transcendentals=0, bytes_accessed=9 << 20),
+    )(which.reshape(1), pairs)
+
+
+def final_kernel(pos_ref, pairs_ref, w2_ref, w1t_ref, out_ref, grad_ref, shift_ref):
     target = grid_row(pos_ref, lax.broadcasted_iota(jnp.int32, (SLOTS * 64, 1), 0))
     rows = lax.broadcasted_iota(jnp.int32, (SLOTS * 64, ROWS), 1)
     perm = (rows == target).astype(F32).astype(BF)
     for field, w_ref in enumerate((w2_ref, w1t_ref)):
-        shift_ref[...] = z_shifts(fields_ref[field].reshape(EXT_ROWS, C), field == 1).reshape(EX, EY, GZ, 3 * C)
-        value = conv(shift_ref, w_ref, field == 1).reshape(ROWS, C) + grid_ref[field].astype(F32)
+        source = pairs_ref[1 - field, field].reshape(EXT_ROWS, C)
+        shift_ref[...] = z_shifts(source, field == 1).reshape(EX, EY, GZ, 3 * C)
+        straight = pairs_ref[field, field, 1 : EX - 1, 1 : EY - 1].reshape(ROWS, C)
+        value = conv(shift_ref, w_ref, field == 1).reshape(ROWS, C) + straight.astype(F32)
         high = value.astype(BF)
         if field == 0:
             out_ref[...] = dot(perm, high).astype(BF)
@@ -219,18 +233,23 @@
     return swap(jnp.broadcast_to(values, (lax.axis_size(axes), *values.shape)), axes)
 
 
-def reduce_terms(terms):
-    share = scatter_sum(terms, "core").astype(BF)
+def reduce_terms(scale, pairs):
+    core = lax.axis_index("core").astype(jnp.int32)
+    cross = [(0, 1), (1, 0)]
+    sent = gram(scale, 1 - core, pairs, BF)
+    got = lax.ppermute(sent, "core", cross)
+    own = gram(scale, core, pairs, F32)
+    share = (own + got.astype(F32)).astype(BF)
     share = scatter_sum(share, YX)
     rows = share.shape[0]
     padded = -(-rows // (8 * lax.axis_size("z_lo"))) * 8 * lax.axis_size("z_lo")
     share = jnp.pad(share, ((0, padded - rows), (0, 0)))
-    share = scatter_sum(share, "z_lo")
-    share = gather(share, "z_hi").sum(axis=0).astype(BF)
+    share = scatter_sum(share, "z_lo").astype(BF)
+    share = gather(share, "z_hi").astype(F32).sum(axis=0).astype(BF)
     share = gather(share, "z_lo").reshape(padded, C)[:rows]
     share = gather(share, YX).reshape(-1, C)
-    other = lax.ppermute(share, "core", [(0, 1), (1, 0)])
-    first = lax.axis_index("core") == 0
+    other = lax.ppermute(share, "core", cross)
+    first = core == 0
     return jnp.where(first, share, other).astype(F32), jnp.where(first, other, share).astype(F32)
 
 
@@ -246,22 +265,23 @@
         args=(block_pos, features, cotangent),
     )
     halo = exchange(faces[:2], faces[2:])
+    one_t, two_t = lax.optimization_barrier((transposed(weight_one), transposed(weight_two)))
     pad = pltpu.VMEM((PX, PY, GZ, C), BF)
-    fields, terms = call(
-        lambda *refs: middle_kernel(scale, *refs),
-        (jax.ShapeDtypeStruct((2, EX, EY, GZ, C), BF), jax.ShapeDtypeStruct((54 * C, C), BF)),
+    pairs = call(
+        middle_kernel,
+        jax.ShapeDtypeStruct((2, 2, EX, EY, GZ, C), BF),
         scratch=(pad, pad, pltpu.VMEM((PX, PY, GZ, 3 * C), BF), pltpu.VMEM((EXT_ROWS, C), F32)),
-        args=(grid, *halo, weight_one, transposed(weight_two)),
+        args=(grid, *halo, weight_one, two_t),
     )
     output, input_grad = call(
         final_kernel,
         (jax.ShapeDtypeStruct(features.shape, BF), jax.ShapeDtypeStruct(features.shape, F32)),
         scratch=(pltpu.VMEM((EX, EY, GZ, 3 * C), BF),),
         smem=1,
-        args=(block_pos, grid, fields, weight_two, transposed(weight_one)),
+        args=(block_pos, pairs, weight_two, one_t),
         cost=pl.CostEstimate(flops=2 * 2 * 27 * ROWS * C * C, transcendentals=0, bytes_accessed=24 << 20),
     )
-    grad_one, grad_two = reduce_terms(terms)
+    grad_one, grad_two = reduce_terms(scale, pairs)
     return output, input_grad, grad_one, grad_two
 
 

time: 146 us -> 144 us (0.986)
  blocking collectives: 80.5 us -> 74 us
  Pallas kernels: 21.1 us -> 26 us
  waiting for transfers between devices: 9.71 us -> 8.05 us
    pallas_call x0 -> x2, Pallas kernels: none -> 6.92 us  [gram(): pl.pallas_call(lambda *refs: gram_kernel(scale, *refs), grid_spec=spec, o...]
    all_to_all x6 -> x5, blocking collectives: 80.5 us -> 74 us  [swap(): return lax.all_to_all(values, axes, 0, 0, tiled=True)]
    pallas_call x3, Pallas kernels: 21.1 us -> 19.1 us  [call(): pl.pallas_call(kernel, out_shape=outs, in_specs=specs, out_specs=jax.tree...]
    ppermute x1, waiting for transfers between devices: 4.91 us -> 3.25 us  [exchange(): y_hi = lax.ppermute(face(0), GYN, backward)]
    convert_element_type x0 -> x1, other arithmetic: none -> 1.65 us  [reduce_terms(): share = (own + got.astype(F32)).astype(BF)]
    ppermute x1 -> x2, starting transfers between devices: 9.29 us -> 10.6 us  [the longest x1 8.7 us: reduce_terms(): other = lax.ppermute(share, 'core', cross)]
  transfers between devices with their start and end apart: 5 -> 6, of which waited for: 3 -> 3; matrix products, arithmetic and copies ran while one was open for 3% -> 3% of each run, Pallas kernels for 5% -> 8%
where the time goes in v5:
time: 144 us
  blocking collectives  74 us (51%)
  Pallas kernels  26 us (18%)
  starting transfers between devices  25 us (17%)
  waiting for transfers between devices  8.05 us (6%)
  other arithmetic  5.79 us (4%)
  local copies, waits for them, and re-layouts  4.13 us (3%)
    all_to_all x5, blocking collectives, swap(): return lax.all_to_all(values, axes, 0, 0, tiled=True)  74 us
    pallas_call x3, Pallas kernels, call(): pl.pallas_call(kernel, out_shape=outs, in_specs=specs, out_specs=jax.tree...  19.1 us
    ppermute x1, starting transfers between devices, reduce_terms(): other = lax.ppermute(share, 'core', cross)  8.7 us
    pallas_call x2, Pallas kernels, gram(): pl.pallas_call(lambda *refs: gram_kernel(scale, *refs), grid_spec=spec, o...  6.92 us
    ppermute x1, starting transfers between devices, exchange(): y_lo = lax.ppermute(face(1), GYN, forward)  6.8 us
    ppermute x1, starting transfers between devices, exchange(): x_lo = lax.ppermute(x_faces[1], GXN, forward)  4.36 us
    ppermute x1, waiting for transfers between devices, exchange(): x_hi = lax.ppermute(x_faces[0], GXN, backward)  3.85 us
    reshape x2, local copies, waits for them, and re-layouts, transposed(): return weight.reshape(27, C, C).transpose(0, 2, 1).reshape(27 * C, C)  3.27 us
  transfers between devices with their start and end apart: 6, of which 3 were waited for; matrix products, arithmetic and copies ran while one was open for 3% of the time, Pallas kernels for 8%

profile of v5, /device:TPU:1, one launch (start us, length us, event | category | flops | bytes accessed | tf_op | source)
XLA Modules:
  0.0 143.8 jit_solution(4648898052153558118)
XLA Ops:
  0.6 0.0 copy-start.1
  0.6 0.0 copy-start
  0.7 3.0 %shard_map.84 = (bf16[2,1024,128]{2,1,0:T(8,128)(2,1)}, bf16[2,256,128]{2,1,0:T(8,128)(2,1)}, bf16[2,256,128]{2,1,0:T(8,128)(2,1)}, bf16[2,8,32,128]{3,2,1,0:T(8,128)(2,1)}, bf16[2,8,32,128]{3,2,1,0:T(8,128)(2,1)}) custom-call(s32[8]{0:T(128)} %pos_ref.3, bf16[512,128]{1,0:T(8,128)(2,1)} %feat_ref.1, bf16[512,128]{1,0:T(8,128)(2,1)} %cot_ref.1), custom_call_target="tpu_custom_call" | custom-call | tf_op jit(solution)/shard_map/pallas_call | solution.py:180
  3.7 4.4 %collective-permute-start = (bf16[2,256,128]{2,1,0:T(8,128)(2,1)}, bf16[2,256,128]{2,1,0:T(8,128)(2,1)S(1)}, u32[]{:S(2)}, u32[]{:S(2)}) collective-permute-start(bf16[2,256,128]{2,1,0:T(8,128)(2,1)} %get-tuple-element.14), channel_id=1, source_target_pairs={{0,4},{4,8},{8,12},{12,16},{16,20},{20,24},{24,28},{28,32},{32,36}... | collective-permute-start | bytes 393224 | tf_op jit(solution)/shard_map/ppermute | solution.py:209
  8.1 1.3 collective-permute-start.1
  9.4 0.9 collective-permute-done.xlo_ref
  10.3 3.9 %collective-permute-done.1.xhi_ref = bf16[2,256,128]{2,1,0:T(8,128)(2,1)S(1)} collective-permute-done((bf16[2,256,128]{2,1,0:T(8,128)(2,1)}, bf16[2,256,128]{2,1,0:T(8,128)(2,1)S(1)}, u32[]{:S(2)}, u32[]{:S(2)}) %collective-permute-start.1) | collective-permute-done | bytes 131104 | tf_op jit(solution)/shard_map/ppermute | solution.py:210
  14.2 1.0 pad_maximum_fusion
  15.1 6.8 %collective-permute-start.2 = (bf16[2,12,32,128]{3,2,1,0:T(8,128)(2,1)S(1)}, bf16[2,12,32,128]{3,2,1,0:T(8,128)(2,1)S(1)}, u32[]{:S(2)}, u32[]{:S(2)}) collective-permute-start(bf16[2,12,32,128]{3,2,1,0:T(8,128)(2,1)S(1)} %pad_maximum_fusion), channel_id=1, source_target_pairs={{0,1},{1,2},{2,3},{4,5},{5,6},{6,7},{8,9},{9,10},{10,11},{12,13},{... | collective-permute-start | bytes 589832 | tf_op jit(solution)/shard_map/ppermute | solution.py:218
  22.0 0.9 pad_maximum_fusion.1
  22.9 1.9 %collective-permute-start.3 = (bf16[2,12,32,128]{3,2,1,0:T(8,128)(2,1)S(1)}, bf16[2,12,32,128]{3,2,1,0:T(8,128)(2,1)S(1)}, u32[]{:S(2)}, u32[]{:S(2)}) collective-permute-start(bf16[2,12,32,128]{3,2,1,0:T(8,128)(2,1)S(1)} %pad_maximum_fusion.1), channel_id=1, source_target_pairs={{1,0},{2,1},{3,2},{5,4},{6,5},{7,6},{9,8},{10,9},{11,10},{13,12},{... | collective-permute-start | bytes 589832 | tf_op jit(solution)/shard_map/ppermute | solution.py:219
  24.8 1.6 %copy.12 = bf16[27,128,128]{1,2,0:T(8,128)(2,1)} copy(bf16[27,128,128]{2,1,0:T(8,128)(2,1)S(1)} %bitcast.22) | data formatting | bytes 1769472 | tf_op jit(solution)/shard_map/reshape | solution.py:193
  26.5 1.6 %copy.11 = bf16[27,128,128]{1,2,0:T(8,128)(2,1)} copy(bf16[27,128,128]{2,1,0:T(8,128)(2,1)S(1)} %bitcast.19) | data formatting | bytes 1769472 | tf_op jit(solution)/shard_map/reshape | solution.py:193
  28.1 0.0 collective-permute-done.2.ylo_ref
  28.1 0.0 copy-start.4
  28.1 3.2 %collective-permute-done.3.yhi_ref = bf16[2,12,32,128]{3,2,1,0:T(8,128)(2,1)S(1)} collective-permute-done((bf16[2,12,32,128]{3,2,1,0:T(8,128)(2,1)S(1)}, bf16[2,12,32,128]{3,2,1,0:T(8,128)(2,1)S(1)}, u32[]{:S(2)}, u32[]{:S(2)}) %collective-permute-start.3) | collective-permute-done | bytes 196640 | tf_op jit(solution)/shard_map/ppermute | solution.py:219
  31.4 0.7 copy-done.5
  32.1 8.1 %shard_map.85.pairs_ref.refs_1_ = bf16[2,2,10,10,16,128]{5,4,3,2,1,0:T(8,128)(2,1)} custom-call(bf16[2,1024,128]{2,1,0:T(8,128)(2,1)} %get-tuple-element.13.grid_ref, bf16[2,256,128]{2,1,0:T(8,128)(2,1)} %copy-done.2, bf16[2,256,128]{2,1,0:T(8,128)(2,1)} %copy-done.3, bf16[2,12,32,128]{3,2,1,0:T(8,128)(2,1)} %copy-done.4, ...), custom_call_target="tpu_custom_call" | custom-call | tf_op jit(solution)/shard_map/pallas_call | solution.py:180
  40.2 3.3 %shard_map.88 = bf16[3456,128]{1,0:T(8,128)(2,1)} custom-call(s32[1]{0:T(128)} %bitcast.9.refs_0_, bf16[2,2,10,10,16,128]{5,4,3,2,1,0:T(8,128)(2,1)} %shard_map.85.pairs_ref.refs_1_), custom_call_target="tpu_custom_call" | custom-call | flops 905969664 | bytes 9437184 | tf_op jit(solution)/shard_map/pallas_call | solution.py:150
  43.5 1.9 %collective-permute-start.4 = (bf16[3456,128]{1,0:T(8,128)(2,1)}, bf16[3456,128]{1,0:T(8,128)(2,1)S(1)}, u32[]{:S(2)}, u32[]{:S(2)}) collective-permute-start(bf16[3456,128]{1,0:T(8,128)(2,1)} %shard_map.88), channel_id=1, source_target_pairs={{0,1},{1,0},{2,3},{3,2},{4,5},{5,4},{6,7},{7,6},{8,9},{9,8},{10,11... | collective-permute-start | bytes 2654216 | tf_op jit(solution)/shard_map/ppermute | solution.py:240
  45.4 3.6 %shard_map.87 = f32[3456,128]{1,0:T(8,128)} custom-call(s32[1]{0:T(128)} %bitcast.8.refs_0_, bf16[2,2,10,10,16,128]{5,4,3,2,1,0:T(8,128)(2,1)} %shard_map.85.pairs_ref.refs_1_), custom_call_target="tpu_custom_call" | custom-call | flops 905969664 | bytes 9437184 | tf_op jit(solution)/shard_map/pallas_call | solution.py:150
  49.0 1.6 %add_convert_fusion = bf16[3456,128]{1,0:T(8,128)(2,1)S(1)} fusion(f32[3456,128]{1,0:T(8,128)} %shard_map.87, bf16[3456,128]{1,0:T(8,128)(2,1)S(1)} %collective-permute-done.4), kind=kLoop, calls=%fused_computation.1 | loop fusion | flops 1327104 | bytes 3538944 | tf_op jit(solution)/shard_map/convert_element_type | solution.py:242
  50.7 24.1 %all_to_all.25 = bf16[16,216,128]{2,1,0:T(8,128)(2,1)S(1)} all-to-all(bf16[16,216,128]{2,1,0:T(8,128)(2,1)S(1)} %bitcast.18), channel_id=1, replica_groups=mesh['y_lo'=2,'x'=4,'z_hi'=4,'z_lo'=4,'y_hi'=2,'core'=2] {'y_hi','y_lo',..., dimensions={0} | all-to-all | bytes 1769472 | tf_op jit(solution)/shard_map/all_to_all | solution.py:224
  74.8 0.1 convert_reduce_fusion
  74.9 7.1 %all_to_all.26 = f32[4,56,128]{2,1,0:T(8,128)S(1)} all-to-all(f32[4,56,128]{2,1,0:T(8,128)S(1)} %bitcast.24), channel_id=1, replica_groups=mesh['y_lo'=2,'x'=4,'z_hi'=4,'z_lo'=4,'y_hi'=2,'core'=2] {'z_lo'}, dimensions={0} | all-to-all | bytes 229376 | tf_op jit(solution)/shard_map/all_to_all | solution.py:224
  82.0 21.6 %all_to_all.27 = bf16[4,56,128]{2,1,0:T(8,128)(2,1)S(1)} all-to-all(bf16[4,56,128]{2,1,0:T(8,128)(2,1)S(1)} %broadcast_in_dim.9), channel_id=1, replica_groups=mesh['y_lo'=2,'x'=4,'z_hi'=4,'z_lo'=4,'y_hi'=2,'core'=2] {'z_hi'}, dimensions={0} | all-to-all | bytes 114688 | tf_op jit(solution)/shard_map/all_to_all | solution.py:224
  103.6 7.1 %all_to_all.28 = bf16[4,56,128]{2,1,0:T(8,128)(2,1)S(1)} all-to-all(bf16[4,56,128]{2,1,0:T(8,128)(2,1)S(1)} %broadcast_in_dim.10), channel_id=1, replica_groups=mesh['y_lo'=2,'x'=4,'z_hi'=4,'z_lo'=4,'y_hi'=2,'core'=2] {'z_lo'}, dimensions={0} | all-to-all | bytes 114688 | tf_op jit(solution)/shard_map/all_to_all | solution.py:224
  110.8 0.1 broadcast_in_dim.11
  110.9 14.1 %all_to_all.29 = bf16[16,216,128]{2,1,0:T(8,128)(2,1)S(1)} all-to-all(bf16[16,216,128]{2,1,0:T(8,128)(2,1)S(1)} %broadcast_in_dim.11), channel_id=1, replica_groups=mesh['y_lo'=2,'x'=4,'z_hi'=4,'z_lo'=4,'y_hi'=2,'core'=2] {'y_hi','y_lo',..., dimensions={0} | all-to-all | bytes 1769472 | tf_op jit(solution)/shard_map/all_to_all | solution.py:224
  125.0 8.7 %collective-permute-start.5 = (bf16[3456,128]{1,0:T(8,128)(2,1)S(1)}, bf16[3456,128]{1,0:T(8,128)(2,1)S(1)}, u32[]{:S(2)}, u32[]{:S(2)}) collective-permute-start(bf16[3456,128]{1,0:T(8,128)(2,1)S(1)} %bitcast.20), channel_id=1, source_target_pairs={{0,1},{1,0},{2,3},{3,2},{4,5},{5,4},{6,7},{7,6},{8,9},{9,8},{10,11... | collective-permute-start | bytes 2654216 | tf_op jit(solution)/shard_map/ppermute | solution.py:251
  133.7 8.0 %shard_map.86 = (bf16[512,128]{1,0:T(8,128)(2,1)}, f32[512,128]{1,0:T(8,128)}) custom-call(s32[8]{0:T(128)} %pos_ref.3, bf16[2,2,10,10,16,128]{5,4,3,2,1,0:T(8,128)(2,1)} %shard_map.85.pairs_ref.refs_1_, bf16[3456,128]{1,0:T(8,128)(2,1)} %w2_ref.1, bf16[3456,128]{1,0:T(8,128)(2,1)} %bitcast.23), custom_call_target="tpu_custom_call" | custom-call | flops 1811939328 | bytes 25165824 | tf_op jit(solution)/shard_map/pallas_call | solution.py:180
  141.7 2.1 %select_convert_fusion = (f32[3456,128]{1,0:T(8,128)}, f32[3456,128]{1,0:T(8,128)}) fusion(bf16[3456,128]{1,0:T(8,128)(2,1)S(1)} %collective-permute-done.5, pred[]{:T(512)S(6)} %eq.3, bf16[16,216,128]{2,1,0:T(8,128)(2,1)S(1)} %all_to_all.29), kind=kLoop, calls=%fused_computation.2 | loop fusion | flops 1769472 | bytes 5308417 | tf_op jit(solution)/shard_map/convert_element_type | solution.py:253
  (18 shorter events, 0.1 us)
Async XLA Ops:
  0.6 24.2 %copy-start.1 = (bf16[3456,128]{1,0:T(8,128)(2,1)S(1)}, bf16[3456,128]{1,0:T(8,128)(2,1)}, u32[]{:S(2)}) copy-start(bf16[3456,128]{1,0:T(8,128)(2,1)} %w2_ref.1) | copy-start | bytes 2654212
  0.6 25.8 %copy-start = (bf16[3456,128]{1,0:T(8,128)(2,1)S(1)}, bf16[3456,128]{1,0:T(8,128)(2,1)}, u32[]{:S(2)}) copy-start(bf16[3456,128]{1,0:T(8,128)(2,1)} %w1_ref.1) | copy-start | bytes 2654212
  3.7 6.6 %collective-permute-start = (bf16[2,256,128]{2,1,0:T(8,128)(2,1)}, bf16[2,256,128]{2,1,0:T(8,128)(2,1)S(1)}, u32[]{:S(2)}, u32[]{:S(2)}) collective-permute-start(bf16[2,256,128]{2,1,0:T(8,128)(2,1)} %get-tuple-element.14), channel_id=1, source_target_pairs={{0,4},{4,8},{8,12},{12,16},{16,20},{20,24},{24,28},{28,32},{32,36}... | collective-permute-start | bytes 393224 | tf_op jit(solution)/shard_map/ppermute | solution.py:209
  8.1 6.1 %collective-permute-start.1 = (bf16[2,256,128]{2,1,0:T(8,128)(2,1)}, bf16[2,256,128]{2,1,0:T(8,128)(2,1)S(1)}, u32[]{:S(2)}, u32[]{:S(2)}) collective-permute-start(bf16[2,256,128]{2,1,0:T(8,128)(2,1)} %get-tuple-element.15), channel_id=1, source_target_pairs={{4,0},{8,4},{12,8},{16,12},{20,16},{24,20},{28,24},{32,28},{36,32}... | collective-permute-start | bytes 393224 | tf_op jit(solution)/shard_map/ppermute | solution.py:210
  10.3 17.8 %copy-start.2 = (bf16[2,256,128]{2,1,0:T(8,128)(2,1)}, bf16[2,256,128]{2,1,0:T(8,128)(2,1)S(1)}, u32[]{:S(2)}) copy-start(bf16[2,256,128]{2,1,0:T(8,128)(2,1)S(1)} %collective-permute-done.xlo_ref) | copy-start | bytes 393220
  14.2 14.0 %copy-start.3 = (bf16[2,256,128]{2,1,0:T(8,128)(2,1)}, bf16[2,256,128]{2,1,0:T(8,128)(2,1)S(1)}, u32[]{:S(2)}) copy-start(bf16[2,256,128]{2,1,0:T(8,128)(2,1)S(1)} %collective-permute-done.1.xhi_ref) | copy-start | bytes 393220
  15.1 13.0 %collective-permute-start.2 = (bf16[2,12,32,128]{3,2,1,0:T(8,128)(2,1)S(1)}, bf16[2,12,32,128]{3,2,1,0:T(8,128)(2,1)S(1)}, u32[]{:S(2)}, u32[]{:S(2)}) collective-permute-start(bf16[2,12,32,128]{3,2,1,0:T(8,128)(2,1)S(1)} %pad_maximum_fusion), channel_id=1, source_target_pairs={{0,1},{1,2},{2,3},{4,5},{5,6},{6,7},{8,9},{9,10},{10,11},{12,13},{... | collective-permute-start | bytes 589832 | tf_op jit(solution)/shard_map/ppermute | solution.py:218
  22.9 8.5 %collective-permute-start.3 = (bf16[2,12,32,128]{3,2,1,0:T(8,128)(2,1)S(1)}, bf16[2,12,32,128]{3,2,1,0:T(8,128)(2,1)S(1)}, u32[]{:S(2)}, u32[]{:S(2)}) collective-permute-start(bf16[2,12,32,128]{3,2,1,0:T(8,128)(2,1)S(1)} %pad_maximum_fusion.1), channel_id=1, source_target_pairs={{1,0},{2,1},{3,2},{5,4},{6,5},{7,6},{9,8},{10,9},{11,10},{13,12},{... | collective-permute-start | bytes 589832 | tf_op jit(solution)/shard_map/ppermute | solution.py:219
  28.1 3.3 %copy-start.4 = (bf16[2,12,32,128]{3,2,1,0:T(8,128)(2,1)}, bf16[2,12,32,128]{3,2,1,0:T(8,128)(2,1)S(1)}, u32[]{:S(2)}) copy-start(bf16[2,12,32,128]{3,2,1,0:T(8,128)(2,1)S(1)} %collective-permute-done.2.ylo_ref) | copy-start | bytes 589828
  31.4 0.7 copy-start.5
  43.5 5.5 %collective-permute-start.4 = (bf16[3456,128]{1,0:T(8,128)(2,1)}, bf16[3456,128]{1,0:T(8,128)(2,1)S(1)}, u32[]{:S(2)}, u32[]{:S(2)}) collective-permute-start(bf16[3456,128]{1,0:T(8,128)(2,1)} %shard_map.88), channel_id=1, source_target_pairs={{0,1},{1,0},{2,3},{3,2},{4,5},{5,4},{6,7},{7,6},{8,9},{9,8},{10,11... | collective-permute-start | bytes 2654216 | tf_op jit(solution)/shard_map/ppermute | solution.py:240
  125.0 16.7 %collective-permute-start.5 = (bf16[3456,128]{1,0:T(8,128)(2,1)S(1)}, bf16[3456,128]{1,0:T(8,128)(2,1)S(1)}, u32[]{:S(2)}, u32[]{:S(2)}) collective-permute-start(bf16[3456,128]{1,0:T(8,128)(2,1)S(1)} %bitcast.20), channel_id=1, source_target_pairs={{0,1},{1,0},{2,3},{3,2},{4,5},{5,4},{6,7},{7,6},{8,9},{9,8},{10,11... | collective-permute-start | bytes 2654216 | tf_op jit(solution)/shard_map/ppermute | solution.py:251

commit v6 on v5

--- a/solution.py
+++ b/solution.py
@@ -110,7 +110,8 @@
 
 
 def middle_kernel(
-    grid_ref, xlo_ref, xhi_ref, ylo_ref, yhi_ref, w1_ref, w2t_ref, pairs_ref, padx_ref, padu_ref, shift_ref, pre_ref,
+    scale, core_ref, grid_ref, xlo_ref, xhi_ref, ylo_ref, yhi_ref, w1_ref, w2t_ref,
+    pairs_ref, other_ref, own_ref, padx_ref, padu_ref, shift_ref, pre_ref,
 ):
     fill_pad(padx_ref, grid_ref[0], xlo_ref[0], xhi_ref[0], ylo_ref[0], yhi_ref[0])
     fill_pad(padu_ref, grid_ref[1], xlo_ref[1], xhi_ref[1], ylo_ref[1], yhi_ref[1])
@@ -125,36 +126,20 @@
     sig = jax.nn.sigmoid(pre)
     pairs_ref[1, 0] = (pre * sig * mask).astype(BF).reshape(EX, EY, GZ, C)
     pairs_ref[0, 1] = (back * (sig * (1.0 + pre * (1.0 - sig))) * mask).astype(BF).reshape(EX, EY, GZ, C)
-
-
-def gram_kernel(scale, which_ref, pair_ref, term_ref):
-    del which_ref
-    left = pair_ref[0, 0, 1 : EX - 1, 1 : EY - 1].reshape(ROWS, C)
+    gram(scale, pairs_ref, 1 - core_ref[0], other_ref)
+    gram(scale, pairs_ref, core_ref[0], own_ref)
+
+
+def gram(scale, pairs_ref, which, term_ref):
+    left = pairs_ref[which, 0, 1 : EX - 1, 1 : EY - 1].reshape(ROWS, C)
     lhs = z_shifts(left).T
     for first in range(0, 9, 2):
         ks = range(first, min(first + 2, 9))
         starts = [(2 - k // 3, 2 - k % 3) for k in ks]
-        rhs = [pair_ref[0, 1, x : x + GX, y : y + GY].reshape(ROWS, C) for x, y in starts]
+        rhs = [pairs_ref[which, 1, x : x + GX, y : y + GY].reshape(ROWS, C) for x, y in starts]
         prod = dot(lhs, jnp.concatenate(rhs, axis=1)) * scale
         for n, k in enumerate(ks):
-            term_ref[3 * k * C : 3 * (k + 1) * C, :] = prod[:, n * C : (n + 1) * C].astype(term_ref.dtype)
-
-
-def gram(scale, which, pairs, dtype):
-    spec = pltpu.PrefetchScalarGridSpec(
-        num_scalar_prefetch=1,
-        grid=(1,),
-        in_specs=[pl.BlockSpec((1, 2, EX, EY, GZ, C), lambda i, which_ref: (which_ref[0], 0, 0, 0, 0, 0))],
-        out_specs=pl.BlockSpec((27 * C, C), lambda i, which_ref: (0, 0)),
-    )
-    return pl.pallas_call(
-        lambda *refs: gram_kernel(scale, *refs),
-        grid_spec=spec,
-        out_shape=jax.ShapeDtypeStruct((27 * C, C), dtype),
-        compiler_params=pltpu.CompilerParams(vmem_limit_bytes=56 << 20),
-        interpret=INTERPRET,
-        cost_estimate=pl.CostEstimate(flops=2 * 27 * ROWS * C * C, transcendentals=0, bytes_accessed=9 << 20),
-    )(which.reshape(1), pairs)
+            term_ref[3 * k * C : 3 * (k + 1) * C, :] = prod[:, n * C : (n + 1) * C].astype(BF)
 
 
 def final_kernel(pos_ref, pairs_ref, w2_ref, w1t_ref, out_ref, grad_ref, shift_ref):
@@ -233,19 +218,16 @@
     return swap(jnp.broadcast_to(values, (lax.axis_size(axes), *values.shape)), axes)
 
 
-def reduce_terms(scale, pairs):
-    core = lax.axis_index("core").astype(jnp.int32)
+def reduce_terms(core, own, other):
     cross = [(0, 1), (1, 0)]
-    sent = gram(scale, 1 - core, pairs, BF)
-    got = lax.ppermute(sent, "core", cross)
-    own = gram(scale, core, pairs, F32)
-    share = (own + got.astype(F32)).astype(BF)
+    got = lax.ppermute(other, "core", cross)
+    share = (own.astype(F32) + got.astype(F32)).astype(BF)
     share = scatter_sum(share, YX)
     rows = share.shape[0]
     padded = -(-rows // (8 * lax.axis_size("z_lo"))) * 8 * lax.axis_size("z_lo")
     share = jnp.pad(share, ((0, padded - rows), (0, 0)))
-    share = scatter_sum(share, "z_lo").astype(BF)
-    share = gather(share, "z_hi").astype(F32).sum(axis=0).astype(BF)
+    share = scatter_sum(share, "z_lo")
+    share = gather(share, "z_hi").sum(axis=0).astype(BF)
     share = gather(share, "z_lo").reshape(padded, C)[:rows]
     share = gather(share, YX).reshape(-1, C)
     other = lax.ppermute(share, "core", cross)
@@ -266,12 +248,15 @@
     )
     halo = exchange(faces[:2], faces[2:])
     one_t, two_t = lax.optimization_barrier((transposed(weight_one), transposed(weight_two)))
+    core = lax.axis_index("core").astype(jnp.int32)
     pad = pltpu.VMEM((PX, PY, GZ, C), BF)
-    pairs = call(
-        middle_kernel,
-        jax.ShapeDtypeStruct((2, 2, EX, EY, GZ, C), BF),
+    term = jax.ShapeDtypeStruct((27 * C, C), BF)
+    pairs, other, own = call(
+        lambda *refs: middle_kernel(scale, *refs),
+        (jax.ShapeDtypeStruct((2, 2, EX, EY, GZ, C), BF), term, term),
         scratch=(pad, pad, pltpu.VMEM((PX, PY, GZ, 3 * C), BF), pltpu.VMEM((EXT_ROWS, C), F32)),
-        args=(grid, *halo, weight_one, two_t),
+        smem=1,
+        args=(core.reshape(1), grid, *halo, weight_one, two_t),
     )
     output, input_grad = call(
         final_kernel,
@@ -281,7 +266,7 @@
         args=(block_pos, pairs, weight_two, one_t),
         cost=pl.CostEstimate(flops=2 * 2 * 27 * ROWS * C * C, transcendentals=0, bytes_accessed=24 << 20),
     )
-    grad_one, grad_two = reduce_terms(scale, pairs)
+    grad_one, grad_two = reduce_terms(core, own, other)
     return output, input_grad, grad_one, grad_two
 
 

time: 144 us -> 142 us (0.986)
  Pallas kernels: 26 us -> 21 us
  starting transfers between devices: 25 us -> 27.8 us
  blocking collectives: 74 us -> 75.8 us
  waiting for transfers between devices: 8.05 us -> 6.3 us
    pallas_call x2 -> x0, Pallas kernels: 6.92 us -> none  [gram(): pl.pallas_call(lambda *refs: gram_kernel(scale, *refs), grid_spec=spec, o...]
    ppermute x1, waiting for transfers between devices: 3.85 us -> 0.62 us  [exchange(): x_hi = lax.ppermute(x_faces[0], GXN, backward)]
    ppermute x1, waiting for transfers between devices: 0.01 us -> 2.6 us  [reduce_terms(): got = lax.ppermute(other, 'core', cross)]
    pallas_call x3, Pallas kernels: 19.1 us -> 21 us  [call(): pl.pallas_call(kernel, out_shape=outs, in_specs=specs, out_specs=jax.tree...]
    all_to_all x5, blocking collectives: 74 us -> 75.8 us  [swap(): return lax.all_to_all(values, axes, 0, 0, tiled=True)]
    ppermute x1, starting transfers between devices: 1.92 us -> 3.71 us  [exchange(): y_hi = lax.ppermute(face(0), GYN, backward)]
    ppermute x1, waiting for transfers between devices: 3.25 us -> 1.47 us  [exchange(): y_hi = lax.ppermute(face(0), GYN, backward)]
  transfers between devices with their start and end apart: 6 -> 6, of which waited for: 3 -> 4; matrix products, arithmetic and copies ran while one was open for 3% -> 3% of each run, Pallas kernels for 8% -> 6%
where the time goes in v6:
time: 142 us; the launch traced here: 141 us
  blocking collectives  75.8 us (53%)
  starting transfers between devices  27.8 us (20%)
  Pallas kernels  21 us (15%)
  waiting for transfers between devices  6.3 us (4%)
  other arithmetic  5.53 us (4%)
  local copies, waits for them, and re-layouts  4.13 us (3%)
    all_to_all x5, blocking collectives, swap(): return lax.all_to_all(values, axes, 0, 0, tiled=True)  75.8 us
    pallas_call x3, Pallas kernels, call(): pl.pallas_call(kernel, out_shape=outs, in_specs=specs, out_specs=jax.tree...  21 us
    ppermute x1, starting transfers between devices, reduce_terms(): other = lax.ppermute(share, 'core', cross)  9.39 us
    ppermute x1, starting transfers between devices, exchange(): y_lo = lax.ppermute(face(1), GYN, forward)  6.47 us
    ppermute x1, starting transfers between devices, exchange(): x_lo = lax.ppermute(x_faces[1], GXN, forward)  5 us
    ppermute x1, starting transfers between devices, exchange(): y_hi = lax.ppermute(face(0), GYN, backward)  3.71 us
    reshape x2, local copies, waits for them, and re-layouts, transposed(): return weight.reshape(27, C, C).transpose(0, 2, 1).reshape(27 * C, C)  3.27 us
  transfers between devices with their start and end apart: 6, of which 4 were waited for; matrix products, arithmetic and copies ran while one was open for 3% of the time, Pallas kernels for 6%

profile of v6, /device:TPU:1, one launch (start us, length us, event | category | flops | bytes accessed | tf_op | source)
XLA Modules:
  0.0 141.4 jit_solution(1973033158762856141)
XLA Ops:
  0.6 0.0 copy-start
  0.6 0.0 copy-start.1
  0.7 3.0 %shard_map.84 = (bf16[2,1024,128]{2,1,0:T(8,128)(2,1)}, bf16[2,256,128]{2,1,0:T(8,128)(2,1)}, bf16[2,256,128]{2,1,0:T(8,128)(2,1)}, bf16[2,8,32,128]{3,2,1,0:T(8,128)(2,1)}, bf16[2,8,32,128]{3,2,1,0:T(8,128)(2,1)}) custom-call(s32[8]{0:T(128)} %pos_ref.3, bf16[512,128]{1,0:T(8,128)(2,1)} %feat_ref.1, bf16[512,128]{1,0:T(8,128)(2,1)} %cot_ref.1), custom_call_target="tpu_custom_call" | custom-call | tf_op jit(solution)/shard_map/pallas_call | solution.py:165
  3.7 1.3 collective-permute-start.1
  5.0 5.0 %collective-permute-start = (bf16[2,256,128]{2,1,0:T(8,128)(2,1)}, bf16[2,256,128]{2,1,0:T(8,128)(2,1)S(1)}, u32[]{:S(2)}, u32[]{:S(2)}) collective-permute-start(bf16[2,256,128]{2,1,0:T(8,128)(2,1)} %get-tuple-element.17), channel_id=1, source_target_pairs={{0,4},{4,8},{8,12},{12,16},{16,20},{20,24},{24,28},{28,32},{32,36}... | collective-permute-start | bytes 393224 | tf_op jit(solution)/shard_map/ppermute | solution.py:194
  10.0 0.6 collective-permute-done.1.refs_3_
  10.6 1.6 %collective-permute-done.refs_2_ = bf16[2,256,128]{2,1,0:T(8,128)(2,1)S(1)} collective-permute-done((bf16[2,256,128]{2,1,0:T(8,128)(2,1)}, bf16[2,256,128]{2,1,0:T(8,128)(2,1)S(1)}, u32[]{:S(2)}, u32[]{:S(2)}) %collective-permute-start) | collective-permute-done | bytes 131104 | tf_op jit(solution)/shard_map/ppermute | solution.py:194
  12.2 1.0 pad_maximum_fusion
  13.2 6.5 %collective-permute-start.2 = (bf16[2,12,32,128]{3,2,1,0:T(8,128)(2,1)S(1)}, bf16[2,12,32,128]{3,2,1,0:T(8,128)(2,1)S(1)}, u32[]{:S(2)}, u32[]{:S(2)}) collective-permute-start(bf16[2,12,32,128]{3,2,1,0:T(8,128)(2,1)S(1)} %pad_maximum_fusion), channel_id=1, source_target_pairs={{0,1},{1,2},{2,3},{4,5},{5,6},{6,7},{8,9},{9,10},{10,11},{12,13},{... | collective-permute-start | bytes 589832 | tf_op jit(solution)/shard_map/ppermute | solution.py:203
  19.7 0.9 pad_maximum_fusion.1
  20.6 3.7 %collective-permute-start.3 = (bf16[2,12,32,128]{3,2,1,0:T(8,128)(2,1)S(1)}, bf16[2,12,32,128]{3,2,1,0:T(8,128)(2,1)S(1)}, u32[]{:S(2)}, u32[]{:S(2)}) collective-permute-start(bf16[2,12,32,128]{3,2,1,0:T(8,128)(2,1)S(1)} %pad_maximum_fusion.1), channel_id=1, source_target_pairs={{1,0},{2,1},{3,2},{5,4},{6,5},{7,6},{9,8},{10,9},{11,10},{13,12},{... | collective-permute-start | bytes 589832 | tf_op jit(solution)/shard_map/ppermute | solution.py:204
  24.4 1.6 %copy.11 = bf16[27,128,128]{1,2,0:T(8,128)(2,1)} copy(bf16[27,128,128]{2,1,0:T(8,128)(2,1)S(1)} %bitcast.17) | data formatting | bytes 1769472 | tf_op jit(solution)/shard_map/reshape | solution.py:178
  26.0 1.6 %copy.12 = bf16[27,128,128]{1,2,0:T(8,128)(2,1)} copy(bf16[27,128,128]{2,1,0:T(8,128)(2,1)S(1)} %bitcast.21) | data formatting | bytes 1769472 | tf_op jit(solution)/shard_map/reshape | solution.py:178
  27.6 0.0 collective-permute-done.2.refs_4_
  27.6 0.0 copy-start.4
  27.6 1.5 %collective-permute-done.3.refs_5_ = bf16[2,12,32,128]{3,2,1,0:T(8,128)(2,1)S(1)} collective-permute-done((bf16[2,12,32,128]{3,2,1,0:T(8,128)(2,1)S(1)}, bf16[2,12,32,128]{3,2,1,0:T(8,128)(2,1)S(1)}, u32[]{:S(2)}, u32[]{:S(2)}) %collective-permute-start.3) | collective-permute-done | bytes 196640 | tf_op jit(solution)/shard_map/ppermute | solution.py:204
  29.1 0.7 copy-done.5
  29.8 10.0 %shard_map.85 = (bf16[2,2,10,10,16,128]{5,4,3,2,1,0:T(8,128)(2,1)}, bf16[3456,128]{1,0:T(8,128)(2,1)}, bf16[3456,128]{1,0:T(8,128)(2,1)}) custom-call(s32[1]{0:T(128)} %bitcast.refs_0_, bf16[2,1024,128]{2,1,0:T(8,128)(2,1)} %get-tuple-element.16.refs_1_, bf16[2,256,128]{2,1,0:T(8,128)(2,1)} %copy-done.3, bf16[2,256,128]{2,1,0:T(8,128)(2,1)} %copy-done.2, ...), custom_call_target="tpu_custom_call" | custom-call | tf_op jit(solution)/shard_map/pallas_call | solution.py:165
  39.8 1.9 %collective-permute-start.4 = (bf16[3456,128]{1,0:T(8,128)(2,1)}, bf16[3456,128]{1,0:T(8,128)(2,1)S(1)}, u32[]{:S(2)}, u32[]{:S(2)}) collective-permute-start(bf16[3456,128]{1,0:T(8,128)(2,1)} %get-tuple-element.27), channel_id=1, source_target_pairs={{0,1},{1,0},{2,3},{3,2},{4,5},{5,4},{6,7},{7,6},{8,9},{9,8},{10,11... | collective-permute-start | bytes 2654216 | tf_op jit(solution)/shard_map/ppermute | solution.py:223
  41.7 2.6 %collective-permute-done.4 = bf16[3456,128]{1,0:T(8,128)(2,1)S(1)} collective-permute-done((bf16[3456,128]{1,0:T(8,128)(2,1)}, bf16[3456,128]{1,0:T(8,128)(2,1)S(1)}, u32[]{:S(2)}, u32[]{:S(2)}) %collective-permute-start.4) | collective-permute-done | bytes 884768 | tf_op jit(solution)/shard_map/ppermute | solution.py:223
  44.3 1.4 add_convert_fusion
  45.7 32.7 %all_to_all.25 = bf16[16,216,128]{2,1,0:T(8,128)(2,1)S(1)} all-to-all(bf16[16,216,128]{2,1,0:T(8,128)(2,1)S(1)} %bitcast.19), channel_id=1, replica_groups=mesh['y_lo'=2,'x'=4,'z_hi'=4,'z_lo'=4,'y_hi'=2,'core'=2] {'y_hi','y_lo',..., dimensions={0} | all-to-all | bytes 1769472 | tf_op jit(solution)/shard_map/all_to_all | solution.py:209
  78.4 0.1 convert_reduce_fusion
  78.6 7.1 %all_to_all.26 = f32[4,56,128]{2,1,0:T(8,128)S(1)} all-to-all(f32[4,56,128]{2,1,0:T(8,128)S(1)} %bitcast.23), channel_id=1, replica_groups=mesh['y_lo'=2,'x'=4,'z_hi'=4,'z_lo'=4,'y_hi'=2,'core'=2] {'z_lo'}, dimensions={0} | all-to-all | bytes 229376 | tf_op jit(solution)/shard_map/all_to_all | solution.py:209
  85.7 14.4 %all_to_all.27 = f32[4,56,128]{2,1,0:T(8,128)S(1)} all-to-all(f32[4,56,128]{2,1,0:T(8,128)S(1)} %broadcast_in_dim.9), channel_id=1, replica_groups=mesh['y_lo'=2,'x'=4,'z_hi'=4,'z_lo'=4,'y_hi'=2,'core'=2] {'z_hi'}, dimensions={0} | all-to-all | bytes 229376 | tf_op jit(solution)/shard_map/all_to_all | solution.py:209
  100.2 7.1 %all_to_all.28 = bf16[4,56,128]{2,1,0:T(8,128)(2,1)S(1)} all-to-all(bf16[4,56,128]{2,1,0:T(8,128)(2,1)S(1)} %broadcast_in_dim.10), channel_id=1, replica_groups=mesh['y_lo'=2,'x'=4,'z_hi'=4,'z_lo'=4,'y_hi'=2,'core'=2] {'z_lo'}, dimensions={0} | all-to-all | bytes 114688 | tf_op jit(solution)/shard_map/all_to_all | solution.py:209
  107.3 0.1 broadcast_in_dim.11
  107.4 14.5 %all_to_all.29 = bf16[16,216,128]{2,1,0:T(8,128)(2,1)S(1)} all-to-all(bf16[16,216,128]{2,1,0:T(8,128)(2,1)S(1)} %broadcast_in_dim.11), channel_id=1, replica_groups=mesh['y_lo'=2,'x'=4,'z_hi'=4,'z_lo'=4,'y_hi'=2,'core'=2] {'y_hi','y_lo',..., dimensions={0} | all-to-all | bytes 1769472 | tf_op jit(solution)/shard_map/all_to_all | solution.py:209
  121.9 9.4 %collective-permute-start.5 = (bf16[3456,128]{1,0:T(8,128)(2,1)S(1)}, bf16[3456,128]{1,0:T(8,128)(2,1)S(1)}, u32[]{:S(2)}, u32[]{:S(2)}) collective-permute-start(bf16[3456,128]{1,0:T(8,128)(2,1)S(1)} %bitcast.20), channel_id=1, source_target_pairs={{0,1},{1,0},{2,3},{3,2},{4,5},{5,4},{6,7},{7,6},{8,9},{9,8},{10,11... | collective-permute-start | bytes 2654216 | tf_op jit(solution)/shard_map/ppermute | solution.py:233
  131.3 8.0 %shard_map.86 = (bf16[512,128]{1,0:T(8,128)(2,1)}, f32[512,128]{1,0:T(8,128)}) custom-call(s32[8]{0:T(128)} %pos_ref.3, bf16[2,2,10,10,16,128]{5,4,3,2,1,0:T(8,128)(2,1)} %get-tuple-element.22.pairs_ref, bf16[3456,128]{1,0:T(8,128)(2,1)} %w2_ref.1, bf16[3456,128]{1,0:T(8,128)(2,1)} %bitcast.22), custom_call_target="tpu_custom_call" | custom-call | flops 1811939328 | bytes 25165824 | tf_op jit(solution)/shard_map/pallas_call | solution.py:165
  139.3 0.0 collective-permute-done.5
  139.3 2.1 %select_convert_fusion = (f32[3456,128]{1,0:T(8,128)}, f32[3456,128]{1,0:T(8,128)}) fusion(bf16[3456,128]{1,0:T(8,128)(2,1)S(1)} %collective-permute-done.5, pred[]{:T(512)S(6)} %eq.3, bf16[16,216,128]{2,1,0:T(8,128)(2,1)S(1)} %all_to_all.29), kind=kLoop, calls=%fused_computation.2 | loop fusion | flops 1769472 | bytes 5308417 | tf_op jit(solution)/shard_map/convert_element_type | solution.py:235
  (16 shorter events, 0.1 us)
Async XLA Ops:
  0.6 23.7 %copy-start = (bf16[3456,128]{1,0:T(8,128)(2,1)S(1)}, bf16[3456,128]{1,0:T(8,128)(2,1)}, u32[]{:S(2)}) copy-start(bf16[3456,128]{1,0:T(8,128)(2,1)} %refs_6_.1) | copy-start | bytes 2654212
  0.6 25.4 %copy-start.1 = (bf16[3456,128]{1,0:T(8,128)(2,1)S(1)}, bf16[3456,128]{1,0:T(8,128)(2,1)}, u32[]{:S(2)}) copy-start(bf16[3456,128]{1,0:T(8,128)(2,1)} %w2_ref.1) | copy-start | bytes 2654212
  3.7 6.9 %collective-permute-start.1 = (bf16[2,256,128]{2,1,0:T(8,128)(2,1)}, bf16[2,256,128]{2,1,0:T(8,128)(2,1)S(1)}, u32[]{:S(2)}, u32[]{:S(2)}) collective-permute-start(bf16[2,256,128]{2,1,0:T(8,128)(2,1)} %get-tuple-element.18), channel_id=1, source_target_pairs={{4,0},{8,4},{12,8},{16,12},{20,16},{24,20},{28,24},{32,28},{36,32}... | collective-permute-start | bytes 393224 | tf_op jit(solution)/shard_map/ppermute | solution.py:195
  5.0 7.2 %collective-permute-start = (bf16[2,256,128]{2,1,0:T(8,128)(2,1)}, bf16[2,256,128]{2,1,0:T(8,128)(2,1)S(1)}, u32[]{:S(2)}, u32[]{:S(2)}) collective-permute-start(bf16[2,256,128]{2,1,0:T(8,128)(2,1)} %get-tuple-element.17), channel_id=1, source_target_pairs={{0,4},{4,8},{8,12},{12,16},{16,20},{20,24},{24,28},{28,32},{32,36}... | collective-permute-start | bytes 393224 | tf_op jit(solution)/shard_map/ppermute | solution.py:194
  10.6 17.0 %copy-start.2 = (bf16[2,256,128]{2,1,0:T(8,128)(2,1)}, bf16[2,256,128]{2,1,0:T(8,128)(2,1)S(1)}, u32[]{:S(2)}) copy-start(bf16[2,256,128]{2,1,0:T(8,128)(2,1)S(1)} %collective-permute-done.1.refs_3_) | copy-start | bytes 393220
  12.2 15.4 %copy-start.3 = (bf16[2,256,128]{2,1,0:T(8,128)(2,1)}, bf16[2,256,128]{2,1,0:T(8,128)(2,1)S(1)}, u32[]{:S(2)}) copy-start(bf16[2,256,128]{2,1,0:T(8,128)(2,1)S(1)} %collective-permute-done.refs_2_) | copy-start | bytes 393220
  13.2 14.4 %collective-permute-start.2 = (bf16[2,12,32,128]{3,2,1,0:T(8,128)(2,1)S(1)}, bf16[2,12,32,128]{3,2,1,0:T(8,128)(2,1)S(1)}, u32[]{:S(2)}, u32[]{:S(2)}) collective-permute-start(bf16[2,12,32,128]{3,2,1,0:T(8,128)(2,1)S(1)} %pad_maximum_fusion), channel_id=1, source_target_pairs={{0,1},{1,2},{2,3},{4,5},{5,6},{6,7},{8,9},{9,10},{10,11},{12,13},{... | collective-permute-start | bytes 589832 | tf_op jit(solution)/shard_map/ppermute | solution.py:203
  20.6 8.5 %collective-permute-start.3 = (bf16[2,12,32,128]{3,2,1,0:T(8,128)(2,1)S(1)}, bf16[2,12,32,128]{3,2,1,0:T(8,128)(2,1)S(1)}, u32[]{:S(2)}, u32[]{:S(2)}) collective-permute-start(bf16[2,12,32,128]{3,2,1,0:T(8,128)(2,1)S(1)} %pad_maximum_fusion.1), channel_id=1, source_target_pairs={{1,0},{2,1},{3,2},{5,4},{6,5},{7,6},{9,8},{10,9},{11,10},{13,12},{... | collective-permute-start | bytes 589832 | tf_op jit(solution)/shard_map/ppermute | solution.py:204
  27.6 1.5 %copy-start.4 = (bf16[2,12,32,128]{3,2,1,0:T(8,128)(2,1)}, bf16[2,12,32,128]{3,2,1,0:T(8,128)(2,1)S(1)}, u32[]{:S(2)}) copy-start(bf16[2,12,32,128]{3,2,1,0:T(8,128)(2,1)S(1)} %collective-permute-done.2.refs_4_) | copy-start | bytes 589828
  29.1 0.7 copy-start.5
  39.8 4.5 %collective-permute-start.4 = (bf16[3456,128]{1,0:T(8,128)(2,1)}, bf16[3456,128]{1,0:T(8,128)(2,1)S(1)}, u32[]{:S(2)}, u32[]{:S(2)}) collective-permute-start(bf16[3456,128]{1,0:T(8,128)(2,1)} %get-tuple-element.27), channel_id=1, source_target_pairs={{0,1},{1,0},{2,3},{3,2},{4,5},{5,4},{6,7},{7,6},{8,9},{9,8},{10,11... | collective-permute-start | bytes 2654216 | tf_op jit(solution)/shard_map/ppermute | solution.py:223
  121.9 17.4 %collective-permute-start.5 = (bf16[3456,128]{1,0:T(8,128)(2,1)S(1)}, bf16[3456,128]{1,0:T(8,128)(2,1)S(1)}, u32[]{:S(2)}, u32[]{:S(2)}) collective-permute-start(bf16[3456,128]{1,0:T(8,128)(2,1)S(1)} %bitcast.20), channel_id=1, source_target_pairs={{0,1},{1,0},{2,3},{3,2},{4,5},{5,4},{6,7},{7,6},{8,9},{9,8},{10,11... | collective-permute-start | bytes 2654216 | tf_op jit(solution)/shard_map/ppermute | solution.py:233

commit v7 on v6

--- a/solution.py
+++ b/solution.py
@@ -110,24 +110,40 @@
 
 
 def middle_kernel(
-    scale, core_ref, grid_ref, xlo_ref, xhi_ref, ylo_ref, yhi_ref, w1_ref, w2t_ref,
-    pairs_ref, other_ref, own_ref, padx_ref, padu_ref, shift_ref, pre_ref,
+    scale, core_ref, grid_ref, xlo_ref, xhi_ref, ylo_ref, yhi_ref, w1_any, w2t_any,
+    pairs_any, other_any, own_any,
+    padx_ref, padu_ref, shift_ref, pre_ref, w1_ref, w2t_ref, pairs_ref, other_ref, own_ref, sems,
 ):
+    first_in = pltpu.make_async_copy(w1_any, w1_ref, sems.at[0])
+    second_in = pltpu.make_async_copy(w2t_any, w2t_ref, sems.at[1])
+    first_in.start()
+    second_in.start()
     fill_pad(padx_ref, grid_ref[0], xlo_ref[0], xhi_ref[0], ylo_ref[0], yhi_ref[0])
     fill_pad(padu_ref, grid_ref[1], xlo_ref[1], xhi_ref[1], ylo_ref[1], yhi_ref[1])
     pairs_ref[0, 0] = padx_ref[1 : PX - 1, 1 : PY - 1]
     pairs_ref[1, 1] = padu_ref[1 : PX - 1, 1 : PY - 1]
     shift_ref[...] = z_shifts(padx_ref[...].reshape(PAD_ROWS, C)).reshape(PX, PY, GZ, 3 * C)
+    first_in.wait()
     pre_ref[...] = conv(shift_ref, w1_ref, False).reshape(EXT_ROWS, C)
     shift_ref[...] = z_shifts(padu_ref[...].reshape(PAD_ROWS, C), True).reshape(PX, PY, GZ, 3 * C)
+    second_in.wait()
     back = conv(shift_ref, w2t_ref, True).reshape(EXT_ROWS, C)
     pre = pre_ref[...]
     mask = active_rows(padx_ref[1 : PX - 1, 1 : PY - 1].astype(F32)).reshape(EXT_ROWS, C)
     sig = jax.nn.sigmoid(pre)
     pairs_ref[1, 0] = (pre * sig * mask).astype(BF).reshape(EX, EY, GZ, C)
     pairs_ref[0, 1] = (back * (sig * (1.0 + pre * (1.0 - sig))) * mask).astype(BF).reshape(EX, EY, GZ, C)
+    pairs_out = pltpu.make_async_copy(pairs_ref, pairs_any, sems.at[2])
+    pairs_out.start()
     gram(scale, pairs_ref, 1 - core_ref[0], other_ref)
+    other_out = pltpu.make_async_copy(other_ref, other_any, sems.at[3])
+    other_out.start()
     gram(scale, pairs_ref, core_ref[0], own_ref)
+    own_out = pltpu.make_async_copy(own_ref, own_any, sems.at[4])
+    own_out.start()
+    pairs_out.wait()
+    other_out.wait()
+    own_out.wait()
 
 
 def gram(scale, pairs_ref, which, term_ref):
@@ -159,14 +175,16 @@
             grad_ref[...] = dot(perm, high) + dot(perm, low)
 
 
-def call(kernel, outs, scratch=(), smem=0, args=(), cost=None):
+def call(kernel, outs, scratch=(), smem=0, args=(), cost=None, manual=0):
     specs = [pl.BlockSpec(memory_space=pltpu.SMEM)] * smem
-    specs += [pl.BlockSpec(memory_space=pltpu.VMEM)] * (len(args) - smem)
+    specs += [pl.BlockSpec(memory_space=pltpu.VMEM)] * (len(args) - smem - manual)
+    specs += [pl.BlockSpec(memory_space=pl.ANY)] * manual
+    out_space = pl.ANY if manual else pltpu.VMEM
     return pl.pallas_call(
         kernel,
         out_shape=outs,
         in_specs=specs,
-        out_specs=jax.tree.map(lambda _: pl.BlockSpec(memory_space=pltpu.VMEM), outs),
+        out_specs=jax.tree.map(lambda _: pl.BlockSpec(memory_space=out_space), outs),
         scratch_shapes=list(scratch),
         compiler_params=pltpu.CompilerParams(vmem_limit_bytes=56 << 20),
         interpret=INTERPRET,
@@ -251,11 +269,16 @@
     core = lax.axis_index("core").astype(jnp.int32)
     pad = pltpu.VMEM((PX, PY, GZ, C), BF)
     term = jax.ShapeDtypeStruct((27 * C, C), BF)
+    block = pltpu.VMEM((27 * C, C), BF)
     pairs, other, own = call(
         lambda *refs: middle_kernel(scale, *refs),
         (jax.ShapeDtypeStruct((2, 2, EX, EY, GZ, C), BF), term, term),
-        scratch=(pad, pad, pltpu.VMEM((PX, PY, GZ, 3 * C), BF), pltpu.VMEM((EXT_ROWS, C), F32)),
+        scratch=(
+            pad, pad, pltpu.VMEM((PX, PY, GZ, 3 * C), BF), pltpu.VMEM((EXT_ROWS, C), F32),
+            block, block, pltpu.VMEM((2, 2, EX, EY, GZ, C), BF), block, block, pltpu.SemaphoreType.DMA((5,)),
+        ),
         smem=1,
+        manual=2,
         args=(core.reshape(1), grid, *halo, weight_one, two_t),
     )
     output, input_grad = call(

time: 142 us -> 143 us (level)
  no operation moved by 1% of the time
where the time goes in v7:
time: 143 us; the launch traced here: 142 us
  blocking collectives  75.8 us (53%)
  starting transfers between devices  27.7 us (19%)
  Pallas kernels  21.7 us (15%)
  waiting for transfers between devices  6.3 us (4%)
  other arithmetic  5.53 us (4%)
  local copies, waits for them, and re-layouts  4.13 us (3%)
    all_to_all x5, blocking collectives, swap(): return lax.all_to_all(values, axes, 0, 0, tiled=True)  75.8 us
    pallas_call x3, Pallas kernels, call(): pl.pallas_call(kernel, out_shape=outs, in_specs=specs, out_specs=jax.tree...  21.7 us
    ppermute x1, starting transfers between devices, reduce_terms(): other = lax.ppermute(share, 'core', cross)  9.31 us
    ppermute x1, starting transfers between devices, exchange(): y_lo = lax.ppermute(face(1), GYN, forward)  6.47 us
    ppermute x1, starting transfers between devices, exchange(): x_lo = lax.ppermute(x_faces[1], GXN, forward)  5 us
    ppermute x1, starting transfers between devices, exchange(): y_hi = lax.ppermute(face(0), GYN, backward)  3.71 us
    reshape x2, local copies, waits for them, and re-layouts, transposed(): return weight.reshape(27, C, C).transpose(0, 2, 1).reshape(27 * C, C)  3.27 us
  transfers between devices with their start and end apart: 6, of which 4 were waited for; matrix products, arithmetic and copies ran while one was open for 3% of the time, Pallas kernels for 6%

profile of v7, /device:TPU:1, one launch (start us, length us, event | category | flops | bytes accessed | tf_op | source)
XLA Modules:
  0.0 142.0 jit_solution(10041016743551722871)
XLA Ops:
  0.6 0.0 copy-start
  0.6 0.0 copy-start.1
  0.7 3.0 %shard_map.84 = (bf16[2,1024,128]{2,1,0:T(8,128)(2,1)}, bf16[2,256,128]{2,1,0:T(8,128)(2,1)}, bf16[2,256,128]{2,1,0:T(8,128)(2,1)}, bf16[2,8,32,128]{3,2,1,0:T(8,128)(2,1)}, bf16[2,8,32,128]{3,2,1,0:T(8,128)(2,1)}) custom-call(s32[8]{0:T(128)} %pos_ref.3, bf16[512,128]{1,0:T(8,128)(2,1)} %feat_ref.1, bf16[512,128]{1,0:T(8,128)(2,1)} %cot_ref.1), custom_call_target="tpu_custom_call" | custom-call | tf_op jit(solution)/shard_map/pallas_call | solution.py:183
  3.7 1.3 collective-permute-start.1
  5.0 5.0 %collective-permute-start = (bf16[2,256,128]{2,1,0:T(8,128)(2,1)}, bf16[2,256,128]{2,1,0:T(8,128)(2,1)S(1)}, u32[]{:S(2)}, u32[]{:S(2)}) collective-permute-start(bf16[2,256,128]{2,1,0:T(8,128)(2,1)} %get-tuple-element.17), channel_id=1, source_target_pairs={{0,4},{4,8},{8,12},{12,16},{16,20},{20,24},{24,28},{28,32},{32,36}... | collective-permute-start | bytes 393224 | tf_op jit(solution)/shard_map/ppermute | solution.py:212
  10.0 0.6 collective-permute-done.1.refs_3_
  10.6 1.6 %collective-permute-done.refs_2_ = bf16[2,256,128]{2,1,0:T(8,128)(2,1)S(1)} collective-permute-done((bf16[2,256,128]{2,1,0:T(8,128)(2,1)}, bf16[2,256,128]{2,1,0:T(8,128)(2,1)S(1)}, u32[]{:S(2)}, u32[]{:S(2)}) %collective-permute-start) | collective-permute-done | bytes 131104 | tf_op jit(solution)/shard_map/ppermute | solution.py:212
  12.2 1.0 pad_maximum_fusion
  13.2 6.5 %collective-permute-start.2 = (bf16[2,12,32,128]{3,2,1,0:T(8,128)(2,1)S(1)}, bf16[2,12,32,128]{3,2,1,0:T(8,128)(2,1)S(1)}, u32[]{:S(2)}, u32[]{:S(2)}) collective-permute-start(bf16[2,12,32,128]{3,2,1,0:T(8,128)(2,1)S(1)} %pad_maximum_fusion), channel_id=1, source_target_pairs={{0,1},{1,2},{2,3},{4,5},{5,6},{6,7},{8,9},{9,10},{10,11},{12,13},{... | collective-permute-start | bytes 589832 | tf_op jit(solution)/shard_map/ppermute | solution.py:221
  19.7 0.9 pad_maximum_fusion.1
  20.6 3.7 %collective-permute-start.3 = (bf16[2,12,32,128]{3,2,1,0:T(8,128)(2,1)S(1)}, bf16[2,12,32,128]{3,2,1,0:T(8,128)(2,1)S(1)}, u32[]{:S(2)}, u32[]{:S(2)}) collective-permute-start(bf16[2,12,32,128]{3,2,1,0:T(8,128)(2,1)S(1)} %pad_maximum_fusion.1), channel_id=1, source_target_pairs={{1,0},{2,1},{3,2},{5,4},{6,5},{7,6},{9,8},{10,9},{11,10},{13,12},{... | collective-permute-start | bytes 589832 | tf_op jit(solution)/shard_map/ppermute | solution.py:222
  24.4 1.6 %copy.11 = bf16[27,128,128]{1,2,0:T(8,128)(2,1)} copy(bf16[27,128,128]{2,1,0:T(8,128)(2,1)S(1)} %bitcast.17) | data formatting | bytes 1769472 | tf_op jit(solution)/shard_map/reshape | solution.py:196
  26.0 1.6 %copy.12 = bf16[27,128,128]{1,2,0:T(8,128)(2,1)} copy(bf16[27,128,128]{2,1,0:T(8,128)(2,1)S(1)} %bitcast.21) | data formatting | bytes 1769472 | tf_op jit(solution)/shard_map/reshape | solution.py:196
  27.6 0.0 collective-permute-done.2.refs_4_
  27.6 0.0 copy-start.4
  27.6 1.5 %collective-permute-done.3.refs_5_ = bf16[2,12,32,128]{3,2,1,0:T(8,128)(2,1)S(1)} collective-permute-done((bf16[2,12,32,128]{3,2,1,0:T(8,128)(2,1)S(1)}, bf16[2,12,32,128]{3,2,1,0:T(8,128)(2,1)S(1)}, u32[]{:S(2)}, u32[]{:S(2)}) %collective-permute-start.3) | collective-permute-done | bytes 196640 | tf_op jit(solution)/shard_map/ppermute | solution.py:222
  29.1 0.7 copy-done.5
  29.8 10.7 %shard_map.85 = (bf16[2,2,10,10,16,128]{5,4,3,2,1,0:T(8,128)(2,1)}, bf16[3456,128]{1,0:T(8,128)(2,1)}, bf16[3456,128]{1,0:T(8,128)(2,1)}) custom-call(s32[1]{0:T(128)} %bitcast.refs_0_, bf16[2,1024,128]{2,1,0:T(8,128)(2,1)} %get-tuple-element.16.refs_1_, bf16[2,256,128]{2,1,0:T(8,128)(2,1)} %copy-done.3, bf16[2,256,128]{2,1,0:T(8,128)(2,1)} %copy-done.2, ...), custom_call_target="tpu_custom_call" | custom-call | tf_op jit(solution)/shard_map/pallas_call | solution.py:183
  40.5 1.9 %collective-permute-start.4 = (bf16[3456,128]{1,0:T(8,128)(2,1)}, bf16[3456,128]{1,0:T(8,128)(2,1)S(1)}, u32[]{:S(2)}, u32[]{:S(2)}) collective-permute-start(bf16[3456,128]{1,0:T(8,128)(2,1)} %get-tuple-element.27), channel_id=1, source_target_pairs={{0,1},{1,0},{2,3},{3,2},{4,5},{5,4},{6,7},{7,6},{8,9},{9,8},{10,11... | collective-permute-start | bytes 2654216 | tf_op jit(solution)/shard_map/ppermute | solution.py:241
  42.4 2.6 %collective-permute-done.4 = bf16[3456,128]{1,0:T(8,128)(2,1)S(1)} collective-permute-done((bf16[3456,128]{1,0:T(8,128)(2,1)}, bf16[3456,128]{1,0:T(8,128)(2,1)S(1)}, u32[]{:S(2)}, u32[]{:S(2)}) %collective-permute-start.4) | collective-permute-done | bytes 884768 | tf_op jit(solution)/shard_map/ppermute | solution.py:241
  45.0 1.4 add_convert_fusion
  46.4 32.7 %all_to_all.25 = bf16[16,216,128]{2,1,0:T(8,128)(2,1)S(1)} all-to-all(bf16[16,216,128]{2,1,0:T(8,128)(2,1)S(1)} %bitcast.19), channel_id=1, replica_groups=mesh['y_lo'=2,'x'=4,'z_hi'=4,'z_lo'=4,'y_hi'=2,'core'=2] {'y_hi','y_lo',..., dimensions={0} | all-to-all | bytes 1769472 | tf_op jit(solution)/shard_map/all_to_all | solution.py:227
  79.1 0.1 convert_reduce_fusion
  79.3 7.1 %all_to_all.26 = f32[4,56,128]{2,1,0:T(8,128)S(1)} all-to-all(f32[4,56,128]{2,1,0:T(8,128)S(1)} %bitcast.23), channel_id=1, replica_groups=mesh['y_lo'=2,'x'=4,'z_hi'=4,'z_lo'=4,'y_hi'=2,'core'=2] {'z_lo'}, dimensions={0} | all-to-all | bytes 229376 | tf_op jit(solution)/shard_map/all_to_all | solution.py:227
  86.4 14.4 %all_to_all.27 = f32[4,56,128]{2,1,0:T(8,128)S(1)} all-to-all(f32[4,56,128]{2,1,0:T(8,128)S(1)} %broadcast_in_dim.9), channel_id=1, replica_groups=mesh['y_lo'=2,'x'=4,'z_hi'=4,'z_lo'=4,'y_hi'=2,'core'=2] {'z_hi'}, dimensions={0} | all-to-all | bytes 229376 | tf_op jit(solution)/shard_map/all_to_all | solution.py:227
  100.9 7.1 %all_to_all.28 = bf16[4,56,128]{2,1,0:T(8,128)(2,1)S(1)} all-to-all(bf16[4,56,128]{2,1,0:T(8,128)(2,1)S(1)} %broadcast_in_dim.10), channel_id=1, replica_groups=mesh['y_lo'=2,'x'=4,'z_hi'=4,'z_lo'=4,'y_hi'=2,'core'=2] {'z_lo'}, dimensions={0} | all-to-all | bytes 114688 | tf_op jit(solution)/shard_map/all_to_all | solution.py:227
  108.0 0.1 broadcast_in_dim.11
  108.1 14.5 %all_to_all.29 = bf16[16,216,128]{2,1,0:T(8,128)(2,1)S(1)} all-to-all(bf16[16,216,128]{2,1,0:T(8,128)(2,1)S(1)} %broadcast_in_dim.11), channel_id=1, replica_groups=mesh['y_lo'=2,'x'=4,'z_hi'=4,'z_lo'=4,'y_hi'=2,'core'=2] {'y_hi','y_lo',..., dimensions={0} | all-to-all | bytes 1769472 | tf_op jit(solution)/shard_map/all_to_all | solution.py:227
  122.6 9.3 %collective-permute-start.5 = (bf16[3456,128]{1,0:T(8,128)(2,1)S(1)}, bf16[3456,128]{1,0:T(8,128)(2,1)S(1)}, u32[]{:S(2)}, u32[]{:S(2)}) collective-permute-start(bf16[3456,128]{1,0:T(8,128)(2,1)S(1)} %bitcast.20), channel_id=1, source_target_pairs={{0,1},{1,0},{2,3},{3,2},{4,5},{5,4},{6,7},{7,6},{8,9},{9,8},{10,11... | collective-permute-start | bytes 2654216 | tf_op jit(solution)/shard_map/ppermute | solution.py:251
  131.9 8.0 %shard_map.86 = (bf16[512,128]{1,0:T(8,128)(2,1)}, f32[512,128]{1,0:T(8,128)}) custom-call(s32[8]{0:T(128)} %pos_ref.3, bf16[2,2,10,10,16,128]{5,4,3,2,1,0:T(8,128)(2,1)} %get-tuple-element.22.pairs_ref, bf16[3456,128]{1,0:T(8,128)(2,1)} %w2_ref.1, bf16[3456,128]{1,0:T(8,128)(2,1)} %bitcast.22), custom_call_target="tpu_custom_call" | custom-call | flops 1811939328 | bytes 25165824 | tf_op jit(solution)/shard_map/pallas_call | solution.py:183
  139.9 0.0 collective-permute-done.5
  139.9 2.1 %select_convert_fusion = (f32[3456,128]{1,0:T(8,128)}, f32[3456,128]{1,0:T(8,128)}) fusion(bf16[3456,128]{1,0:T(8,128)(2,1)S(1)} %collective-permute-done.5, pred[]{:T(512)S(6)} %eq.3, bf16[16,216,128]{2,1,0:T(8,128)(2,1)S(1)} %all_to_all.29), kind=kLoop, calls=%fused_computation.2 | loop fusion | flops 1769472 | bytes 5308417 | tf_op jit(solution)/shard_map/convert_element_type | solution.py:253
  (16 shorter events, 0.1 us)
Async XLA Ops:
  0.6 23.7 %copy-start = (bf16[3456,128]{1,0:T(8,128)(2,1)S(1)}, bf16[3456,128]{1,0:T(8,128)(2,1)}, u32[]{:S(2)}) copy-start(bf16[3456,128]{1,0:T(8,128)(2,1)} %refs_6_.1) | copy-start | bytes 2654212
  0.6 25.4 %copy-start.1 = (bf16[3456,128]{1,0:T(8,128)(2,1)S(1)}, bf16[3456,128]{1,0:T(8,128)(2,1)}, u32[]{:S(2)}) copy-start(bf16[3456,128]{1,0:T(8,128)(2,1)} %w2_ref.1) | copy-start | bytes 2654212
  3.7 6.9 %collective-permute-start.1 = (bf16[2,256,128]{2,1,0:T(8,128)(2,1)}, bf16[2,256,128]{2,1,0:T(8,128)(2,1)S(1)}, u32[]{:S(2)}, u32[]{:S(2)}) collective-permute-start(bf16[2,256,128]{2,1,0:T(8,128)(2,1)} %get-tuple-element.18), channel_id=1, source_target_pairs={{4,0},{8,4},{12,8},{16,12},{20,16},{24,20},{28,24},{32,28},{36,32}... | collective-permute-start | bytes 393224 | tf_op jit(solution)/shard_map/ppermute | solution.py:213
  5.0 7.2 %collective-permute-start = (bf16[2,256,128]{2,1,0:T(8,128)(2,1)}, bf16[2,256,128]{2,1,0:T(8,128)(2,1)S(1)}, u32[]{:S(2)}, u32[]{:S(2)}) collective-permute-start(bf16[2,256,128]{2,1,0:T(8,128)(2,1)} %get-tuple-element.17), channel_id=1, source_target_pairs={{0,4},{4,8},{8,12},{12,16},{16,20},{20,24},{24,28},{28,32},{32,36}... | collective-permute-start | bytes 393224 | tf_op jit(solution)/shard_map/ppermute | solution.py:212
  10.6 17.0 %copy-start.2 = (bf16[2,256,128]{2,1,0:T(8,128)(2,1)}, bf16[2,256,128]{2,1,0:T(8,128)(2,1)S(1)}, u32[]{:S(2)}) copy-start(bf16[2,256,128]{2,1,0:T(8,128)(2,1)S(1)} %collective-permute-done.1.refs_3_) | copy-start | bytes 393220
  12.2 15.4 %copy-start.3 = (bf16[2,256,128]{2,1,0:T(8,128)(2,1)}, bf16[2,256,128]{2,1,0:T(8,128)(2,1)S(1)}, u32[]{:S(2)}) copy-start(bf16[2,256,128]{2,1,0:T(8,128)(2,1)S(1)} %collective-permute-done.refs_2_) | copy-start | bytes 393220
  13.2 14.4 %collective-permute-start.2 = (bf16[2,12,32,128]{3,2,1,0:T(8,128)(2,1)S(1)}, bf16[2,12,32,128]{3,2,1,0:T(8,128)(2,1)S(1)}, u32[]{:S(2)}, u32[]{:S(2)}) collective-permute-start(bf16[2,12,32,128]{3,2,1,0:T(8,128)(2,1)S(1)} %pad_maximum_fusion), channel_id=1, source_target_pairs={{0,1},{1,2},{2,3},{4,5},{5,6},{6,7},{8,9},{9,10},{10,11},{12,13},{... | collective-permute-start | bytes 589832 | tf_op jit(solution)/shard_map/ppermute | solution.py:221
  20.6 8.5 %collective-permute-start.3 = (bf16[2,12,32,128]{3,2,1,0:T(8,128)(2,1)S(1)}, bf16[2,12,32,128]{3,2,1,0:T(8,128)(2,1)S(1)}, u32[]{:S(2)}, u32[]{:S(2)}) collective-permute-start(bf16[2,12,32,128]{3,2,1,0:T(8,128)(2,1)S(1)} %pad_maximum_fusion.1), channel_id=1, source_target_pairs={{1,0},{2,1},{3,2},{5,4},{6,5},{7,6},{9,8},{10,9},{11,10},{13,12},{... | collective-permute-start | bytes 589832 | tf_op jit(solution)/shard_map/ppermute | solution.py:222
  27.6 1.5 %copy-start.4 = (bf16[2,12,32,128]{3,2,1,0:T(8,128)(2,1)}, bf16[2,12,32,128]{3,2,1,0:T(8,128)(2,1)S(1)}, u32[]{:S(2)}) copy-start(bf16[2,12,32,128]{3,2,1,0:T(8,128)(2,1)S(1)} %collective-permute-done.2.refs_4_) | copy-start | bytes 589828
  29.1 0.7 copy-start.5
  40.5 4.5 %collective-permute-start.4 = (bf16[3456,128]{1,0:T(8,128)(2,1)}, bf16[3456,128]{1,0:T(8,128)(2,1)S(1)}, u32[]{:S(2)}, u32[]{:S(2)}) collective-permute-start(bf16[3456,128]{1,0:T(8,128)(2,1)} %get-tuple-element.27), channel_id=1, source_target_pairs={{0,1},{1,0},{2,3},{3,2},{4,5},{5,4},{6,7},{7,6},{8,9},{9,8},{10,11... | collective-permute-start | bytes 2654216 | tf_op jit(solution)/shard_map/ppermute | solution.py:241
  122.6 17.3 %collective-permute-start.5 = (bf16[3456,128]{1,0:T(8,128)(2,1)S(1)}, bf16[3456,128]{1,0:T(8,128)(2,1)S(1)}, u32[]{:S(2)}, u32[]{:S(2)}) collective-permute-start(bf16[3456,128]{1,0:T(8,128)(2,1)S(1)} %bitcast.20), channel_id=1, source_target_pairs={{0,1},{1,0},{2,3},{3,2},{4,5},{5,4},{6,7},{7,6},{8,9},{9,8},{10,11... | collective-permute-start | bytes 2654216 | tf_op jit(solution)/shard_map/ppermute | solution.py:251

commit v8 on v6

--- a/solution.py
+++ b/solution.py
@@ -187,6 +187,7 @@
 GXN = ("y_lo", "x", "z_hi", "z_lo")
 GYN = ("y_hi", "core")
 YX = ("y_hi", "y_lo", "x")
+Z = ("z_hi", "z_lo")
 
 
 def exchange(x_faces, y_faces):
@@ -224,11 +225,10 @@
     share = (own.astype(F32) + got.astype(F32)).astype(BF)
     share = scatter_sum(share, YX)
     rows = share.shape[0]
-    padded = -(-rows // (8 * lax.axis_size("z_lo"))) * 8 * lax.axis_size("z_lo")
-    share = jnp.pad(share, ((0, padded - rows), (0, 0)))
-    share = scatter_sum(share, "z_lo")
-    share = gather(share, "z_hi").sum(axis=0).astype(BF)
-    share = gather(share, "z_lo").reshape(padded, C)[:rows]
+    padded = -(-rows // (8 * lax.axis_size(Z))) * 8 * lax.axis_size(Z)
+    share = jnp.pad(share, ((0, padded - rows), (0, 0))).astype(BF)
+    share = scatter_sum(share, Z).astype(BF)
+    share = gather(share, Z).reshape(padded, C)[:rows]
     share = gather(share, YX).reshape(-1, C)
     other = lax.ppermute(share, "core", cross)
     first = core == 0

time: 142 us -> 140 us (0.986)
  starting transfers between devices: 27.8 us -> 24.9 us
    ppermute x1, starting transfers between devices: 9.39 us -> 6.59 us  [reduce_terms(): other = lax.ppermute(share, 'core', cross)]
    all_to_all x5 -> x4, blocking collectives: 75.8 us -> 76.4 us  [swap(): return lax.all_to_all(values, axes, 0, 0, tiled=True)]
where the time goes in v8:
time: 140 us; the launch traced here: 139 us
  blocking collectives  76.4 us (55%)
  starting transfers between devices  24.9 us (18%)
  Pallas kernels  21 us (15%)
  waiting for transfers between devices  6.3 us (4%)
  other arithmetic  5.53 us (4%)
  local copies, waits for them, and re-layouts  4.12 us (3%)
    all_to_all x4, blocking collectives, swap(): return lax.all_to_all(values, axes, 0, 0, tiled=True)  76.4 us
    pallas_call x3, Pallas kernels, call(): pl.pallas_call(kernel, out_shape=outs, in_specs=specs, out_specs=jax.tree...  21 us
    ppermute x1, starting transfers between devices, reduce_terms(): other = lax.ppermute(share, 'core', cross)  6.59 us
    ppermute x1, starting transfers between devices, exchange(): y_lo = lax.ppermute(face(1), GYN, forward)  6.47 us
    ppermute x1, starting transfers between devices, exchange(): x_lo = lax.ppermute(x_faces[1], GXN, forward)  5 us
    ppermute x1, starting transfers between devices, exchange(): y_hi = lax.ppermute(face(0), GYN, backward)  3.71 us
    reshape x2, local copies, waits for them, and re-layouts, transposed(): return weight.reshape(27, C, C).transpose(0, 2, 1).reshape(27 * C, C)  3.27 us
  transfers between devices with their start and end apart: 6, of which 4 were waited for; matrix products, arithmetic and copies ran while one was open for 3% of the time, Pallas kernels for 6%

profile of v8, /device:TPU:1, one launch (start us, length us, event | category | flops | bytes accessed | tf_op | source)
XLA Modules:
  0.0 139.1 jit_solution(14978861411211620107)
XLA Ops:
  0.6 0.0 copy-start
  0.6 0.0 copy-start.1
  0.7 3.0 %shard_map.84 = (bf16[2,1024,128]{2,1,0:T(8,128)(2,1)}, bf16[2,256,128]{2,1,0:T(8,128)(2,1)}, bf16[2,256,128]{2,1,0:T(8,128)(2,1)}, bf16[2,8,32,128]{3,2,1,0:T(8,128)(2,1)}, bf16[2,8,32,128]{3,2,1,0:T(8,128)(2,1)}) custom-call(s32[8]{0:T(128)} %pos_ref.3, bf16[512,128]{1,0:T(8,128)(2,1)} %feat_ref.1, bf16[512,128]{1,0:T(8,128)(2,1)} %cot_ref.1), custom_call_target="tpu_custom_call" | custom-call | tf_op jit(solution)/shard_map/pallas_call | solution.py:165
  3.7 1.3 collective-permute-start.1
  5.0 5.0 %collective-permute-start = (bf16[2,256,128]{2,1,0:T(8,128)(2,1)}, bf16[2,256,128]{2,1,0:T(8,128)(2,1)S(1)}, u32[]{:S(2)}, u32[]{:S(2)}) collective-permute-start(bf16[2,256,128]{2,1,0:T(8,128)(2,1)} %get-tuple-element.17), channel_id=1, source_target_pairs={{0,4},{4,8},{8,12},{12,16},{16,20},{20,24},{24,28},{28,32},{32,36}... | collective-permute-start | bytes 393224 | tf_op jit(solution)/shard_map/ppermute | solution.py:195
  10.0 0.6 collective-permute-done.1.refs_3_
  10.6 1.6 %collective-permute-done.refs_2_ = bf16[2,256,128]{2,1,0:T(8,128)(2,1)S(1)} collective-permute-done((bf16[2,256,128]{2,1,0:T(8,128)(2,1)}, bf16[2,256,128]{2,1,0:T(8,128)(2,1)S(1)}, u32[]{:S(2)}, u32[]{:S(2)}) %collective-permute-start) | collective-permute-done | bytes 131104 | tf_op jit(solution)/shard_map/ppermute | solution.py:195
  12.2 1.0 pad_maximum_fusion
  13.2 6.5 %collective-permute-start.2 = (bf16[2,12,32,128]{3,2,1,0:T(8,128)(2,1)S(1)}, bf16[2,12,32,128]{3,2,1,0:T(8,128)(2,1)S(1)}, u32[]{:S(2)}, u32[]{:S(2)}) collective-permute-start(bf16[2,12,32,128]{3,2,1,0:T(8,128)(2,1)S(1)} %pad_maximum_fusion), channel_id=1, source_target_pairs={{0,1},{1,2},{2,3},{4,5},{5,6},{6,7},{8,9},{9,10},{10,11},{12,13},{... | collective-permute-start | bytes 589832 | tf_op jit(solution)/shard_map/ppermute | solution.py:204
  19.7 0.9 pad_maximum_fusion.1
  20.6 3.7 %collective-permute-start.3 = (bf16[2,12,32,128]{3,2,1,0:T(8,128)(2,1)S(1)}, bf16[2,12,32,128]{3,2,1,0:T(8,128)(2,1)S(1)}, u32[]{:S(2)}, u32[]{:S(2)}) collective-permute-start(bf16[2,12,32,128]{3,2,1,0:T(8,128)(2,1)S(1)} %pad_maximum_fusion.1), channel_id=1, source_target_pairs={{1,0},{2,1},{3,2},{5,4},{6,5},{7,6},{9,8},{10,9},{11,10},{13,12},{... | collective-permute-start | bytes 589832 | tf_op jit(solution)/shard_map/ppermute | solution.py:205
  24.3 0.0 copy-done
  24.4 1.6 %copy.11 = bf16[27,128,128]{1,2,0:T(8,128)(2,1)} copy(bf16[27,128,128]{2,1,0:T(8,128)(2,1)S(1)} %bitcast.17) | data formatting | bytes 1769472 | tf_op jit(solution)/shard_map/reshape | solution.py:178
  26.0 1.6 %copy.12 = bf16[27,128,128]{1,2,0:T(8,128)(2,1)} copy(bf16[27,128,128]{2,1,0:T(8,128)(2,1)S(1)} %bitcast.21) | data formatting | bytes 1769472 | tf_op jit(solution)/shard_map/reshape | solution.py:178
  27.6 0.0 collective-permute-done.2.refs_4_
  27.6 0.0 copy-start.4
  27.6 1.5 %collective-permute-done.3.refs_5_ = bf16[2,12,32,128]{3,2,1,0:T(8,128)(2,1)S(1)} collective-permute-done((bf16[2,12,32,128]{3,2,1,0:T(8,128)(2,1)S(1)}, bf16[2,12,32,128]{3,2,1,0:T(8,128)(2,1)S(1)}, u32[]{:S(2)}, u32[]{:S(2)}) %collective-permute-start.3) | collective-permute-done | bytes 196640 | tf_op jit(solution)/shard_map/ppermute | solution.py:205
  29.1 0.7 copy-done.5
  29.8 10.0 %shard_map.85 = (bf16[2,2,10,10,16,128]{5,4,3,2,1,0:T(8,128)(2,1)}, bf16[3456,128]{1,0:T(8,128)(2,1)}, bf16[3456,128]{1,0:T(8,128)(2,1)}) custom-call(s32[1]{0:T(128)} %bitcast.refs_0_, bf16[2,1024,128]{2,1,0:T(8,128)(2,1)} %get-tuple-element.16.refs_1_, bf16[2,256,128]{2,1,0:T(8,128)(2,1)} %copy-done.3, bf16[2,256,128]{2,1,0:T(8,128)(2,1)} %copy-done.2, ...), custom_call_target="tpu_custom_call" | custom-call | tf_op jit(solution)/shard_map/pallas_call | solution.py:165
  39.8 1.9 %collective-permute-start.4 = (bf16[3456,128]{1,0:T(8,128)(2,1)}, bf16[3456,128]{1,0:T(8,128)(2,1)S(1)}, u32[]{:S(2)}, u32[]{:S(2)}) collective-permute-start(bf16[3456,128]{1,0:T(8,128)(2,1)} %get-tuple-element.27), channel_id=1, source_target_pairs={{0,1},{1,0},{2,3},{3,2},{4,5},{5,4},{6,7},{7,6},{8,9},{9,8},{10,11... | collective-permute-start | bytes 2654216 | tf_op jit(solution)/shard_map/ppermute | solution.py:224
  41.7 2.6 %collective-permute-done.4 = bf16[3456,128]{1,0:T(8,128)(2,1)S(1)} collective-permute-done((bf16[3456,128]{1,0:T(8,128)(2,1)}, bf16[3456,128]{1,0:T(8,128)(2,1)S(1)}, u32[]{:S(2)}, u32[]{:S(2)}) %collective-permute-start.4) | collective-permute-done | bytes 884768 | tf_op jit(solution)/shard_map/ppermute | solution.py:224
  44.3 1.4 %add_convert_fusion = bf16[3456,128]{1,0:T(8,128)(2,1)S(1)} fusion(bf16[3456,128]{1,0:T(8,128)(2,1)S(1)} %collective-permute-done.4, bf16[3456,128]{1,0:T(8,128)(2,1)} %get-tuple-element.26), kind=kLoop, calls=%fused_computation | loop fusion | flops 1769472 | bytes 2654208 | tf_op jit(solution)/shard_map/convert_element_type | solution.py:225
  45.7 32.7 %all_to_all.20 = bf16[16,216,128]{2,1,0:T(8,128)(2,1)S(1)} all-to-all(bf16[16,216,128]{2,1,0:T(8,128)(2,1)S(1)} %bitcast.19), channel_id=1, replica_groups=mesh['y_lo'=2,'x'=4,'z_hi'=4,'z_lo'=4,'y_hi'=2,'core'=2] {'y_hi','y_lo',..., dimensions={0} | all-to-all | bytes 1769472 | tf_op jit(solution)/shard_map/all_to_all | solution.py:210
  78.4 0.1 reduce.1
  78.6 14.2 %all_to_all.21 = bf16[16,16,128]{2,1,0:T(8,128)(2,1)S(1)} all-to-all(bf16[16,16,128]{2,1,0:T(8,128)(2,1)S(1)} %bitcast.25), channel_id=1, replica_groups=mesh['y_lo'=2,'x'=4,'z_hi'=4,'z_lo'=4,'y_hi'=2,'core'=2] {'z_hi','z_lo'}, dimensions={0} | all-to-all | bytes 131072 | tf_op jit(solution)/shard_map/all_to_all | solution.py:210
  92.8 14.3 %all_to_all.22 = bf16[16,16,128]{2,1,0:T(8,128)(2,1)S(1)} all-to-all(bf16[16,16,128]{2,1,0:T(8,128)(2,1)S(1)} %broadcast_in_dim.6), channel_id=1, replica_groups=mesh['y_lo'=2,'x'=4,'z_hi'=4,'z_lo'=4,'y_hi'=2,'core'=2] {'z_hi','z_lo'}, dimensions={0} | all-to-all | bytes 131072 | tf_op jit(solution)/shard_map/all_to_all | solution.py:210
  107.2 0.1 broadcast_in_dim.7
  107.3 15.1 %all_to_all.23 = bf16[16,216,128]{2,1,0:T(8,128)(2,1)S(1)} all-to-all(bf16[16,216,128]{2,1,0:T(8,128)(2,1)S(1)} %broadcast_in_dim.7), channel_id=1, replica_groups=mesh['y_lo'=2,'x'=4,'z_hi'=4,'z_lo'=4,'y_hi'=2,'core'=2] {'y_hi','y_lo',..., dimensions={0} | all-to-all | bytes 1769472 | tf_op jit(solution)/shard_map/all_to_all | solution.py:210
  122.4 6.6 %collective-permute-start.5 = (bf16[3456,128]{1,0:T(8,128)(2,1)S(1)}, bf16[3456,128]{1,0:T(8,128)(2,1)S(1)}, u32[]{:S(2)}, u32[]{:S(2)}) collective-permute-start(bf16[3456,128]{1,0:T(8,128)(2,1)S(1)} %bitcast.20), channel_id=1, source_target_pairs={{0,1},{1,0},{2,3},{3,2},{4,5},{5,4},{6,7},{7,6},{8,9},{9,8},{10,11... | collective-permute-start | bytes 2654216 | tf_op jit(solution)/shard_map/ppermute | solution.py:233
  129.0 8.0 %shard_map.86 = (bf16[512,128]{1,0:T(8,128)(2,1)}, f32[512,128]{1,0:T(8,128)}) custom-call(s32[8]{0:T(128)} %pos_ref.3, bf16[2,2,10,10,16,128]{5,4,3,2,1,0:T(8,128)(2,1)} %get-tuple-element.22.pairs_ref, bf16[3456,128]{1,0:T(8,128)(2,1)} %w2_ref.1, bf16[3456,128]{1,0:T(8,128)(2,1)} %bitcast.22), custom_call_target="tpu_custom_call" | custom-call | flops 1811939328 | bytes 25165824 | tf_op jit(solution)/shard_map/pallas_call | solution.py:165
  137.0 0.0 collective-permute-done.5
  137.0 2.1 %select_convert_fusion = (f32[3456,128]{1,0:T(8,128)}, f32[3456,128]{1,0:T(8,128)}) fusion(bf16[3456,128]{1,0:T(8,128)(2,1)S(1)} %collective-permute-done.5, pred[]{:T(512)S(6)} %eq.3, bf16[16,216,128]{2,1,0:T(8,128)(2,1)S(1)} %all_to_all.23), kind=kLoop, calls=%fused_computation.1 | loop fusion | flops 1769472 | bytes 5308417 | tf_op jit(solution)/shard_map/convert_element_type | solution.py:235
  (13 shorter events, 0.1 us)
Async XLA Ops:
  0.6 23.7 %copy-start = (bf16[3456,128]{1,0:T(8,128)(2,1)S(1)}, bf16[3456,128]{1,0:T(8,128)(2,1)}, u32[]{:S(2)}) copy-start(bf16[3456,128]{1,0:T(8,128)(2,1)} %refs_6_.1) | copy-start | bytes 2654212
  0.6 25.4 %copy-start.1 = (bf16[3456,128]{1,0:T(8,128)(2,1)S(1)}, bf16[3456,128]{1,0:T(8,128)(2,1)}, u32[]{:S(2)}) copy-start(bf16[3456,128]{1,0:T(8,128)(2,1)} %w2_ref.1) | copy-start | bytes 2654212
  3.7 6.9 %collective-permute-start.1 = (bf16[2,256,128]{2,1,0:T(8,128)(2,1)}, bf16[2,256,128]{2,1,0:T(8,128)(2,1)S(1)}, u32[]{:S(2)}, u32[]{:S(2)}) collective-permute-start(bf16[2,256,128]{2,1,0:T(8,128)(2,1)} %get-tuple-element.18), channel_id=1, source_target_pairs={{4,0},{8,4},{12,8},{16,12},{20,16},{24,20},{28,24},{32,28},{36,32}... | collective-permute-start | bytes 393224 | tf_op jit(solution)/shard_map/ppermute | solution.py:196
  5.0 7.2 %collective-permute-start = (bf16[2,256,128]{2,1,0:T(8,128)(2,1)}, bf16[2,256,128]{2,1,0:T(8,128)(2,1)S(1)}, u32[]{:S(2)}, u32[]{:S(2)}) collective-permute-start(bf16[2,256,128]{2,1,0:T(8,128)(2,1)} %get-tuple-element.17), channel_id=1, source_target_pairs={{0,4},{4,8},{8,12},{12,16},{16,20},{20,24},{24,28},{28,32},{32,36}... | collective-permute-start | bytes 393224 | tf_op jit(solution)/shard_map/ppermute | solution.py:195
  10.6 17.0 %copy-start.2 = (bf16[2,256,128]{2,1,0:T(8,128)(2,1)}, bf16[2,256,128]{2,1,0:T(8,128)(2,1)S(1)}, u32[]{:S(2)}) copy-start(bf16[2,256,128]{2,1,0:T(8,128)(2,1)S(1)} %collective-permute-done.1.refs_3_) | copy-start | bytes 393220
  12.2 15.4 %copy-start.3 = (bf16[2,256,128]{2,1,0:T(8,128)(2,1)}, bf16[2,256,128]{2,1,0:T(8,128)(2,1)S(1)}, u32[]{:S(2)}) copy-start(bf16[2,256,128]{2,1,0:T(8,128)(2,1)S(1)} %collective-permute-done.refs_2_) | copy-start | bytes 393220
  13.2 14.4 %collective-permute-start.2 = (bf16[2,12,32,128]{3,2,1,0:T(8,128)(2,1)S(1)}, bf16[2,12,32,128]{3,2,1,0:T(8,128)(2,1)S(1)}, u32[]{:S(2)}, u32[]{:S(2)}) collective-permute-start(bf16[2,12,32,128]{3,2,1,0:T(8,128)(2,1)S(1)} %pad_maximum_fusion), channel_id=1, source_target_pairs={{0,1},{1,2},{2,3},{4,5},{5,6},{6,7},{8,9},{9,10},{10,11},{12,13},{... | collective-permute-start | bytes 589832 | tf_op jit(solution)/shard_map/ppermute | solution.py:204
  20.6 8.5 %collective-permute-start.3 = (bf16[2,12,32,128]{3,2,1,0:T(8,128)(2,1)S(1)}, bf16[2,12,32,128]{3,2,1,0:T(8,128)(2,1)S(1)}, u32[]{:S(2)}, u32[]{:S(2)}) collective-permute-start(bf16[2,12,32,128]{3,2,1,0:T(8,128)(2,1)S(1)} %pad_maximum_fusion.1), channel_id=1, source_target_pairs={{1,0},{2,1},{3,2},{5,4},{6,5},{7,6},{9,8},{10,9},{11,10},{13,12},{... | collective-permute-start | bytes 589832 | tf_op jit(solution)/shard_map/ppermute | solution.py:205
  27.6 1.5 %copy-start.4 = (bf16[2,12,32,128]{3,2,1,0:T(8,128)(2,1)}, bf16[2,12,32,128]{3,2,1,0:T(8,128)(2,1)S(1)}, u32[]{:S(2)}) copy-start(bf16[2,12,32,128]{3,2,1,0:T(8,128)(2,1)S(1)} %collective-permute-done.2.refs_4_) | copy-start | bytes 589828
  29.1 0.7 copy-start.5
  39.8 4.5 %collective-permute-start.4 = (bf16[3456,128]{1,0:T(8,128)(2,1)}, bf16[3456,128]{1,0:T(8,128)(2,1)S(1)}, u32[]{:S(2)}, u32[]{:S(2)}) collective-permute-start(bf16[3456,128]{1,0:T(8,128)(2,1)} %get-tuple-element.27), channel_id=1, source_target_pairs={{0,1},{1,0},{2,3},{3,2},{4,5},{5,4},{6,7},{7,6},{8,9},{9,8},{10,11... | collective-permute-start | bytes 2654216 | tf_op jit(solution)/shard_map/ppermute | solution.py:224
  122.4 14.6 %collective-permute-start.5 = (bf16[3456,128]{1,0:T(8,128)(2,1)S(1)}, bf16[3456,128]{1,0:T(8,128)(2,1)S(1)}, u32[]{:S(2)}, u32[]{:S(2)}) collective-permute-start(bf16[3456,128]{1,0:T(8,128)(2,1)S(1)} %bitcast.20), channel_id=1, source_target_pairs={{0,1},{1,0},{2,3},{3,2},{4,5},{5,4},{6,7},{7,6},{8,9},{9,8},{10,11... | collective-permute-start | bytes 2654216 | tf_op jit(solution)/shard_map/ppermute | solution.py:233
